TPU v7x, 128 devices: a whole 4x4x4 slice. The times are simulated.
128 devices in a mesh: gx: 8 (over z, core), gy: 4 (over x), gz: 4 (over y).
Axes of the slice: x: 4, y: 4, z: 4, core: 2. Of those that a mesh axis runs over, the one named last changes fastest.
Arguments:
- source_residual: float32 [64, 256, 1024], P('gz', 'gx', 'gy'), may hold values from -8 to 8
- storage: float32 [64, 256, 1024], P('gz', 'gx', 'gy'), may hold values from 0.05 to 3
- conductivity: float32 [64, 256, 1024], P('gz', 'gx', 'gy'), may hold values from 0.05 to 2
- primal_label: int32 [64, 256, 4], P('gz', 'gx', 'gy'), may hold values from 0 to 31
- zone_of_block: int32 [16384, 1], P(('gx', 'gy', 'gz')), may hold values from 0 to 127; in each aligned block of 128 rows (0 to 127, 128 to 255, ...) at most 4 rows name the same one
- coarse_factor: float32 [4096, 4096], P(('gx', 'gy', 'gz')), may hold values from -0.0009765625 to 0.0009765625
- zone_factor: bfloat16 [128, 256, 256], P(('gx', 'gy', 'gz')), may hold values from -0.375 to 0.375
Outputs:
- solution: float32 [64, 256, 1024], P('gz', 'gx', 'gy')
- residual: float32 [64, 256, 1024], P('gz', 'gx', 'gy')
Inputs may be any that keep to these rules, and one draw needn't show every extreme that they name: `zone_of_block`: among the face blocks of one subdomain, no zone is named more than 4 times.
All inputs are finite; a program needn't handle non-finite values.
Results may differ from a plain program's by a relative error of at most 0.018.
Values may be sent and summed in bfloat16 or wider, within the bound.
No kernel may reach another device: no remote copies, remote signals or barrier semaphores. Data moves between devices by JAX's collectives and lax.ppermute only.
A program may use at most 64 MiB of HBM per device.

v0:
```python
import jax
import jax.numpy as jnp
from jax import lax
from jax.sharding import PartitionSpec as P

FB = 256
KC = 32
INNER = 8
ITERS = 2
CAP = 4


HIGHEST = lax.Precision.HIGHEST


def padded_2(block, sides, width):
    for axis, dim in sides:
        count = lax.axis_size(axis)
        forward = [(i, i + 1) for i in range(count - 1)]
        backward = [(target, source) for source, target in forward]
        low = lax.ppermute(
            lax.slice_in_dim(block, block.shape[dim] - width, None, axis=dim), axis, forward
        )
        high = lax.ppermute(lax.slice_in_dim(block, 0, width, axis=dim), axis, backward)
        block = jnp.concatenate([low, block, high], axis=dim)
    return block


def neighbour_sum(conductances, padded):
    summed = conductances[0] * padded[2:, 1:-1, 1:-1] + conductances[1] * padded[:-2, 1:-1, 1:-1]
    summed = (
        summed
        + conductances[2] * padded[1:-1, 2:, 1:-1]
        + conductances[3] * padded[1:-1, :-2, 1:-1]
    )
    summed = (
        summed
        + conductances[4] * padded[1:-1, 1:-1, 2:]
        + conductances[5] * padded[1:-1, 1:-1, :-2]
    )
    return summed


def face_conductances(conductivity):
    padded = padded_2(conductivity, (("gx", 1), ("gy", 2), ("gz", 0)), 1)
    return (
        0.5 * (padded[2:, 1:-1, 1:-1] + conductivity),
        0.5 * (padded[:-2, 1:-1, 1:-1] + conductivity),
        0.5 * (padded[1:-1, 2:, 1:-1] + conductivity),
        0.5 * (padded[1:-1, :-2, 1:-1] + conductivity),
        0.5 * (padded[1:-1, 1:-1, 2:] + conductivity),
        0.5 * (padded[1:-1, 1:-1, :-2] + conductivity),
    )


def apply_global(field, conductances, diagonal):
    padded = padded_2(field.astype(jnp.bfloat16), (("gx", 1), ("gy", 2), ("gz", 0)), 1).astype(
        field.dtype
    )
    return diagonal * field - neighbour_sum(conductances, padded)


def local_solve(rhs, conductances, diagonal):
    iterate = jnp.zeros_like(rhs)
    remain = rhs
    scaled = remain / diagonal
    search = scaled
    inner_rz = jnp.sum(remain * scaled)
    for sweep_index in range(INNER):
        applied = diagonal * search - neighbour_sum(conductances, jnp.pad(search, 1))
        step_size = inner_rz / jnp.sum(search * applied)
        iterate = iterate + step_size * search
        remain = remain - step_size * applied
        scaled = remain / diagonal
        inner_next = jnp.sum(remain * scaled)
        search = scaled + inner_next / inner_rz * search
        inner_rz = inner_next
    return iterate


def dispatch_table(zone_of_block, zone_count):
    zone_vec = zone_of_block[:, 0]
    hits = (zone_vec[:, None] == jnp.arange(zone_count, dtype=jnp.int32)[None, :]).astype(jnp.int32)
    before = jnp.cumsum(hits, axis=0) - hits
    slot_of = jnp.sum(before * hits, axis=1)
    slot_hits = (slot_of[:, None] == jnp.arange(CAP, dtype=jnp.int32)[None, :]).astype(jnp.int32)
    dispatch = hits[:, :, None] * slot_hits[:, None, :]
    return dispatch.reshape(zone_vec.shape[0], zone_count * CAP).astype(jnp.bfloat16)


def lift_return(received, factor):
    lifted = jnp.einsum("sif,fg->sig", received, factor, preferred_element_type=jnp.float32).astype(
        jnp.bfloat16
    )
    return jnp.einsum("sig,fg->sif", lifted, factor, preferred_element_type=jnp.float32).astype(
        jnp.bfloat16
    )


def per_device(
    source_residual, storage, conductivity, primal_label, zone_of_block, coarse_factor, zone_factor
):
    conductances = face_conductances(conductivity)
    diagonal = (
        storage
        + conductances[0]
        + conductances[1]
        + conductances[2]
        + conductances[3]
        + conductances[4]
        + conductances[5]
    )
    onehot = (primal_label.reshape(-1)[:, None] == jnp.arange(KC, dtype=jnp.int32)[None, :]).astype(
        jnp.float32
    )
    zone_count = lax.axis_size(("gx", "gy", "gz"))
    dispatch = dispatch_table(zone_of_block, zone_count)
    factor = zone_factor[0]
    cells_z, cells_x, cells_y = source_residual.shape

    def refine_term(field):
        layers = jnp.concatenate([field[:2], field[-2:]], axis=0)
        blocks = layers.reshape(-1, FB).astype(jnp.bfloat16)
        outgoing = jnp.einsum(
            "bs,bf->sf", dispatch, blocks, preferred_element_type=jnp.float32
        ).astype(jnp.bfloat16)
        outgoing = outgoing.reshape(zone_count, CAP, FB)
        returned = lax.all_to_all(
            lift_return(
                lax.all_to_all(
                    outgoing, ("gx", "gy", "gz"), split_axis=0, concat_axis=0, tiled=True
                ),
                factor,
            ),
            ("gx", "gy", "gz"),
            split_axis=0,
            concat_axis=0,
            tiled=True,
        )
        returned = returned.reshape(zone_count * CAP, FB)
        placed = jnp.dot(dispatch, returned, preferred_element_type=jnp.float32)
        placed = placed.reshape(4, cells_x, cells_y)
        middle = jnp.zeros((cells_z - 4, cells_x, cells_y), jnp.float32)
        return jnp.concatenate([placed[:2], middle, placed[2:]], axis=0)

    def coarse_partial(field):
        line_values = jnp.sum(field, axis=2).reshape(-1)
        restricted = jnp.dot(line_values, onehot, precision=HIGHEST)
        return jnp.dot(restricted, coarse_factor, precision=HIGHEST)

    def coarse_vector(field):
        return lax.psum(coarse_partial(field), ("gx", "gy", "gz"))

    def product_sum(value):
        return lax.psum(value, ("gx", "gy", "gz"))

    def precondition(field, summed):
        coarse_coef = jnp.dot(coarse_factor, summed, precision=HIGHEST)
        line_values = jnp.dot(onehot, coarse_coef, precision=HIGHEST).reshape(cells_z, cells_x, 1)
        return local_solve(field, conductances, diagonal) + line_values + refine_term(field)

    solution = jnp.zeros_like(source_residual)
    residual = source_residual
    summed = coarse_vector(residual)
    precond = precondition(residual, summed)
    current_rz = product_sum(jnp.sum(residual * precond))
    direction = precond
    for outer_step in range(ITERS):
        applied = apply_global(direction, conductances, diagonal)
        final_step = outer_step + 1 == ITERS
        curvature = lax.psum(jnp.sum(direction * applied), ("gx", "gy", "gz"))
        step_size = current_rz / curvature
        solution = solution + step_size * direction
        residual = residual - step_size * applied
        if not final_step:
            summed = coarse_vector(residual)
            precond = precondition(residual, summed)
            next_rz = product_sum(jnp.sum(residual * precond))
            direction = precond + next_rz / current_rz * direction
            current_rz = next_rz
    return (solution, residual)


def solution(mesh):
    in_specs = (
        P("gz", "gx", "gy"),
        P("gz", "gx", "gy"),
        P("gz", "gx", "gy"),
        P("gz", "gx", "gy"),
        P(("gx", "gy", "gz"), None),
        P(("gx", "gy", "gz"), None),
        P(("gx", "gy", "gz"), None, None),
    )
    out_specs = (P("gz", "gx", "gy"), P("gz", "gx", "gy"))
    return jax.shard_map(
        per_device, mesh=mesh, in_specs=in_specs, out_specs=out_specs, check_vma=False
    )
```

profile of v0, /device:TPU:1, one launch (start us, length us, event | category | flops | bytes accessed | tf_op | source)
XLA Modules:
  0.0 639.4 jit_solution(13267346616168054444)
XLA Ops:
  1.7 3.3 collective-permute-start.1
  5.0 3.5 collective-permute-start
  11.7 3.1 collective-permute-start.2
  16.2 5.5 collective-permute-done.2
  21.8 4.1 collective-permute-done.3
  27.3 4.6 collective-permute-start.5
  33.5 2.4 fusion.261
  35.9 2.3 fusion.241
  39.0 66.3 %psum.42 = f32[4096]{0:T(1024)S(1)} all-reduce(f32[4096]{0:T(1024)S(1)} %bitcast.65), channel_id=1, replica_groups=mesh['gx'=8,'gy'=4,'gz'=4] {'gx','gy','gz'}, use_global_device_ids=true, to_apply=%region_17.18 | all-reduce | flops 4096 | bytes 32768 | tf_op jit(solution)/shard_map/psum | solution.py:152
  107.6 3.2 multiply_reduce_fusion.31
  115.5 6.6 %all-to-all-start = ((bf16[128,4,256]{2,1,0:T(4,128)(2,1)}), bf16[128,4,256]{2,1,0:T(4,128)(2,1)}, u32[]{:S(2)}, u32[]{:S(2)}) async-start(bf16[128,4,256]{2,1,0:T(4,128)(2,1)} %reshape.106), calls=%async_computation | async-start | bytes 524288 | tf_op jit(solution)/shard_map/all_to_all | solution.py:130
  123.5 2.2 multiply_reduce_fusion.30
  127.0 2.9 multiply_reduce_fusion.29
  132.6 2.2 multiply_reduce_fusion.28
  136.1 2.9 multiply_reduce_fusion.27
  141.7 2.2 multiply_reduce_fusion.26
  145.2 2.9 multiply_reduce_fusion.25
  150.7 2.2 multiply_reduce_fusion.24
  154.0 2.9 multiply_reduce_fusion.23
  159.5 2.2 multiply_reduce_fusion.22
  163.0 2.9 multiply_reduce_fusion.21
  168.6 2.2 multiply_reduce_fusion.20
  175.3 2.3 multiply_add_fusion.9
  177.6 2.2 convolution_convert_fusion.3
  181.7 10.2 %all-to-all-start.1 = ((bf16[128,4,256]{2,1,0:T(4,128)(2,1)}), bf16[128,4,256]{2,1,0:T(4,128)(2,1)}, u32[]{:S(2)}, u32[]{:S(2)}) async-start(bf16[128,4,256]{2,1,0:T(4,128)(2,1)} %copy.23), calls=%async_computation.1 | async-start | bytes 524288 | tf_op jit(solution)/shard_map/all_to_all | solution.py:128
  191.9 3.9 fusion.219
  197.1 5.6 all-to-all-done.1
  203.9 2.6 fusion.253
  206.6 3.1 collective-permute-start.6
  211.7 3.1 collective-permute-done.7
  215.1 2.2 collective-permute-start.8
  219.8 4.3 collective-permute-done.9
  224.2 2.3 collective-permute-start.10
  227.8 3.8 collective-permute-done.11
  232.0 2.4 multiply_reduce_fusion.17
  234.4 73.4 %all-reduce.16 = (f32[]{:T(128)}, f32[]{:T(128)}) all-reduce(f32[]{:T(128)} %get-tuple-element.6, f32[]{:T(128)} %get-tuple-element.5), channel_id=1, replica_groups=mesh['gx'=8,'gy'=4,'gz'=4] {'gx','gy','gz'}, use_global_device_ids=true, to_apply=%region_21.22 | all-reduce | flops 2 | bytes 16 | tf_op jit(solution)/shard_map/psum | solution.py:155
  310.6 2.3 fusion.240
  313.6 64.2 %psum.45 = f32[4096]{0:T(1024)S(1)} all-reduce(f32[4096]{0:T(1024)S(1)} %bitcast.67), channel_id=1, replica_groups=mesh['gx'=8,'gy'=4,'gz'=4] {'gx','gy','gz'}, use_global_device_ids=true, to_apply=%region_41.42 | all-reduce | flops 4096 | bytes 32768 | tf_op jit(solution)/shard_map/psum | solution.py:152
  379.9 3.1 multiply_reduce_fusion.14
  387.7 5.5 all-to-all-start.2
  394.6 2.2 multiply_reduce_fusion.13
  398.0 2.9 multiply_reduce_fusion.12
  403.4 2.1 multiply_reduce_fusion.11
  406.7 2.9 multiply_reduce_fusion.10
  412.2 2.1 multiply_reduce_fusion.9
  415.6 3.0 multiply_reduce_fusion.8
  421.2 2.2 multiply_reduce_fusion.7
  424.6 3.0 multiply_reduce_fusion.6
  430.2 2.2 multiply_reduce_fusion.5
  433.8 3.0 multiply_reduce_fusion.4
  439.5 2.2 multiply_reduce_fusion.3
  446.3 2.4 multiply_add_fusion.2
  452.6 10.4 %all-to-all-start.3 = ((bf16[128,4,256]{2,1,0:T(4,128)(2,1)}), bf16[128,4,256]{2,1,0:T(4,128)(2,1)}, u32[]{:S(2)}, u32[]{:S(2)}) async-start(bf16[128,4,256]{2,1,0:T(4,128)(2,1)} %copy.27), calls=%async_computation.3 | async-start | bytes 524288 | tf_op jit(solution)/shard_map/all_to_all | solution.py:128
  463.0 3.8 fusion.218
  468.1 5.7 all-to-all-done.3
  475.0 4.2 multiply_reduce_fusion.1
  479.2 62.7 %psum.46 = f32[]{:T(128)} all-reduce(f32[]{:T(128)} %get-tuple-element.16), channel_id=1, replica_groups=mesh['gx'=8,'gy'=4,'gz'=4] {'gx','gy','gz'}, use_global_device_ids=true, to_apply=%region_43.44 | all-reduce | flops 1 | bytes 8 | tf_op jit(solution)/shard_map/psum | solution.py:155
  544.5 3.3 collective-permute-start.12
  549.7 3.1 collective-permute-done.13
  557.3 4.2 collective-permute-done.15
  565.0 3.6 collective-permute-done.17
  569.1 2.2 multiply_reduce_fusion
  571.3 63.8 %psum.47 = f32[]{:T(128)} all-reduce(f32[]{:T(128)} %get-tuple-element.12), channel_id=1, replica_groups=mesh['gx'=8,'gy'=4,'gz'=4] {'gx','gy','gz'}, use_global_device_ids=true, to_apply=%region_45.46 | all-reduce | flops 1 | bytes 8 | tf_op jit(solution)/shard_map/psum | solution.py:171
  636.4 2.7 multiply_subtract_fusion
  (177 shorter events, 66.5 us)
Async XLA Ops:
  0.6 38.0 %copy-start = (f32[32,4096]{1,0:T(8,128)S(1)}, f32[32,4096]{1,0:T(8,128)}, u32[]{:S(2)}) copy-start(f32[32,4096]{1,0:T(8,128)} %param.12) | copy-start | bytes 1572868
  1.7 8.6 %collective-permute-start.1 = (f32[16,1,256]{2,1,0:T(1,128)S(1)}, f32[16,1,256]{2,1,0:T(1,128)S(1)}, u32[]{:S(2)}, u32[]{:S(2)}) collective-permute-start(f32[16,1,256]{2,1,0:T(1,128)S(1)} %get-tuple-element.101), channel_id=1, source_target_pairs={{16,0},{32,16},{48,32},{64,48},{80,64},{96,80},{112,96},{17,1},{33... | collective-permute-start | bytes 49160 | tf_op jit(solution)/shard_map/ppermute | solution.py:24
  5.0 5.3 collective-permute-start
  10.3 15.6 %copy-start.1 = (f32[16,32,256]{2,1,0:T(8,128)S(1)}, f32[16,32,256]{2,1,0:T(8,128)}, u32[]{:S(2)}) copy-start(f32[16,32,256]{2,1,0:T(8,128)} %param.9) | copy-start | bytes 1572868
  11.7 20.9 %copy-start.41 = (s32[16,32,1]{1,2,0:T(1,128)S(1)}, s32[16,32,1]{1,2,0:T(1,128)}, u32[]{:S(2)}) copy-start(s32[16,32,1]{1,2,0:T(1,128)} %param.10) | copy-start | bytes 6148
  11.7 10.1 %collective-permute-start.2 = (f32[16,34,1]{2,1,0:T(8,128)S(1)}, f32[16,34,1]{2,1,0:T(8,128)S(1)}, u32[]{:S(2)}, u32[]{:S(2)}) collective-permute-start(f32[16,34,1]{2,1,0:T(8,128)S(1)} %get-tuple-element.93), channel_id=1, source_target_pairs={{0,4},{4,8},{8,12},{1,5},{5,9},{9,13},{2,6},{6,10},{10,14},{3,7},{... | collective-permute-start | bytes 6536 | tf_op jit(solution)/shard_map/ppermute | solution.py:21
  14.8 11.0 %collective-permute-start.3 = (f32[16,34,1]{2,1,0:T(8,128)S(1)}, f32[16,34,1]{2,1,0:T(8,128)S(1)}, u32[]{:S(2)}, u32[]{:S(2)}) collective-permute-start(f32[16,34,1]{2,1,0:T(8,128)S(1)} %get-tuple-element.94), channel_id=1, source_target_pairs={{4,0},{8,4},{12,8},{5,1},{9,5},{13,9},{6,2},{10,6},{14,10},{7,3},{... | collective-permute-start | bytes 6536 | tf_op jit(solution)/shard_map/ppermute | solution.py:24
  21.8 11.7 %copy-start.39 = (f32[16,34,1]{2,1,0:T(8,128)}, f32[16,34,1]{2,1,0:T(8,128)S(1)}, u32[]{:S(2)}) copy-start(f32[16,34,1]{2,1,0:T(8,128)S(1)} %collective-permute-done.2) | copy-start | bytes 6532
  25.9 7.6 %copy-start.40 = (f32[16,34,1]{2,1,0:T(8,128)}, f32[16,34,1]{2,1,0:T(8,128)S(1)}, u32[]{:S(2)}) copy-start(f32[16,34,1]{2,1,0:T(8,128)S(1)} %collective-permute-done.3) | copy-start | bytes 6532
  26.0 7.5 %collective-permute-start.4 = (f32[1,34,258]{2,1,0:T(8,128)S(1)}, f32[1,34,258]{2,1,0:T(8,128)S(1)}, u32[]{:S(2)}, u32[]{:S(2)}) collective-permute-start(f32[1,34,258]{2,1,0:T(8,128)S(1)} %get-tuple-element.91), channel_id=1, source_target_pairs={{1,0},{2,1},{3,2},{5,4},{6,5},{7,6},{9,8},{10,9},{11,10},{13,12},{... | collective-permute-start | bytes 105272 | tf_op jit(solution)/shard_map/ppermute | solution.py:24
  27.3 6.2 collective-permute-start.5
  33.5 2.5 copy-start.20
  35.9 2.3 copy-start.2
  35.9 2.3 copy-start.37
  115.5 62.1 %all-to-all-start = ((bf16[128,4,256]{2,1,0:T(4,128)(2,1)}), bf16[128,4,256]{2,1,0:T(4,128)(2,1)}, u32[]{:S(2)}, u32[]{:S(2)}) async-start(bf16[128,4,256]{2,1,0:T(4,128)(2,1)} %reshape.106), calls=%async_computation | async-start | bytes 524288 | tf_op jit(solution)/shard_map/all_to_all | solution.py:130
  122.1 1.4 copy-start.3
  123.5 2.2 copy-start.26
  131.2 1.4 copy-start.4
  132.6 2.2 copy-start.28
  140.3 1.4 copy-start.5
  141.7 2.2 copy-start.30
  149.3 1.4 copy-start.6
  150.6 2.2 copy-start.32
  158.1 1.4 copy-start.7
  159.5 2.2 copy-start.34
  167.2 1.4 copy-start.8
  168.5 2.2 copy-start.23
  181.7 21.0 %all-to-all-start.1 = ((bf16[128,4,256]{2,1,0:T(4,128)(2,1)}), bf16[128,4,256]{2,1,0:T(4,128)(2,1)}, u32[]{:S(2)}, u32[]{:S(2)}) async-start(bf16[128,4,256]{2,1,0:T(4,128)(2,1)} %copy.23), calls=%async_computation.1 | async-start | bytes 524288 | tf_op jit(solution)/shard_map/all_to_all | solution.py:128
  202.7 1.2 copy-start.24
  206.6 25.4 %copy-start.35 = (f32[16,32,256]{2,1,0:T(8,128)}, f32[16,32,256]{2,1,0:T(8,128)S(1)}, u32[]{:S(2)}) copy-start(f32[16,32,256]{2,1,0:T(8,128)S(1)} %get-tuple-element.53) | copy-start | bytes 1572868
  206.6 5.1 collective-permute-start.6
  209.8 5.1 collective-permute-start.7
  215.1 4.7 collective-permute-start.8
  217.3 14.7 %copy-start.9 = (f32[16,32,256]{2,1,0:T(8,128)S(1)}, f32[16,32,256]{2,1,0:T(8,128)}, u32[]{:S(2)}) copy-start(f32[16,32,256]{2,1,0:T(8,128)} %copy-done.2) | copy-start | bytes 1572868
  217.3 14.7 %copy-start.21 = (f32[16,32,256]{2,1,0:T(8,128)S(1)}, f32[16,32,256]{2,1,0:T(8,128)}, u32[]{:S(2)}) copy-start(f32[16,32,256]{2,1,0:T(8,128)} %param.7) | copy-start | bytes 1572868
  217.3 6.7 %collective-permute-start.9 = (bf16[16,34,1]{2,1,0:T(8,128)(2,1)S(1)}, bf16[16,34,1]{2,1,0:T(8,128)(2,1)S(1)}, u32[]{:S(2)}, u32[]{:S(2)}) collective-permute-start(bf16[16,34,1]{2,1,0:T(8,128)(2,1)S(1)} %get-tuple-element.106), channel_id=1, source_target_pairs={{4,0},{8,4},{12,8},{5,1},{9,5},{13,9},{6,2},{10,6},{14,10},{7,3},{... | collective-permute-start | bytes 3272 | tf_op jit(solution)/shard_map/ppermute | solution.py:24
  224.2 3.6 collective-permute-start.10
  226.4 5.1 collective-permute-start.11
  309.1 1.4 copy-start.10
  310.5 2.3 copy-start.18
  310.6 2.3 copy-start.36
  387.7 61.0 %all-to-all-start.2 = ((bf16[128,4,256]{2,1,0:T(4,128)(2,1)}), bf16[128,4,256]{2,1,0:T(4,128)(2,1)}, u32[]{:S(2)}, u32[]{:S(2)}) async-start(bf16[128,4,256]{2,1,0:T(4,128)(2,1)} %reshape.108), calls=%async_computation.2 | async-start | bytes 524288 | tf_op jit(solution)/shard_map/all_to_all | solution.py:130
  393.2 1.4 copy-start.11
  394.6 2.2 copy-start.25
  402.0 1.4 copy-start.12
  403.4 2.1 copy-start.27
  410.8 1.4 copy-start.13
  412.2 2.2 copy-start.29
  419.8 1.4 copy-start.14
  421.2 2.2 copy-start.31
  428.9 1.4 copy-start.15
  430.2 2.2 copy-start.33
  438.1 1.4 copy-start.16
  439.5 2.2 copy-start.22
  446.3 2.4 copy-start.42
  452.6 21.2 %all-to-all-start.3 = ((bf16[128,4,256]{2,1,0:T(4,128)(2,1)}), bf16[128,4,256]{2,1,0:T(4,128)(2,1)}, u32[]{:S(2)}, u32[]{:S(2)}) async-start(bf16[128,4,256]{2,1,0:T(4,128)(2,1)} %copy.27), calls=%async_computation.3 | async-start | bytes 524288 | tf_op jit(solution)/shard_map/all_to_all | solution.py:128
  544.5 24.6 %copy-start.38 = (f32[16,32,256]{2,1,0:T(8,128)}, f32[16,32,256]{2,1,0:T(8,128)S(1)}, u32[]{:S(2)}) copy-start(f32[16,32,256]{2,1,0:T(8,128)S(1)} %get-tuple-element.15) | copy-start | bytes 1572868
  544.5 5.2 collective-permute-start.12
  547.8 5.1 collective-permute-start.13
  553.1 4.1 collective-permute-start.14
  554.5 14.6 %copy-start.17 = (f32[16,32,256]{2,1,0:T(8,128)S(1)}, f32[16,32,256]{2,1,0:T(8,128)}, u32[]{:S(2)}) copy-start(f32[16,32,256]{2,1,0:T(8,128)} %copy-done.2) | copy-start | bytes 1572868
  554.5 7.0 %collective-permute-start.15 = (bf16[16,34,1]{2,1,0:T(8,128)(2,1)S(1)}, bf16[16,34,1]{2,1,0:T(8,128)(2,1)S(1)}, u32[]{:S(2)}, u32[]{:S(2)}) collective-permute-start(bf16[16,34,1]{2,1,0:T(8,128)(2,1)S(1)} %get-tuple-element.104), channel_id=1, source_target_pairs={{4,0},{8,4},{12,8},{5,1},{9,5},{13,9},{6,2},{10,6},{14,10},{7,3},{... | collective-permute-start | bytes 3272 | tf_op jit(solution)/shard_map/ppermute | solution.py:24
  561.6 3.4 collective-permute-start.16
  563.5 5.1 collective-permute-start.17
  (1 other events, 1.2 us)
where the time goes:
time: 647 us; the launch traced here: 639 us
  blocking collectives  330 us (51%)
  other arithmetic  123 us (19%)
  starting transfers between devices  73.5 us (11%)
  waiting for transfers between devices  45.4 us (7%)
  between operations  43.5 us (7%)
  local copies, waits for them, and re-layouts  11.7 us (2%)
  matrix products  11.4 us (2%)
    psum x2, blocking collectives, product_sum(): return lax.psum(value, ('gx', 'gy', 'gz'))  136 us
    psum x2, blocking collectives, coarse_vector(): return lax.psum(coarse_partial(field), ('gx', 'gy', 'gz'))  131 us
    psum x1, blocking collectives, per_device(): curvature = lax.psum(jnp.sum(direction * applied), ('gx', 'gy', 'gz'))  63.8 us
    reduce_sum x14, other arithmetic, local_solve(): inner_next = jnp.sum(remain * scaled)  39.8 us
    reduce_sum x14, other arithmetic, local_solve(): step_size = inner_rz / jnp.sum(search * applied)  33.9 us
    ppermute x9, waiting for transfers between devices, padded_2(): lax.ppermute(lax.slice_in_dim(block, 0, width, axis=dim), axis, backward)  26.2 us
    ppermute x9, starting transfers between devices, padded_2(): lax.ppermute(lax.slice_in_dim(block, block.shape[dim] - width, None, axis...  25.4 us
    add x14, other arithmetic, local_solve(): search = scaled + inner_next / inner_rz * search  20.8 us
  transfers between devices with their start and end apart: 22, of which 12 were waited for; matrix products, arithmetic and copies ran while one was open for 14% of the time, Pallas kernels for 0%

commit v1 on v0

v1 whole, which is shorter than its diff:
```python
import jax
import jax.numpy as jnp
from jax import lax
from jax.experimental import pallas as pl
from jax.experimental.pallas import tpu as pltpu
from jax.sharding import PartitionSpec as P

CZ = 16
CX = 32
CY = 256
KC = 32
INNER = 8
CAP = 4
ZN = 128
FB = 256
LANES = 128
WIDE = CAP * FB
SEND = WIDE + 2 * LANES
AX = ("gx", "gy", "gz")
F32 = jnp.float32
BF16 = jnp.bfloat16

VMEM = pl.BlockSpec(memory_space=pltpu.VMEM)
SMEM = pl.BlockSpec(memory_space=pltpu.SMEM)


def sds(shape, dtype=F32):
    return jax.ShapeDtypeStruct(shape, dtype)


def call(body, outs, n_in, scratch=(), smem_in=()):
    return pl.pallas_call(
        body,
        out_shape=outs,
        in_specs=[SMEM if i in smem_in else VMEM for i in range(n_in)],
        out_specs=jax.tree.map(lambda _: VMEM, outs),
        scratch_shapes=scratch,
        compiler_params=pltpu.CompilerParams(vmem_limit_bytes=48 * 1024 * 1024),
    )


def iota(shape, dim):
    return lax.broadcasted_iota(jnp.int32, shape, dim)


def total(x):
    return jnp.sum(jnp.sum(x, axis=1, keepdims=True), axis=0, keepdims=True)


def fold(x):
    half = x[:, :LANES] + x[:, LANES:]
    return half[0:8] + half[8:16] + half[16:24] + half[24:32]


def split3(x):
    high = x.astype(BF16).astype(F32)
    rest = x - high
    mid = rest.astype(BF16).astype(F32)
    return high, mid, rest - mid


def face_store(plane_of, refs, xs_lo, xs_hi):
    zlo, zhi, xlo, xhi, ylo, yhi = refs
    lane = iota((CX, LANES), 1)
    acc_lo = jnp.zeros((CX, LANES), F32)
    acc_hi = jnp.zeros((CX, LANES), F32)
    for z in range(CZ):
        plane = plane_of(z)
        if z == 0:
            zlo[...] = plane.astype(BF16)
        if z == CZ - 1:
            zhi[...] = plane.astype(BF16)
        xs_lo[z : z + 1, :] = plane[0:1, :]
        xs_hi[z : z + 1, :] = plane[CX - 1 : CX, :]
        acc_lo = jnp.where(lane == z, plane[:, 0:1], acc_lo)
        acc_hi = jnp.where(lane == z, plane[:, CY - 1 : CY], acc_hi)
    xlo[...] = xs_lo[...].astype(BF16)
    xhi[...] = xs_hi[...].astype(BF16)
    ylo[...] = acc_lo.astype(BF16)
    yhi[...] = acc_hi.astype(BF16)


FACE_OUTS = (
    sds((CX, CY), BF16),
    sds((CX, CY), BF16),
    sds((CZ, CY), BF16),
    sds((CZ, CY), BF16),
    sds((CX, LANES), BF16),
    sds((CX, LANES), BF16),
)
FACE_SCRATCH = (pltpu.VMEM((CZ, CY), F32), pltpu.VMEM((CZ, CY), F32))


def exchange(faces):
    out = []
    for axis, (low, high) in zip(("gz", "gx", "gy"), (faces[0:2], faces[2:4], faces[4:6])):
        n = lax.axis_size(axis)
        forward = [(i, (i + 1) % n) for i in range(n)]
        backward = [((i + 1) % n, i) for i in range(n)]
        out.append(lax.ppermute(high, axis, forward))
        out.append(lax.ppermute(low, axis, backward))
    return out


def zone_tables(zrow, zcol):
    shape = (ZN, ZN)
    row = jnp.broadcast_to(zrow, shape)
    col = jnp.broadcast_to(zcol, shape)
    return row, col, row == col


def store_send(send, blocks, zrow, zcol, u_rows, scalars, tile):
    row, col, same = zone_tables(zrow, zcol)
    sub, lane = iota((ZN, ZN), 0), iota((ZN, ZN), 1)
    slot = jnp.sum(jnp.where(same & (sub < lane), 1.0, 0.0), axis=0, keepdims=True)
    hit = row == sub
    for k in range(CAP):
        put = jnp.where(hit & (jnp.broadcast_to(slot, (ZN, ZN)) == float(k)), 1.0, 0.0)
        send[:, k * FB : (k + 1) * FB] = jnp.dot(
            put.astype(BF16), blocks, preferred_element_type=F32
        ).astype(BF16)
    high = u_rows.astype(BF16).astype(F32)
    tile[0:32, :] = high
    tile[32:64, :] = u_rows - high
    tile[64:128, :] = jnp.zeros((64, LANES), F32)
    for i, value in enumerate(scalars):
        for j, piece in enumerate(split3(value)):
            at = 64 + 3 * i + j
            tile[at : at + 1, :] = jnp.broadcast_to(piece, (1, LANES))
    send[:, WIDE : WIDE + LANES] = tile[...].T.astype(BF16)
    send[:, WIDE + LANES :] = jnp.zeros((ZN, LANES), BF16)


def coarse_rows(line_of, label, factor, rows):
    lane = iota((CX, LANES), 1)
    sub = iota((CX, LANES), 0)
    acc = jnp.zeros((CX, LANES), F32)
    for z in range(CZ):
        acc = acc + jnp.where(label[z] == lane, line_of(z), 0.0)
    g_row = jnp.broadcast_to(jnp.sum(acc, axis=0, keepdims=True), (CX, LANES))
    g_col = jnp.sum(jnp.where(sub == lane, g_row, 0.0), axis=1, keepdims=True)
    g = jnp.broadcast_to(g_col, (KC, LANES))
    for t in range(32):
        rows[t : t + 1, :] = jnp.sum(
            factor[:, t * LANES : (t + 1) * LANES] * g, axis=0, keepdims=True
        )
    return rows[...]


def face_blocks(field):
    return jnp.concatenate([field[0], field[1], field[CZ - 2], field[CZ - 1]], axis=0).astype(BF16)


def faces_body(k, *refs):
    face_store(lambda z: k[z], refs[:6], *refs[6:])


def pack_body(r, label, zrow, zcol, factor, send, tile, rows):
    u_rows = coarse_rows(
        lambda z: jnp.sum(r[z], axis=1, keepdims=True), label, factor, rows
    )
    store_send(send, face_blocks(r), zrow[...], zcol[...], u_rows, (), tile)


def lift_store(out, x_of, tail, zone):
    factor = zone[0]
    for k in range(CAP):
        lifted = jnp.dot(x_of(k), factor, preferred_element_type=F32).astype(BF16)
        back = lax.dot_general(
            lifted, factor, (((1,), (1,)), ((), ())), preferred_element_type=F32
        )
        out[:, k * FB : (k + 1) * FB] = back.astype(BF16)
    lane = iota((1, LANES), 1)
    u = jnp.where(lane < 32, tail + pltpu.roll(tail, LANES - 32, 1), 0.0)
    high = u.astype(BF16).astype(F32)
    both = high + pltpu.roll(u - high, 32, 1)
    out[:, WIDE : WIDE + LANES] = jnp.broadcast_to(both, (ZN, LANES)).astype(BF16)
    out[:, WIDE + LANES :] = jnp.zeros((ZN, LANES), BF16)


def tail_sum(got):
    return jnp.sum(got[:, WIDE : WIDE + LANES].astype(F32), axis=0, keepdims=True)


def lift0_body(got, zone, out):
    lift_store(out, lambda k: got[:, k * FB : (k + 1) * FB], tail_sum(got), zone)


def lift1_body(got0, got1, zone, out, scalars):
    tail0, tail1 = tail_sum(got0), tail_sum(got1)
    lane = iota((1, LANES), 1)

    def scalar(i):
        keep = (lane >= 64 + 3 * i) & (lane < 67 + 3 * i)
        return jnp.sum(jnp.where(keep, tail1, 0.0), axis=1, keepdims=True)

    rz, curvature = scalar(0), scalar(1)
    alpha = rz / curvature

    def x_of(k):
        old = got0[:, k * FB : (k + 1) * FB].astype(F32)
        new = got1[:, k * FB : (k + 1) * FB].astype(F32)
        return (old - alpha * new).astype(BF16)

    lift_store(out, x_of, tail0 - alpha * tail1, zone)
    scalars[0:1, :] = jnp.broadcast_to(alpha, (1, LANES))
    scalars[1:2, :] = jnp.broadcast_to(rz, (1, LANES))
    scalars[2:3, :] = jnp.broadcast_to(curvature, (1, LANES))
    scalars[3:8, :] = jnp.zeros((5, LANES), F32)


def minus_neighbours(p, below, above, cz_below, cz_above, cx, cy):
    tx = cx * p
    ty = cy * p
    out = p - cx * pltpu.roll(p, CX - 1, 0) - pltpu.roll(tx, 1, 0)
    out = out - cy * pltpu.roll(p, CY - 1, 1) - pltpu.roll(ty, 1, 1)
    if below is not None:
        out = out - cz_below * below
    if above is not None:
        out = out - cz_above * above
    return out


def cg(cz, cx, cy, p, q, e, y, rho):
    def step(_, carry):
        rho, beta = carry
        acc = jnp.zeros((8, LANES), F32)
        below, now = None, q[0] + beta * p[0]
        p[0] = now
        for z in range(CZ):
            above = None
            if z + 1 < CZ:
                above = q[z + 1] + beta * p[z + 1]
                p[z + 1] = above
            image = minus_neighbours(
                now,
                below,
                above,
                cz[z - 1] if z else None,
                cz[z] if z + 1 < CZ else None,
                cx[z],
                cy[z],
            )
            e[z] = image
            acc = acc + fold(now * image)
            below, now = now, above
        a = rho / total(acc)
        acc = jnp.zeros((8, LANES), F32)
        for z in range(CZ):
            y[z] = y[z] + a * p[z]
            left = q[z] - a * e[z]
            q[z] = left
            acc = acc + fold(left * left)
        new = total(acc)
        return new, new / rho

    lax.fori_loop(0, INNER, step, (rho, jnp.zeros((1, 1), F32)))


def start_cg(r_of, s, p, q, y):
    acc = jnp.zeros((8, LANES), F32)
    for z in range(CZ):
        left = s[z] * r_of(z)
        q[z] = left
        p[z] = jnp.zeros((CX, CY), F32)
        y[z] = jnp.zeros((CX, CY), F32)
        acc = acc + fold(left * left)
    return total(acc)


def solve0_body(
    flags, k, storage, r, kzl, kzh, kxl, kxh, kyl, kyh,
    local, s, sinv, cz, cx, cy, bzl, bzh, bxl, bxh, byl, byh,
    p, q, e, y,
):
    sub, lane = iota((CX, CY), 0), iota((CX, CY), 1)
    zl, zh = flags[0] * kzl[...].astype(F32), flags[1] * kzh[...].astype(F32)
    xl, xh = flags[2] * kxl[...].astype(F32), flags[3] * kxh[...].astype(F32)
    yl, yh = flags[4] * kyl[...].astype(F32), flags[5] * kyh[...].astype(F32)
    bzl[...] = flags[0] * 0.5 * (k[0] + zl)
    bzh[...] = flags[1] * 0.5 * (k[CZ - 1] + zh)
    lane_half = iota((CX, LANES), 1)
    y_edge_lo = jnp.zeros((CX, LANES), F32)
    y_edge_hi = jnp.zeros((CX, LANES), F32)
    for z in range(CZ):
        c = k[z]
        x_row_lo, x_row_hi = xl[z : z + 1, :], xh[z : z + 1, :]
        bxl[z : z + 1, :] = flags[2] * 0.5 * (c[0:1, :] + x_row_lo)
        bxh[z : z + 1, :] = flags[3] * 0.5 * (c[CX - 1 : CX, :] + x_row_hi)
        y_edge_lo = jnp.where(lane_half == z, c[:, 0:1], y_edge_lo)
        y_edge_hi = jnp.where(lane_half == z, c[:, CY - 1 : CY], y_edge_hi)
        around = (k[z - 1] if z else zl) + (k[z + 1] if z + 1 < CZ else zh)
        right = pltpu.roll(c, CX - 1, 0)
        around = around + jnp.where(sub == CX - 1, x_row_hi, right)
        around = around + jnp.where(sub == 0, x_row_lo, pltpu.roll(c, 1, 0))
        ahead = pltpu.roll(c, CY - 1, 1)
        end = pltpu.roll(yh, LANES - 1 - z, 1)
        around = around + jnp.where(lane == CY - 1, jnp.concatenate([end, end], axis=1), ahead)
        begin = pltpu.roll(yl, (LANES - z) % LANES, 1)
        around = around + jnp.where(
            lane == 0, jnp.concatenate([begin, begin], axis=1), pltpu.roll(c, 1, 1)
        )
        diagonal = storage[z] + 3.0 * c + 0.5 * around
        root = lax.rsqrt(diagonal)
        root = root * (1.5 - 0.5 * diagonal * root * root)
        s[z] = root
        sinv[z] = diagonal * root
        cx[z] = jnp.where(sub == CX - 1, 0.0, 0.5 * (c + right) * root * pltpu.roll(root, CX - 1, 0))
        cy[z] = jnp.where(lane == CY - 1, 0.0, 0.5 * (c + ahead) * root * pltpu.roll(root, CY - 1, 1))
        if z:
            cz[z - 1] = 0.5 * (k[z - 1] + c) * s[z - 1] * root
    cz[CZ - 1] = jnp.zeros((CX, CY), F32)
    byl[...] = flags[4] * 0.5 * (y_edge_lo + yl)
    byh[...] = flags[5] * 0.5 * (y_edge_hi + yh)
    rho = start_cg(lambda z: r[z], s, p, q, y)
    cg(cz, cx, cy, p, q, e, y, rho)
    for z in range(CZ):
        local[z] = s[z] * y[z]


def solve1_body(scalars, r, image, s, cz, cx, cy, local, p, q, e, y):
    alpha = scalars[0:1, 0:1]
    rho = start_cg(lambda z: r[z] - alpha * image[z], s, p, q, y)
    cg(cz, cx, cy, p, q, e, y, rho)
    for z in range(CZ):
        local[z] = s[z] * y[z]


def combine_body(local, got, label, zcol, zrow, factor, out, *refs):
    lane, sub = iota((CX, LANES), 1), iota((CX, LANES), 0)
    flipped = got[:, WIDE : WIDE + LANES].astype(F32).T
    u = flipped[0:32, :] + flipped[32:64, :]
    acc = jnp.zeros((KC, LANES), F32)
    for t in range(32):
        acc = acc + factor[:, t * LANES : (t + 1) * LANES] * u[t : t + 1, :]
    coef_col = jnp.sum(acc, axis=1, keepdims=True)
    coef = jnp.sum(jnp.where(sub == lane, coef_col, 0.0), axis=0, keepdims=True)
    coef = jnp.broadcast_to(coef, (CX, LANES))
    row, col, same = zone_tables(zrow[...], zcol[...])
    zsub, zlane = iota((ZN, ZN), 0), iota((ZN, ZN), 1)
    slot = jnp.sum(jnp.where(same & (zlane < zsub), 1.0, 0.0), axis=1, keepdims=True)
    slot = jnp.broadcast_to(slot, (ZN, ZN))
    placed = jnp.zeros((ZN, FB), F32)
    for k in range(CAP):
        take = jnp.where((col == zlane) & (slot == float(k)), 1.0, 0.0).astype(BF16)
        placed = placed + jnp.dot(
            take, got[:, k * FB : (k + 1) * FB], preferred_element_type=F32
        )
    order = {0: 0, 1: 1, CZ - 2: 2, CZ - 1: 3}
    for z in range(CZ):
        value = jnp.sum(jnp.where(label[z] == lane, coef, 0.0), axis=1, keepdims=True)
        plane = local[z] + value
        if z in order:
            at = order[z] * CX
            plane = plane + placed[at : at + CX, :]
        out[z] = plane
    face_store(lambda z: out[z], refs[:6], *refs[6:])


def apply_plane(z, v, sinv, cz, cx, cy, bounds, halos, masks):
    bzl, bzh, bxl, bxh, byl, byh = bounds
    hzl, hzh, hxl, hxh, hyl, hyh = halos
    first_row, last_row, first_lane, last_lane = masks
    inverse = sinv[z]
    scaled = minus_neighbours(
        v[z] * inverse,
        v[z - 1] * sinv[z - 1] if z else None,
        v[z + 1] * sinv[z + 1] if z + 1 < CZ else None,
        cz[z - 1] if z else None,
        cz[z] if z + 1 < CZ else None,
        cx[z],
        cy[z],
    )
    out = scaled * inverse
    out = out - jnp.where(first_row, bxl[z : z + 1, :] * hxl[z : z + 1, :], 0.0)
    out = out - jnp.where(last_row, bxh[z : z + 1, :] * hxh[z : z + 1, :], 0.0)
    low = pltpu.roll(byl * hyl, (LANES - z) % LANES, 1)
    high = pltpu.roll(byh * hyh, LANES - 1 - z, 1)
    out = out - jnp.where(first_lane, jnp.concatenate([low, low], axis=1), 0.0)
    out = out - jnp.where(last_lane, jnp.concatenate([high, high], axis=1), 0.0)
    if z == 0:
        out = out - bzl[...] * hzl
    if z == CZ - 1:
        out = out - bzh[...] * hzh
    return out


def apply_inputs(bound_refs, halo_refs):
    bzl, bzh, bxl, bxh, byl, byh = bound_refs
    halos = [h[...].astype(F32) for h in halo_refs]
    bounds = (bzl, bzh, bxl[...], bxh[...], byl[...], byh[...])
    sub, lane = iota((CX, CY), 0), iota((CX, CY), 1)
    return bounds, halos, (sub == 0, sub == CX - 1, lane == 0, lane == CY - 1)


def apply0_body(v, r, sinv, cz, cx, cy, *refs):
    bounds, halos, masks = apply_inputs(refs[0:6], refs[6:12])
    label, zrow, zcol, factor, image, send, tile, rows = refs[12:]
    rz = jnp.zeros((8, LANES), F32)
    curvature = jnp.zeros((8, LANES), F32)
    lines = []
    for z in range(CZ):
        out = apply_plane(z, v, sinv, cz, cx, cy, bounds, halos, masks)
        image[z] = out
        lines.append(jnp.sum(out, axis=1, keepdims=True))
        rz = rz + fold(r[z] * v[z])
        curvature = curvature + fold(v[z] * out)
    u_rows = coarse_rows(lambda z: lines[z], label, factor, rows)
    store_send(
        send, face_blocks(image), zrow[...], zcol[...], u_rows, (total(rz), total(curvature)), tile
    )


def apply1_body(scalars, v, r, image0, sinv, cz, cx, cy, *refs):
    bounds, halos, masks = apply_inputs(refs[0:6], refs[6:12])
    image, sums = refs[12:]
    alpha = scalars[0:1, 0:1]
    sums3 = [jnp.zeros((8, LANES), F32) for _ in range(3)]
    for z in range(CZ):
        out = apply_plane(z, v, sinv, cz, cx, cy, bounds, halos, masks)
        image[z] = out
        at = v[z]
        sums3[0] = sums3[0] + fold((r[z] - alpha * image0[z]) * at)
        sums3[1] = sums3[1] + fold(at * out)
        sums3[2] = sums3[2] + fold(at * image0[z])
    lane = iota((ZN, LANES), 1)
    row = jnp.zeros((ZN, LANES), F32)
    for i in range(3):
        row = jnp.where(lane == i, total(sums3[i]), row)
    sums[...] = row


def final_body(scalars, got, v, d, r, image0, image1, solution, residual):
    sums = jnp.sum(got[...], axis=0, keepdims=True)
    alpha0, rz0, curvature0 = scalars[0:1, 0:1], scalars[1:2, 0:1], scalars[2:3, 0:1]
    rz1, vav, vad = sums[:, 0:1], sums[:, 1:2], sums[:, 2:3]
    beta = rz1 / rz0
    alpha1 = rz1 / (vav + 2.0 * beta * vad + beta * beta * curvature0)
    mix = alpha0 + alpha1 * beta
    for z in range(CZ):
        solution[z] = mix * d[z] + alpha1 * v[z]
        residual[z] = r[z] - mix * image0[z] - alpha1 * image1[z]


FIELD = sds((CZ, CX, CY))
FIELD_SCRATCH = pltpu.VMEM((CZ, CX, CY), F32)
BOUND_OUTS = (
    sds((CX, CY)),
    sds((CX, CY)),
    sds((CZ, CY)),
    sds((CZ, CY)),
    sds((CX, LANES)),
    sds((CX, LANES)),
)
PACKED = sds((ZN, SEND), BF16)
TILE = pltpu.VMEM((LANES, LANES), F32)
ROWS = pltpu.VMEM((KC, LANES), F32)


def swap(x):
    return lax.all_to_all(x, AX, split_axis=0, concat_axis=0, tiled=True)


def per_device(r, storage, k, label, zone_of_block, factor, zone_factor):
    zcol = zone_of_block
    zrow = zone_of_block.reshape(1, ZN)
    flags = jnp.stack(
        [
            (lax.axis_index(axis) != edge).astype(F32)
            for axis in ("gz", "gx", "gy")
            for edge in (0, lax.axis_size(axis) - 1)
        ]
    )
    k_faces = call(faces_body, FACE_OUTS, 1, FACE_SCRATCH)(k)
    send0 = call(pack_body, PACKED, 5, (TILE, ROWS))(r, label, zrow, zcol, factor)
    got0 = swap(send0)
    k_halos = exchange(k_faces)
    back0 = swap(call(lift0_body, PACKED, 2)(got0, zone_factor))
    local, s, sinv, cz, cx, cy, *bounds = call(
        solve0_body, (FIELD,) * 6 + BOUND_OUTS, 10, (FIELD_SCRATCH,) * 4, (0,)
    )(flags, k, storage, r, *k_halos)

    def combine(local, back):
        z, *faces = call(combine_body, (FIELD,) + FACE_OUTS, 6, FACE_SCRATCH)(
            local, back, label, zcol, zrow, factor
        )
        return z, exchange(faces)

    d, halos = combine(local, back0)
    image0, send1 = call(apply0_body, (FIELD, PACKED), 22, (TILE, ROWS))(
        d, r, sinv, cz, cx, cy, *bounds, *halos, label, zrow, zcol, factor
    )
    got1 = swap(send1)
    back1, scalars = call(lift1_body, (PACKED, sds((8, LANES))), 3)(got0, got1, zone_factor)
    back1 = swap(back1)
    local = call(solve1_body, FIELD, 7, (FIELD_SCRATCH,) * 4)(scalars, r, image0, s, cz, cx, cy)
    v, halos = combine(local, back1)
    image1, sums = call(apply1_body, (FIELD, sds((ZN, LANES))), 20)(
        scalars, v, r, image0, sinv, cz, cx, cy, *bounds, *halos
    )
    return call(final_body, (FIELD, FIELD), 7)(scalars, swap(sums), v, d, r, image0, image1)


def solution(mesh):
    field = P("gz", "gx", "gy")
    in_specs = (field, field, field, field, P(AX, None), P(AX, None), P(AX, None, None))
    return jax.shard_map(
        per_device, mesh=mesh, in_specs=in_specs, out_specs=(field, field), check_vma=False
    )
```

time: 647 us -> 174 us (0.27); the launches traced: 639 us -> 173 us
  blocking collectives: 330 us -> 59.2 us
  other arithmetic: 123 us -> 6.36 us
  between operations: 43.5 us -> 1.05 us
  waiting for transfers between devices: 45.4 us -> 5.35 us
  starting transfers between devices: 73.5 us -> 35 us
  local copies, waits for them, and re-layouts: 11.7 us -> 40.5 us
  Pallas kernels: 0 us -> 25.5 us
  matrix products: 11.4 us -> 0 us
    psum x5 -> x0, blocking collectives: 330 us -> none  [the longest x2 136 us: product_sum(): return lax.psum(value, ('gx', 'gy', 'gz'))]
    reduce_sum x34 -> x0, other arithmetic: 87.9 us -> none  [the longest x14 39.8 us: local_solve(): inner_next = jnp.sum(remain * scaled)]
    all_to_all x0 -> x3, blocking collectives: none -> 59.2 us  [swap(): return lax.all_to_all(x, AX, split_axis=0, concat_axis=0, tiled=True)]
    unnamed x87 -> x116, local copies, waits for them, and re-layouts: 0.74 us -> 39.8 us
    ppermute x18, waiting for transfers between devices: 34.1 us -> 2.87 us  [the longest x9 1.89 us: exchange(): out.append(lax.ppermute(high, axis, forward))]
    pallas_call x0 -> x11, Pallas kernels: none -> 25.5 us  [the longest x1 8.4 us: per_device(): call(solve0_body, (FIELD,) * 6 + BOUND_OUTS, 10, (FIELD_SCRATCH,) * 4, (0,))]
    all_to_all x4 -> x2, starting transfers between devices: 32.7 us -> 11.4 us  [swap(): return lax.all_to_all(x, AX, split_axis=0, concat_axis=0, tiled=True)]
    add x14 -> x0, other arithmetic: 20.8 us -> none  [local_solve(): search = scaled + inner_next / inner_rz * search]
  transfers between devices with their start and end apart: 22 -> 20, of which waited for: 12 -> 5; matrix products, arithmetic and copies ran while one was open for 14% -> 0% of each run, Pallas kernels for 0% -> 9%
where the time goes in v1:
time: 174 us; the launch traced here: 173 us
  blocking collectives  59.2 us (34%)
  local copies, waits for them, and re-layouts  40.5 us (23%)
  starting transfers between devices  35 us (20%)
  Pallas kernels  25.5 us (15%)
  other arithmetic  6.36 us (4%)
  waiting for transfers between devices  5.35 us (3%)
    all_to_all x3, blocking collectives, swap(): return lax.all_to_all(x, AX, split_axis=0, concat_axis=0, tiled=True)  59.2 us
    unnamed x116, local copies, waits for them, and re-layouts  39.8 us
    ppermute x9, starting transfers between devices, exchange(): out.append(lax.ppermute(low, axis, backward))  13.8 us
    all_to_all x2, starting transfers between devices, swap(): return lax.all_to_all(x, AX, split_axis=0, concat_axis=0, tiled=True)  11.4 us
    ppermute x9, starting transfers between devices, exchange(): out.append(lax.ppermute(high, axis, forward))  9.71 us
    pallas_call x1, Pallas kernels, per_device(): call(solve0_body, (FIELD,) * 6 + BOUND_OUTS, 10, (FIELD_SCRATCH,) * 4, (0,))  8.4 us
    all_to_all x4, other arithmetic, swap(): return lax.all_to_all(x, AX, split_axis=0, concat_axis=0, tiled=True)  6.35 us
    pallas_call x1, Pallas kernels, per_device(): call(solve1_body, FIELD, 7, (FIELD_SCRATCH,) * 4)  6.21 us
  transfers between devices with their start and end apart: 20, of which 5 were waited for; matrix products, arithmetic and copies ran while one was open for 0% of the time, Pallas kernels for 9%

profile of v1, /device:TPU:1, one launch (start us, length us, event | category | flops | bytes accessed | tf_op | source)
XLA Modules:
  0.0 172.9 jit_solution(13529815144539622772)
XLA Ops:
  0.6 0.8 copy.31.zcol.refs_14_
  1.6 0.7 copy-done.39
  2.2 1.0 copy-done
  3.3 1.0 copy-done.2
  5.4 0.8 reduce
  6.3 22.7 %all_to_all.55 = bf16[128,2,640]{2,1,0:T(2,128)(2,1)S(1)} all-to-all(bf16[128,2,640]{2,1,0:T(2,128)(2,1)S(1)} %reshape.18), channel_id=1, replica_groups=mesh['gx'=8,'gy'=4,'gz'=4] {'gx','gy','gz'}, dimensions={0} | all-to-all | bytes 655360 | tf_op jit(solution)/shard_map/all_to_all | solution.py:461
  29.3 0.8 copy-done.19
  30.6 0.8 reduce.1
  31.4 0.8 reshape.20
  32.2 5.8 %all-to-all-start.1 = ((bf16[128,2,640]{2,1,0:T(2,128)(2,1)}), bf16[128,2,640]{2,1,0:T(2,128)(2,1)}, u32[]{:S(2)}, u32[]{:S(2)}) async-start(bf16[128,2,640]{2,1,0:T(2,128)(2,1)} %reshape.20), calls=%async_computation.1 | async-start | bytes 655360 | tf_op jit(solution)/shard_map/all_to_all | solution.py:461
  38.1 1.9 %collective-permute-start.2 = (bf16[16,256]{1,0:T(8,128)(2,1)S(1)}, bf16[16,256]{1,0:T(8,128)(2,1)S(1)}, u32[]{:S(2)}, u32[]{:S(2)}) collective-permute-start(bf16[16,256]{1,0:T(8,128)(2,1)S(1)} %get-tuple-element.42), channel_id=1, source_target_pairs={{0,16},{16,32},{32,48},{48,64},{64,80},{80,96},{96,112},{112,0},{1... | collective-permute-start | bytes 24584 | tf_op jit(solution)/shard_map/ppermute | solution.py:100
  40.1 1.2 collective-permute-start
  41.3 1.4 collective-permute-start.1
  42.8 1.2 collective-permute-start.4
  43.9 1.5 collective-permute-start.5
  45.5 0.8 collective-permute-done.3.kxh
  48.1 0.6 copy-done.35
  48.7 0.6 copy-done.37
  49.3 0.7 copy-done.36
  50.1 0.7 copy-done.38
  50.8 0.7 copy-done.43
  51.5 0.7 copy-done.45
  52.2 0.7 copy-done.47
  52.9 0.7 copy-done.49
  53.6 8.4 %shard_map.88 = (f32[16,32,256]{2,1,0:T(8,128)S(1)}, f32[16,32,256]{2,1,0:T(8,128)S(1)}, f32[16,32,256]{2,1,0:T(8,128)S(1)}, f32[16,32,256]{2,1,0:T(8,128)S(1)},...) custom-call(f32[6]{0:T(128)S(1)} %stack.36.flags, ...), custom_call_target="tpu_custom_call" | custom-call | tf_op jit(solution)/shard_map/pallas_call | solution.py:479
  62.0 0.8 copy-done.7
  62.8 0.8 copy-done.15
  63.6 0.8 copy-done.17
  66.2 3.3 %reshape.21 = bf16[128,1,1280]{2,1,0:T(2,128)(2,1)} reshape(bf16[128,2,640]{2,1,0:T(2,128)(2,1)} %all-to-all-done.1) | data formatting | bytes 655360
  69.5 1.2 copy.53
  70.7 0.6 copy-done.40
  71.3 2.5 %shard_map.90 = (f32[16,32,256]{2,1,0:T(8,128)S(1)}, bf16[32,256]{1,0:T(8,128)(2,1)S(1)}, bf16[32,256]{1,0:T(8,128)(2,1)S(1)}, bf16[16,256]{1,0:T(8,128)(2,1)S(1...) custom-call(f32[16,32,256]{2,1,0:T(8,128)S(1)} %copy-done.16, ...), custom_call_target="tpu_custom_call" | custom-call | tf_op jit(solution)/shard_map/pallas_call | solution.py:484
  73.8 2.4 %collective-permute-start.8 = (bf16[16,256]{1,0:T(8,128)(2,1)S(1)}, bf16[16,256]{1,0:T(8,128)(2,1)S(1)}, u32[]{:S(2)}, u32[]{:S(2)}) collective-permute-start(bf16[16,256]{1,0:T(8,128)(2,1)S(1)} %get-tuple-element.60), channel_id=1, source_target_pairs={{0,16},{16,32},{32,48},{48,64},{64,80},{80,96},{96,112},{112,0},{1... | collective-permute-start | bytes 24584 | tf_op jit(solution)/shard_map/ppermute | solution.py:100
  76.3 2.6 %collective-permute-start.7 = (bf16[32,256]{1,0:T(8,128)(2,1)S(1)}, bf16[32,256]{1,0:T(8,128)(2,1)S(1)}, u32[]{:S(2)}, u32[]{:S(2)}) collective-permute-start(bf16[32,256]{1,0:T(8,128)(2,1)S(1)} %get-tuple-element.59), channel_id=1, source_target_pairs={{1,0},{2,1},{3,2},{0,3},{5,4},{6,5},{7,6},{4,7},{9,8},{10,9},{11,1... | collective-permute-start | bytes 49160 | tf_op jit(solution)/shard_map/ppermute | solution.py:101
  78.9 1.2 collective-permute-start.9
  80.7 2.2 %collective-permute-start.11 = (bf16[32,128]{1,0:T(8,128)(2,1)S(1)}, bf16[32,128]{1,0:T(8,128)(2,1)S(1)}, u32[]{:S(2)}, u32[]{:S(2)}) collective-permute-start(bf16[32,128]{1,0:T(8,128)(2,1)S(1)} %get-tuple-element.63), channel_id=1, source_target_pairs={{4,0},{8,4},{12,8},{0,12},{5,1},{9,5},{13,9},{1,13},{6,2},{10,6},{... | collective-permute-start | bytes 24584 | tf_op jit(solution)/shard_map/ppermute | solution.py:101
  82.8 1.0 collective-permute-done.10.refs_10_
  83.9 2.0 %shard_map.91 = (f32[16,32,256]{2,1,0:T(8,128)S(1)}, bf16[128,1280]{1,0:T(8,128)(2,1)S(1)}) custom-call(f32[16,32,256]{2,1,0:T(8,128)S(1)} %get-tuple-element.47.v.d, f32[16,32,256]{2,1,0:T(8,128)S(1)} %copy-done.1, f32[16,32,256]{2,1,0:T(8,128)S(1)} %copy-done.8, f32[16,32,256]{2,1,0:T(8,128)S(1)} %get-tuple-element.49.cz, ...), custom_call_target="tpu_custom_call" | custom-call | tf_op jit(solution)/shard_map/pallas_call | solution.py:490
  86.0 0.7 copy-done.21
  86.7 2.4 %reduce.2 = bf16[128,1280]{1,0:T(8,128)(2,1)} reduce(bf16[128,1,1280]{2,0,1:T(8,128)(2,1)} %bitcast.34, bf16[]{:T(256)} %broadcast), dimensions={1}, to_apply=%copy.38.reduce_sub_computation | reduce | bytes 655362 | tf_op jit(solution)/shard_map/all_to_all | solution.py:461
  89.1 1.8 %reshape.22 = bf16[128,2,640]{2,1,0:T(2,128)(2,1)} reshape(bf16[128,1280]{1,0:T(8,128)(2,1)} %reduce.2) | data formatting | bytes 655360
  90.9 19.6 %all_to_all.56 = bf16[128,2,640]{2,1,0:T(2,128)(2,1)} all-to-all(bf16[128,2,640]{2,1,0:T(2,128)(2,1)} %reshape.22), channel_id=1, replica_groups=mesh['gx'=8,'gy'=4,'gz'=4] {'gx','gy','gz'}, dimensions={0} | all-to-all | bytes 655360 | tf_op jit(solution)/shard_map/all_to_all | solution.py:461
  110.4 3.2 %reshape.23 = bf16[128,1,1280]{2,1,0:T(2,128)(2,1)} reshape(bf16[128,2,640]{2,1,0:T(2,128)(2,1)} %all_to_all.56) | data formatting | bytes 655360
  113.6 1.2 copy.52
  115.4 0.7 copy-done.22
  116.7 2.4 %reduce.3 = bf16[128,1280]{1,0:T(8,128)(2,1)} reduce(bf16[128,1,1280]{2,0,1:T(8,128)(2,1)} %bitcast.35, bf16[]{:T(256)} %broadcast), dimensions={1}, to_apply=%copy.39.reduce_sub_computation | reduce | bytes 655362 | tf_op jit(solution)/shard_map/all_to_all | solution.py:461
  119.1 1.8 %reshape.24 = bf16[128,2,640]{2,1,0:T(2,128)(2,1)} reshape(bf16[128,1280]{1,0:T(8,128)(2,1)} %reduce.3) | data formatting | bytes 655360
  120.9 5.7 %all-to-all-start.3 = ((bf16[128,2,640]{2,1,0:T(2,128)(2,1)}), bf16[128,2,640]{2,1,0:T(2,128)(2,1)}, u32[]{:S(2)}, u32[]{:S(2)}) async-start(bf16[128,2,640]{2,1,0:T(2,128)(2,1)} %reshape.24), calls=%async_computation.3 | async-start | bytes 655360 | tf_op jit(solution)/shard_map/all_to_all | solution.py:461
  126.6 0.7 copy-done.33
  127.3 1.0 copy-done.18
  128.3 6.2 %shard_map.93.local = f32[16,32,256]{2,1,0:T(8,128)S(1)} custom-call(f32[8,128]{1,0:T(8,128)S(1)} %copy-done.33, f32[16,32,256]{2,1,0:T(8,128)S(1)} %copy-done.1, f32[16,32,256]{2,1,0:T(8,128)S(1)} %get-tuple-element.66.image.image0, f32[16,32,256]{2,1,0:T(8,128)S(1)} %copy-done.18, f32[16,32,256]{2,1,0:T(8,128)S(1)} %get-tuple-element.49.cz, ...), custom_call_target="tpu_custom_call" | custom-call | tf_op jit(solution)/shard_map/pallas_call | solution.py:496
  134.5 0.8 copy-done.12
  135.3 2.5 %all-to-all-done.3 = bf16[128,2,640]{2,1,0:T(2,128)(2,1)} async-done(((bf16[128,2,640]{2,1,0:T(2,128)(2,1)}), bf16[128,2,640]{2,1,0:T(2,128)(2,1)}, u32[]{:S(2)}, u32[]{:S(2)}) %all-to-all-start.3) | async-done | bytes 327712 | tf_op jit(solution)/shard_map/all_to_all | solution.py:461
  137.8 3.2 %reshape.25 = bf16[128,1,1280]{2,1,0:T(2,128)(2,1)} reshape(bf16[128,2,640]{2,1,0:T(2,128)(2,1)} %all-to-all-done.3) | data formatting | bytes 655360
  141.0 1.2 copy.51
  142.3 0.6 copy-done.41
  142.9 2.5 %shard_map.94 = (f32[16,32,256]{2,1,0:T(8,128)S(1)}, bf16[32,256]{1,0:T(8,128)(2,1)S(1)}, bf16[32,256]{1,0:T(8,128)(2,1)S(1)}, bf16[16,256]{1,0:T(8,128)(2,1)S(1...) custom-call(f32[16,32,256]{2,1,0:T(8,128)S(1)} %copy-done.13, ...), custom_call_target="tpu_custom_call" | custom-call | tf_op jit(solution)/shard_map/pallas_call | solution.py:484
  145.3 1.7 collective-permute-start.14
  147.4 2.3 %collective-permute-start.13 = (bf16[32,256]{1,0:T(8,128)(2,1)S(1)}, bf16[32,256]{1,0:T(8,128)(2,1)S(1)}, u32[]{:S(2)}, u32[]{:S(2)}) collective-permute-start(bf16[32,256]{1,0:T(8,128)(2,1)S(1)} %get-tuple-element.71), channel_id=1, source_target_pairs={{1,0},{2,1},{3,2},{0,3},{5,4},{6,5},{7,6},{4,7},{9,8},{10,9},{11,1... | collective-permute-start | bytes 49160 | tf_op jit(solution)/shard_map/ppermute | solution.py:101
  150.2 2.4 %collective-permute-start.17 = (bf16[32,128]{1,0:T(8,128)(2,1)S(1)}, bf16[32,128]{1,0:T(8,128)(2,1)S(1)}, u32[]{:S(2)}, u32[]{:S(2)}) collective-permute-start(bf16[32,128]{1,0:T(8,128)(2,1)S(1)} %get-tuple-element.75), channel_id=1, source_target_pairs={{4,0},{8,4},{12,8},{0,12},{5,1},{9,5},{13,9},{1,13},{6,2},{10,6},{... | collective-permute-start | bytes 24584 | tf_op jit(solution)/shard_map/ppermute | solution.py:101
  152.8 0.8 collective-permute-done.16.refs_10_
  153.7 0.8 shard_map.95
  154.6 16.9 %all_to_all.57 = f32[128,1,128]{2,1,0:T(1,128)S(1)} all-to-all(f32[128,1,128]{2,1,0:T(1,128)S(1)} %bitcast.37), channel_id=1, replica_groups=mesh['gx'=8,'gy'=4,'gz'=4] {'gx','gy','gz'}, dimensions={0} | all-to-all | bytes 131072 | tf_op jit(solution)/shard_map/all_to_all | solution.py:461
  171.5 1.4 shard_map.96
  (113 shorter events, 9.0 us)
Async XLA Ops:
  0.6 0.8 copy-start.50
  1.6 0.7 copy-start.39
  2.2 1.0 copy-start
  3.3 1.0 copy-start.2
  29.2 0.9 copy-start.19
  29.3 1.3 copy-start.4
  31.4 6.6 %copy-start.6 = (f32[16,32,256]{2,1,0:T(8,128)S(1)}, f32[16,32,256]{2,1,0:T(8,128)}, u32[]{:S(2)}) copy-start(f32[16,32,256]{2,1,0:T(8,128)} %k.3) | copy-start | bytes 1572868
  32.2 17.1 %copy-start.1 = (f32[16,32,256]{2,1,0:T(8,128)S(1)}, f32[16,32,256]{2,1,0:T(8,128)}, u32[]{:S(2)}) copy-start(f32[16,32,256]{2,1,0:T(8,128)} %r.11) | copy-start | bytes 1572868
  32.2 17.1 %copy-start.14 = (f32[16,32,256]{2,1,0:T(8,128)S(1)}, f32[16,32,256]{2,1,0:T(8,128)}, u32[]{:S(2)}) copy-start(f32[16,32,256]{2,1,0:T(8,128)} %storage.1) | copy-start | bytes 1572868
  32.2 34.0 %all-to-all-start.1 = ((bf16[128,2,640]{2,1,0:T(2,128)(2,1)}), bf16[128,2,640]{2,1,0:T(2,128)(2,1)}, u32[]{:S(2)}, u32[]{:S(2)}) async-start(bf16[128,2,640]{2,1,0:T(2,128)(2,1)} %reshape.20), calls=%async_computation.1 | async-start | bytes 655360 | tf_op jit(solution)/shard_map/all_to_all | solution.py:461
  38.1 5.8 %collective-permute-start.2 = (bf16[16,256]{1,0:T(8,128)(2,1)S(1)}, bf16[16,256]{1,0:T(8,128)(2,1)S(1)}, u32[]{:S(2)}, u32[]{:S(2)}) collective-permute-start(bf16[16,256]{1,0:T(8,128)(2,1)S(1)} %get-tuple-element.42), channel_id=1, source_target_pairs={{0,16},{16,32},{32,48},{48,64},{64,80},{80,96},{96,112},{112,0},{1... | collective-permute-start | bytes 24584 | tf_op jit(solution)/shard_map/ppermute | solution.py:100
  40.1 8.1 %collective-permute-start = (bf16[32,256]{1,0:T(8,128)(2,1)S(1)}, bf16[32,256]{1,0:T(8,128)(2,1)S(1)}, u32[]{:S(2)}, u32[]{:S(2)}) collective-permute-start(bf16[32,256]{1,0:T(8,128)(2,1)S(1)} %get-tuple-element.40), channel_id=1, source_target_pairs={{0,1},{1,2},{2,3},{3,0},{4,5},{5,6},{6,7},{7,4},{8,9},{9,10},{10,1... | collective-permute-start | bytes 49160 | tf_op jit(solution)/shard_map/ppermute | solution.py:100
  41.3 7.4 %collective-permute-start.1 = (bf16[32,256]{1,0:T(8,128)(2,1)S(1)}, bf16[32,256]{1,0:T(8,128)(2,1)S(1)}, u32[]{:S(2)}, u32[]{:S(2)}) collective-permute-start(bf16[32,256]{1,0:T(8,128)(2,1)S(1)} %get-tuple-element.41), channel_id=1, source_target_pairs={{1,0},{2,1},{3,2},{0,3},{5,4},{6,5},{7,6},{4,7},{9,8},{10,9},{11,1... | collective-permute-start | bytes 49160 | tf_op jit(solution)/shard_map/ppermute | solution.py:101
  42.7 3.6 %collective-permute-start.3 = (bf16[16,256]{1,0:T(8,128)(2,1)S(1)}, bf16[16,256]{1,0:T(8,128)(2,1)S(1)}, u32[]{:S(2)}, u32[]{:S(2)}) collective-permute-start(bf16[16,256]{1,0:T(8,128)(2,1)S(1)} %get-tuple-element.43), channel_id=1, source_target_pairs={{16,0},{32,16},{48,32},{64,48},{80,64},{96,80},{112,96},{0,112},{1... | collective-permute-start | bytes 24584 | tf_op jit(solution)/shard_map/ppermute | solution.py:101
  42.8 4.2 %collective-permute-start.4 = (bf16[32,128]{1,0:T(8,128)(2,1)S(1)}, bf16[32,128]{1,0:T(8,128)(2,1)S(1)}, u32[]{:S(2)}, u32[]{:S(2)}) collective-permute-start(bf16[32,128]{1,0:T(8,128)(2,1)S(1)} %get-tuple-element.44), channel_id=1, source_target_pairs={{0,4},{4,8},{8,12},{12,0},{1,5},{5,9},{9,13},{13,1},{2,6},{6,10},{... | collective-permute-start | bytes 24584 | tf_op jit(solution)/shard_map/ppermute | solution.py:100
  43.9 1.5 copy-start.42
  43.9 3.6 %collective-permute-start.5 = (bf16[32,128]{1,0:T(8,128)(2,1)S(1)}, bf16[32,128]{1,0:T(8,128)(2,1)S(1)}, u32[]{:S(2)}, u32[]{:S(2)}) collective-permute-start(bf16[32,128]{1,0:T(8,128)(2,1)S(1)} %get-tuple-element.45), channel_id=1, source_target_pairs={{4,0},{8,4},{12,8},{0,12},{5,1},{9,5},{13,9},{1,13},{6,2},{10,6},{... | collective-permute-start | bytes 24584 | tf_op jit(solution)/shard_map/ppermute | solution.py:101
  48.1 0.6 copy-start.35
  48.7 0.6 copy-start.37
  49.3 0.7 copy-start.36
  50.1 0.7 copy-start.38
  50.8 0.7 copy-start.43
  51.5 0.7 copy-start.45
  52.2 0.7 copy-start.47
  52.9 0.7 copy-start.49
  62.0 0.8 copy-start.7
  62.8 0.8 copy-start.15
  63.6 0.8 copy-start.17
  66.2 4.5 %copy-start.16 = (f32[16,32,256]{2,1,0:T(8,128)S(1)}, f32[16,32,256]{2,1,0:T(8,128)}, u32[]{:S(2)}) copy-start(f32[16,32,256]{2,1,0:T(8,128)} %copy-done.15) | copy-start | bytes 1572868
  69.5 1.2 copy-start.3
  70.6 0.7 copy-start.40
  71.3 12.5 %copy-start.8 = (f32[16,32,256]{2,1,0:T(8,128)S(1)}, f32[16,32,256]{2,1,0:T(8,128)}, u32[]{:S(2)}) copy-start(f32[16,32,256]{2,1,0:T(8,128)} %copy-done.7) | copy-start | bytes 1572868
  71.3 12.6 %copy-start.30 = (f32[32,128]{1,0:T(8,128)S(1)}, f32[32,128]{1,0:T(8,128)}, u32[]{:S(2)}) copy-start(f32[32,128]{1,0:T(8,128)} %copy-done.29) | copy-start | bytes 49156
  73.8 12.2 %copy-start.10 = (f32[16,32,256]{2,1,0:T(8,128)}, f32[16,32,256]{2,1,0:T(8,128)S(1)}, u32[]{:S(2)}) copy-start(f32[16,32,256]{2,1,0:T(8,128)S(1)} %get-tuple-element.47.v.d) | copy-start | bytes 1572868
  73.8 10.1 %copy-start.24 = (f32[16,256]{1,0:T(8,128)S(1)}, f32[16,256]{1,0:T(8,128)}, u32[]{:S(2)}) copy-start(f32[16,256]{1,0:T(8,128)} %copy-done.23) | copy-start | bytes 49156
  73.8 10.1 %copy-start.27 = (f32[32,128]{1,0:T(8,128)S(1)}, f32[32,128]{1,0:T(8,128)}, u32[]{:S(2)}) copy-start(f32[32,128]{1,0:T(8,128)} %copy-done.26) | copy-start | bytes 49156
  73.8 6.9 %collective-permute-start.8 = (bf16[16,256]{1,0:T(8,128)(2,1)S(1)}, bf16[16,256]{1,0:T(8,128)(2,1)S(1)}, u32[]{:S(2)}, u32[]{:S(2)}) collective-permute-start(bf16[16,256]{1,0:T(8,128)(2,1)S(1)} %get-tuple-element.60), channel_id=1, source_target_pairs={{0,16},{16,32},{32,48},{48,64},{64,80},{80,96},{96,112},{112,0},{1... | collective-permute-start | bytes 24584 | tf_op jit(solution)/shard_map/ppermute | solution.py:100
  76.2 7.6 %collective-permute-start.6 = (bf16[32,256]{1,0:T(8,128)(2,1)S(1)}, bf16[32,256]{1,0:T(8,128)(2,1)S(1)}, u32[]{:S(2)}, u32[]{:S(2)}) collective-permute-start(bf16[32,256]{1,0:T(8,128)(2,1)S(1)} %get-tuple-element.58), channel_id=1, source_target_pairs={{0,1},{1,2},{2,3},{3,0},{4,5},{5,6},{6,7},{7,4},{8,9},{9,10},{10,1... | collective-permute-start | bytes 49160 | tf_op jit(solution)/shard_map/ppermute | solution.py:100
  76.3 7.6 %collective-permute-start.7 = (bf16[32,256]{1,0:T(8,128)(2,1)S(1)}, bf16[32,256]{1,0:T(8,128)(2,1)S(1)}, u32[]{:S(2)}, u32[]{:S(2)}) collective-permute-start(bf16[32,256]{1,0:T(8,128)(2,1)S(1)} %get-tuple-element.59), channel_id=1, source_target_pairs={{1,0},{2,1},{3,2},{0,3},{5,4},{6,5},{7,6},{4,7},{9,8},{10,9},{11,1... | collective-permute-start | bytes 49160 | tf_op jit(solution)/shard_map/ppermute | solution.py:101
  78.9 3.9 %collective-permute-start.9 = (bf16[16,256]{1,0:T(8,128)(2,1)S(1)}, bf16[16,256]{1,0:T(8,128)(2,1)S(1)}, u32[]{:S(2)}, u32[]{:S(2)}) collective-permute-start(bf16[16,256]{1,0:T(8,128)(2,1)S(1)} %get-tuple-element.61), channel_id=1, source_target_pairs={{16,0},{32,16},{48,32},{64,48},{80,64},{96,80},{112,96},{0,112},{1... | collective-permute-start | bytes 24584 | tf_op jit(solution)/shard_map/ppermute | solution.py:101
  80.1 3.7 %collective-permute-start.10 = (bf16[32,128]{1,0:T(8,128)(2,1)S(1)}, bf16[32,128]{1,0:T(8,128)(2,1)S(1)}, u32[]{:S(2)}, u32[]{:S(2)}) collective-permute-start(bf16[32,128]{1,0:T(8,128)(2,1)S(1)} %get-tuple-element.62), channel_id=1, source_target_pairs={{0,4},{4,8},{8,12},{12,0},{1,5},{5,9},{9,13},{13,1},{2,6},{6,10},{... | collective-permute-start | bytes 24584 | tf_op jit(solution)/shard_map/ppermute | solution.py:100
  80.7 3.2 %collective-permute-start.11 = (bf16[32,128]{1,0:T(8,128)(2,1)S(1)}, bf16[32,128]{1,0:T(8,128)(2,1)S(1)}, u32[]{:S(2)}, u32[]{:S(2)}) collective-permute-start(bf16[32,128]{1,0:T(8,128)(2,1)S(1)} %get-tuple-element.63), channel_id=1, source_target_pairs={{4,0},{8,4},{12,8},{0,12},{5,1},{9,5},{13,9},{1,13},{6,2},{10,6},{... | collective-permute-start | bytes 24584 | tf_op jit(solution)/shard_map/ppermute | solution.py:101
  86.0 0.7 copy-start.21
  113.6 1.2 copy-start.5
  113.6 1.2 copy-start.20
  115.4 0.7 copy-start.22
  120.9 16.9 %all-to-all-start.3 = ((bf16[128,2,640]{2,1,0:T(2,128)(2,1)}), bf16[128,2,640]{2,1,0:T(2,128)(2,1)}, u32[]{:S(2)}, u32[]{:S(2)}) async-start(bf16[128,2,640]{2,1,0:T(2,128)(2,1)} %reshape.24), calls=%async_computation.3 | async-start | bytes 655360 | tf_op jit(solution)/shard_map/all_to_all | solution.py:461
  126.6 0.7 copy-start.33
  127.3 1.0 copy-start.18
  134.5 0.8 copy-start.12
  141.0 1.2 copy-start.13
  142.2 0.7 copy-start.41
  142.9 10.8 %copy-start.9 = (f32[16,32,256]{2,1,0:T(8,128)S(1)}, f32[16,32,256]{2,1,0:T(8,128)}, u32[]{:S(2)}) copy-start(f32[16,32,256]{2,1,0:T(8,128)} %copy-done.7) | copy-start | bytes 1572868
  142.9 10.8 %copy-start.25 = (f32[16,256]{1,0:T(8,128)S(1)}, f32[16,256]{1,0:T(8,128)}, u32[]{:S(2)}) copy-start(f32[16,256]{1,0:T(8,128)} %copy-done.23) | copy-start | bytes 49156
  142.9 10.8 %copy-start.28 = (f32[32,128]{1,0:T(8,128)S(1)}, f32[32,128]{1,0:T(8,128)}, u32[]{:S(2)}) copy-start(f32[32,128]{1,0:T(8,128)} %copy-done.26) | copy-start | bytes 49156
  142.9 10.8 %copy-start.31 = (f32[32,128]{1,0:T(8,128)S(1)}, f32[32,128]{1,0:T(8,128)}, u32[]{:S(2)}) copy-start(f32[32,128]{1,0:T(8,128)} %copy-done.29) | copy-start | bytes 49156
  145.3 4.9 %collective-permute-start.14 = (bf16[16,256]{1,0:T(8,128)(2,1)S(1)}, bf16[16,256]{1,0:T(8,128)(2,1)S(1)}, u32[]{:S(2)}, u32[]{:S(2)}) collective-permute-start(bf16[16,256]{1,0:T(8,128)(2,1)S(1)} %get-tuple-element.72), channel_id=1, source_target_pairs={{0,16},{16,32},{32,48},{48,64},{64,80},{80,96},{96,112},{112,0},{1... | collective-permute-start | bytes 24584 | tf_op jit(solution)/shard_map/ppermute | solution.py:100
  147.1 6.6 %collective-permute-start.12 = (bf16[32,256]{1,0:T(8,128)(2,1)S(1)}, bf16[32,256]{1,0:T(8,128)(2,1)S(1)}, u32[]{:S(2)}, u32[]{:S(2)}) collective-permute-start(bf16[32,256]{1,0:T(8,128)(2,1)S(1)} %get-tuple-element.70), channel_id=1, source_target_pairs={{0,1},{1,2},{2,3},{3,0},{4,5},{5,6},{6,7},{7,4},{8,9},{9,10},{10,1... | collective-permute-start | bytes 49160 | tf_op jit(solution)/shard_map/ppermute | solution.py:100
  147.4 6.3 %copy-start.34 = (f32[8,128]{1,0:T(8,128)S(1)}, f32[8,128]{1,0:T(8,128)}, u32[]{:S(2)}) copy-start(f32[8,128]{1,0:T(8,128)} %copy-done.32) | copy-start | bytes 12292
  147.4 6.2 %collective-permute-start.13 = (bf16[32,256]{1,0:T(8,128)(2,1)S(1)}, bf16[32,256]{1,0:T(8,128)(2,1)S(1)}, u32[]{:S(2)}, u32[]{:S(2)}) collective-permute-start(bf16[32,256]{1,0:T(8,128)(2,1)S(1)} %get-tuple-element.71), channel_id=1, source_target_pairs={{1,0},{2,1},{3,2},{0,3},{5,4},{6,5},{7,6},{4,7},{9,8},{10,9},{11,1... | collective-permute-start | bytes 49160 | tf_op jit(solution)/shard_map/ppermute | solution.py:101
  149.7 3.1 %collective-permute-start.15 = (bf16[16,256]{1,0:T(8,128)(2,1)S(1)}, bf16[16,256]{1,0:T(8,128)(2,1)S(1)}, u32[]{:S(2)}, u32[]{:S(2)}) collective-permute-start(bf16[16,256]{1,0:T(8,128)(2,1)S(1)} %get-tuple-element.73), channel_id=1, source_target_pairs={{16,0},{32,16},{48,32},{64,48},{80,64},{96,80},{112,96},{0,112},{1... | collective-permute-start | bytes 24584 | tf_op jit(solution)/shard_map/ppermute | solution.py:101
  149.9 3.7 %collective-permute-start.16 = (bf16[32,128]{1,0:T(8,128)(2,1)S(1)}, bf16[32,128]{1,0:T(8,128)(2,1)S(1)}, u32[]{:S(2)}, u32[]{:S(2)}) collective-permute-start(bf16[32,128]{1,0:T(8,128)(2,1)S(1)} %get-tuple-element.74), channel_id=1, source_target_pairs={{0,4},{4,8},{8,12},{12,0},{1,5},{5,9},{9,13},{13,1},{2,6},{6,10},{... | collective-permute-start | bytes 24584 | tf_op jit(solution)/shard_map/ppermute | solution.py:100
  150.2 3.4 %collective-permute-start.17 = (bf16[32,128]{1,0:T(8,128)(2,1)S(1)}, bf16[32,128]{1,0:T(8,128)(2,1)S(1)}, u32[]{:S(2)}, u32[]{:S(2)}) collective-permute-start(bf16[32,128]{1,0:T(8,128)(2,1)S(1)} %get-tuple-element.75), channel_id=1, source_target_pairs={{4,0},{8,4},{12,8},{0,12},{5,1},{9,5},{13,9},{1,13},{6,2},{10,6},{... | collective-permute-start | bytes 24584 | tf_op jit(solution)/shard_map/ppermute | solution.py:101
  153.7 17.8 %copy-start.11 = (f32[16,32,256]{2,1,0:T(8,128)S(1)}, f32[16,32,256]{2,1,0:T(8,128)}, u32[]{:S(2)}) copy-start(f32[16,32,256]{2,1,0:T(8,128)} %copy-done.10) | copy-start | bytes 1572868
  (7 other events, 4.2 us)

commit v2 on v1

v2 whole, which is shorter than its diff:
```python
import jax
import jax.numpy as jnp
from jax import lax
from jax.experimental import pallas as pl
from jax.experimental.pallas import tpu as pltpu
from jax.sharding import PartitionSpec as P

CZ = 16
CX = 32
CY = 256
KC = 32
INNER = 8
CAP = 4
ZN = 128
FB = 256
EXTRA = 2 * CAP
PARTS = EXTRA + 2
LANES = 128
AX = ("gx", "gy", "gz")
F32 = jnp.float32
BF16 = jnp.bfloat16

def sds(shape, dtype=F32):
    return jax.ShapeDtypeStruct(shape, dtype)


class Load:
    def __init__(self, source, buffer, sems, chunks):
        self.buffer = buffer
        self.size = buffer.shape[0] // chunks
        self.copies = []
        for i in range(chunks):
            part = pl.ds(i * self.size, self.size)
            self.copies.append(
                pltpu.make_async_copy(source.at[part], buffer.at[part], sems.at[i])
            )

    def start(self, i):
        self.copies[i].start()

    def wait(self, i):
        if self.copies[i] is not None:
            self.copies[i].wait()
            self.copies[i] = None

    def full(self):
        for i in range(len(self.copies)):
            self.wait(i)
        return self.buffer

    def __getitem__(self, z):
        self.wait(z // self.size)
        return self.buffer[z]


class Store:
    def __init__(self, target, buffer, sems, chunks):
        self.buffer, self.target, self.sems = buffer, target, sems
        self.size = buffer.shape[0] // chunks
        self.copies = [None] * chunks

    def flush(self, i):
        part = pl.ds(i * self.size, self.size)
        copy = pltpu.make_async_copy(self.buffer.at[part], self.target.at[part], self.sems.at[i])
        copy.start()
        self.copies[i] = copy

    def __setitem__(self, z, value):
        self.buffer[z] = value
        if z % self.size == self.size - 1:
            self.flush(z // self.size)

    def __getitem__(self, z):
        return self.buffer[z]

    def send(self):
        for i, copy in enumerate(self.copies):
            if copy is None:
                self.flush(i)

    def finish(self):
        self.send()
        for copy in self.copies:
            copy.wait()


SPACE = {"a": pl.ANY, "o": pltpu.HBM, "s": pltpu.SMEM, "v": pltpu.VMEM, "h": pltpu.HBM, "c": pltpu.HBM, "p": pltpu.HBM}
COPIED = "hcpa"
CHUNKS = 4


def spec(mode):
    return pl.BlockSpec(memory_space=SPACE[mode])


def run(body, ins, outs, scratch=(), mixed=()):
    moved = [(m, a) for side in (ins, outs) for m, a in side if m in COPIED]
    n_chunks = [1 if m in "ha" else CHUNKS for m, _ in moved]
    buffers = [pltpu.VMEM(a.shape, a.dtype) for m, a in moved if m != "p"]
    sems = [pltpu.SemaphoreType.DMA((n,)) for n in n_chunks]
    passed = [sds(a.shape, a.dtype) for m, a in ins if m == "p"]
    n_in, n_out, n_pass, n_own = len(ins), len(outs), len(passed), len(scratch)

    def kernel(*refs):
        refs = list(refs)

        def take(n):
            head = refs[:n]
            del refs[:n]
            return head

        in_refs, out_refs, pass_refs, own = take(n_in), take(n_out), take(n_pass), take(n_own)
        bufs = take(len(buffers))
        given, made, loads, stores = [], [], [], []
        for (m, _), ref in zip(ins, in_refs):
            if m in COPIED:
                buf = pass_refs.pop(0) if m == "p" else bufs.pop(0)
                given.append(Load(ref, buf, refs.pop(0), 1 if m in "ha" else CHUNKS))
                loads.append(given[-1])
            else:
                given.append(ref)
        for (m, _), ref in zip(outs, out_refs):
            if m in COPIED:
                made.append(Store(ref, bufs.pop(0), refs.pop(0), 1 if m in "ha" else CHUNKS))
                stores.append(made[-1])
            else:
                made.append(ref)
        groups = {id(given[g[0]]): [given[i] for i in g] for g in mixed}
        joined = [id(given[i]) for g in mixed for i in g]
        for x in loads:
            for i in range(len(x.copies)):
                if id(x) not in joined:
                    x.start(i)
                for one in groups.get(id(x), ()):
                    one.start(i)
        body(given, made, *own)
        for x in stores:
            x.send()
        for x in loads:
            x.full()
        for x in stores:
            x.finish()

    return pl.pallas_call(
        kernel,
        out_shape=tuple(
            pltpu.HBM(a.shape, a.dtype) if m in "hco" else a for m, a in outs
        )
        + tuple(passed),
        in_specs=[spec(m) for m, _ in ins],
        out_specs=tuple(spec(m) for m, _ in outs) + (spec("v"),) * n_pass,
        scratch_shapes=tuple(scratch) + tuple(buffers) + tuple(sems),
        compiler_params=pltpu.CompilerParams(vmem_limit_bytes=24 * 1024 * 1024),
    )(*[pltpu.with_memory_space_constraint(a, pltpu.HBM) if m in "hcp" else a for m, a in ins])


def full(x):
    return x.full() if isinstance(x, Load) else x


def raw(x):
    return x.buffer if isinstance(x, (Load, Store)) else x


def iota(shape, dim):
    return lax.broadcasted_iota(jnp.int32, shape, dim)


def total(x):
    return jnp.sum(jnp.sum(x, axis=1, keepdims=True), axis=0, keepdims=True)


def fold(x):
    half = x[:, :LANES] + x[:, LANES:]
    return half[0:8] + half[8:16] + half[16:24] + half[24:32]


def split3(x):
    high = x.astype(BF16).astype(F32)
    rest = x - high
    mid = rest.astype(BF16).astype(F32)
    return high, mid, rest - mid


def face_store(plane_of, refs, xs_lo, xs_hi):
    zlo, zhi, xlo, xhi, ylo, yhi = (raw(x) for x in refs)
    lane = iota((CX, LANES), 1)
    acc_lo = jnp.zeros((CX, LANES), F32)
    acc_hi = jnp.zeros((CX, LANES), F32)
    for z in range(CZ):
        plane = plane_of(z)
        if z == 0:
            zlo[...] = plane.astype(BF16)
        if z == CZ - 1:
            zhi[...] = plane.astype(BF16)
        xs_lo[z : z + 1, :] = plane[0:1, :]
        xs_hi[z : z + 1, :] = plane[CX - 1 : CX, :]
        acc_lo = jnp.where(lane == z, plane[:, 0:1], acc_lo)
        acc_hi = jnp.where(lane == z, plane[:, CY - 1 : CY], acc_hi)
    xlo[...] = xs_lo[...].astype(BF16)
    xhi[...] = xs_hi[...].astype(BF16)
    ylo[...] = acc_lo.astype(BF16)
    yhi[...] = acc_hi.astype(BF16)


FACE_OUTS = (
    sds((CX, CY), BF16),
    sds((CX, CY), BF16),
    sds((CZ, CY), BF16),
    sds((CZ, CY), BF16),
    sds((CX, LANES), BF16),
    sds((CX, LANES), BF16),
)
FACE_SCRATCH = (pltpu.VMEM((CZ, CY), F32), pltpu.VMEM((CZ, CY), F32))


def exchange(faces):
    out = []
    for axis, (low, high) in zip(("gz", "gx", "gy"), (faces[0:2], faces[2:4], faces[4:6])):
        n = lax.axis_size(axis)
        forward = [(i, (i + 1) % n) for i in range(n)]
        backward = [((i + 1) % n, i) for i in range(n)]
        out.append(lax.ppermute(high, axis, forward))
        out.append(lax.ppermute(low, axis, backward))
    return out


def slots(zrow):
    shape = (ZN, ZN)
    sub, lane = iota(shape, 0), iota(shape, 1)
    row = jnp.broadcast_to(zrow, shape)
    zcol = jnp.sum(jnp.where(sub == lane, row, 0), axis=1, keepdims=True)
    same = row == zcol
    slot_row = jnp.sum(jnp.where(same & (sub < lane), 1, 0), axis=0, keepdims=True)
    slot_col = jnp.sum(jnp.where(same & (lane < sub), 1, 0), axis=1, keepdims=True)
    return zrow + ZN * slot_row, zcol + ZN * slot_col


def part_rows(part, first=0, count=ZN):
    return pl.ds(first * PARTS + part, count, stride=PARTS)


def store_send(send, blocks, zrow, u_rows, scalars, tile, wide):
    key, _ = slots(zrow)
    put = jnp.where(iota((CAP * ZN, ZN), 0) == key, 1.0, 0.0).astype(BF16)
    placed = jnp.dot(put, blocks, preferred_element_type=F32)
    for k in range(CAP):
        rows = placed[k * ZN : (k + 1) * ZN, :]
        wide[part_rows(k), :] = rows[:, :LANES]
        wide[part_rows(CAP + k), :] = rows[:, LANES:]
    high = u_rows.astype(BF16).astype(F32)
    tile[0:32, :] = high
    tile[32:64, :] = u_rows - high
    tile[64:128, :] = jnp.zeros((64, LANES), F32)
    for i, value in enumerate(scalars):
        for j, piece in enumerate(split3(value)):
            at = 64 + 3 * i + j
            tile[at : at + 1, :] = jnp.broadcast_to(piece, (1, LANES))
    wide[part_rows(EXTRA), :] = tile[...].T
    wide[part_rows(EXTRA + 1), :] = jnp.zeros((ZN, LANES), F32)
    send[...] = wide[...].astype(BF16)


def label_columns(label, tile):
    tile[...] = jnp.zeros((LANES, LANES), F32)
    tile[0:CZ, 0:CX] = full(label)[...].astype(F32)
    return tile[...].T[0:CX, :]


def coarse_rows(line_of, columns, factor, rows):
    lane = iota((CX, LANES), 1)
    kind = lane.astype(F32)
    sub = iota((CX, LANES), 0)
    acc = jnp.zeros((CX, LANES), F32)
    for z in range(CZ):
        acc = acc + jnp.where(columns[:, z : z + 1] == kind, line_of(z), 0.0)
    g_row = jnp.broadcast_to(jnp.sum(acc, axis=0, keepdims=True), (CX, LANES))
    g_col = jnp.sum(jnp.where(sub == lane, g_row, 0.0), axis=1, keepdims=True)
    g = jnp.broadcast_to(g_col, (KC, LANES))
    factor = full(factor)
    for t in range(32):
        rows[t : t + 1, :] = jnp.sum(
            factor[:, t * LANES : (t + 1) * LANES] * g, axis=0, keepdims=True
        )
    return rows[...]


def face_blocks(field):
    return jnp.concatenate([field[0], field[1], field[CZ - 2], field[CZ - 1]], axis=0).astype(BF16)


def pack_body(ins, outs, tile, rows, wide, xs_lo, xs_hi):
    label, zrow, r, factor, k = ins
    send, *faces = outs
    columns = label_columns(label, tile)
    u_rows = coarse_rows(
        lambda z: jnp.sum(r[z], axis=1, keepdims=True), columns, factor, rows
    )
    store_send(raw(send), face_blocks(r), full(zrow)[...], u_rows, (), tile, wide)
    send.send()
    face_store(lambda z: k[z], faces, xs_lo, xs_hi)


def lift_store(out, wide, tail, zone):
    factor = zone[0]
    lane = iota((1, LANES), 1)
    u = jnp.where(lane < 32, tail + pltpu.roll(tail, LANES - 32, 1), 0.0)
    high = u.astype(BF16).astype(F32)
    both = high + pltpu.roll(u - high, 32, 1)
    size = ZN // CHUNKS
    for i in range(CHUNKS):
        at = i * size
        x = jnp.concatenate(
            [
                jnp.concatenate(
                    [wide[part_rows(k, at, size), :], wide[part_rows(CAP + k, at, size), :]],
                    axis=1,
                )
                for k in range(CAP)
            ],
            axis=0,
        ).astype(BF16)
        lifted = jnp.dot(x, factor, preferred_element_type=F32).astype(BF16)
        back = lax.dot_general(
            lifted, factor, (((1,), (1,)), ((), ())), preferred_element_type=F32
        )
        for k in range(CAP):
            rows = back[k * size : (k + 1) * size, :]
            wide[part_rows(k, at, size), :] = rows[:, :LANES]
            wide[part_rows(CAP + k, at, size), :] = rows[:, LANES:]
        wide[part_rows(EXTRA, at, size), :] = jnp.broadcast_to(both, (size, LANES))
        part = slice(at * PARTS, (at + size) * PARTS)
        out.buffer[part, :] = wide[part, :].astype(BF16)
        out.flush(i)


def tail_sum(wide):
    return jnp.sum(wide[part_rows(EXTRA), :], axis=0, keepdims=True)


def lift0_body(ins, outs, wide, sem):
    got, zone = ins
    out, kept = outs
    keep = pltpu.make_async_copy(got, kept, sem)
    keep.start()
    wide[...] = got[...].astype(F32)
    lift_store(out, wide, tail_sum(wide), full(zone))
    keep.wait()


def lift1_body(ins, outs, wide):
    zone, got0, got1 = ins
    out, scalars = outs
    store, scalars = scalars, raw(scalars)
    wide[...] = got1[...].astype(F32)
    tail1 = tail_sum(wide)
    lane = iota((1, LANES), 1)

    def scalar(i):
        keep = (lane >= 64 + 3 * i) & (lane < 67 + 3 * i)
        return jnp.sum(jnp.where(keep, tail1, 0.0), axis=1, keepdims=True)

    rz, curvature = scalar(0), scalar(1)
    alpha = rz / curvature
    scalars[0:1, :] = jnp.broadcast_to(alpha, (1, LANES))
    scalars[1:2, :] = jnp.broadcast_to(rz, (1, LANES))
    scalars[2:3, :] = jnp.broadcast_to(curvature, (1, LANES))
    scalars[3:8, :] = jnp.zeros((5, LANES), F32)
    store.send()
    wide[...] = full(got0)[...].astype(F32) - alpha * wide[...]
    lift_store(out, wide, tail_sum(wide), full(zone))


def minus_neighbours(p, below, above, cz_below, cz_above, cx, cy):
    tx = cx * p
    ty = cy * p
    out = p - cx * pltpu.roll(p, CX - 1, 0) - pltpu.roll(tx, 1, 0)
    out = out - cy * pltpu.roll(p, CY - 1, 1) - pltpu.roll(ty, 1, 1)
    if below is not None:
        out = out - cz_below * below
    if above is not None:
        out = out - cz_above * above
    return out


def apply_scaled(p_of, cz, cx, cy, e):
    acc = jnp.zeros((8, LANES), F32)
    below, now = None, p_of(0)
    for z in range(CZ):
        above = p_of(z + 1) if z + 1 < CZ else None
        image = minus_neighbours(
            now,
            below,
            above,
            cz[z - 1] if z else None,
            cz[z] if z + 1 < CZ else None,
            cx[z],
            cy[z],
        )
        e[z] = image
        acc = acc + fold(now * image)
        below, now = now, above
    return total(acc)


def cg(cz, cx, cy, s, p, q, e, y, rho, local):
    def first_of(z):
        p[z] = q[z]
        return q[z]

    a = rho / apply_scaled(first_of, cz, cx, cy, e)

    def move(a, started):
        acc = jnp.zeros((8, LANES), F32)
        for z in range(CZ):
            y[z] = y[z] + a * p[z] if started else a * p[z]
            left = q[z] - a * e[z]
            q[z] = left
            acc = acc + fold(left * left)
        return total(acc)

    new = move(a, False)
    carry = (new, new / rho)
    cz, cx, cy = raw(cz), raw(cx), raw(cy)

    def advance(beta):
        def next_of(z):
            value = q[z] + beta * p[z]
            p[z] = value
            return value

        return apply_scaled(next_of, cz, cx, cy, e)

    def step(_, carry):
        rho, beta = carry
        new = move(rho / advance(beta), True)
        return new, new / rho

    rho, beta = lax.fori_loop(0, INNER - 2, step, carry)
    a = rho / advance(beta)
    for z in range(CZ):
        local[z] = s[z] * (y[z] + a * p[z])


def start_cg(r_of, s, q):
    acc = jnp.zeros((8, LANES), F32)
    for z in range(CZ):
        left = s[z] * r_of(z)
        q[z] = left
        acc = acc + fold(left * left)
    return total(acc)


def solve0_body(ins, outs, p, q, e, y):
    flags, *halos, k, storage, r = ins
    local, s, sinv, cz, cx, cy, bounds_zx, bounds_y = outs
    kzl, kzh, kxl, kxh, kyl, kyh = (full(h) for h in halos)
    zx, by = raw(bounds_zx), raw(bounds_y)
    sub, lane = iota((CX, CY), 0), iota((CX, CY), 1)
    zl, zh = flags[0] * kzl[...].astype(F32), flags[1] * kzh[...].astype(F32)
    xl, xh = flags[2] * kxl[...].astype(F32), flags[3] * kxh[...].astype(F32)
    yl, yh = flags[4] * kyl[...].astype(F32), flags[5] * kyh[...].astype(F32)
    zx[0:32, :] = flags[0] * 0.5 * (k[0] + zl)
    zx[32:64, :] = flags[1] * 0.5 * (k[CZ - 1] + zh)
    lane_half = iota((CX, LANES), 1)
    y_edge_lo = jnp.zeros((CX, LANES), F32)
    y_edge_hi = jnp.zeros((CX, LANES), F32)
    for z in range(CZ):
        c = k[z]
        x_row_lo, x_row_hi = xl[z : z + 1, :], xh[z : z + 1, :]
        zx[64 + z : 65 + z, :] = flags[2] * 0.5 * (c[0:1, :] + x_row_lo)
        zx[80 + z : 81 + z, :] = flags[3] * 0.5 * (c[CX - 1 : CX, :] + x_row_hi)
        y_edge_lo = jnp.where(lane_half == z, c[:, 0:1], y_edge_lo)
        y_edge_hi = jnp.where(lane_half == z, c[:, CY - 1 : CY], y_edge_hi)
        around = (k[z - 1] if z else zl) + (k[z + 1] if z + 1 < CZ else zh)
        right = pltpu.roll(c, CX - 1, 0)
        around = around + jnp.where(sub == CX - 1, x_row_hi, right)
        around = around + jnp.where(sub == 0, x_row_lo, pltpu.roll(c, 1, 0))
        ahead = pltpu.roll(c, CY - 1, 1)
        end = pltpu.roll(yh, LANES - 1 - z, 1)
        around = around + jnp.where(lane == CY - 1, jnp.concatenate([end, end], axis=1), ahead)
        begin = pltpu.roll(yl, (LANES - z) % LANES, 1)
        around = around + jnp.where(
            lane == 0, jnp.concatenate([begin, begin], axis=1), pltpu.roll(c, 1, 1)
        )
        diagonal = storage[z] + 3.0 * c + 0.5 * around
        root = lax.rsqrt(diagonal)
        root = root * (1.5 - 0.5 * diagonal * root * root)
        s[z] = root
        sinv[z] = diagonal * root
        cx[z] = jnp.where(sub == CX - 1, 0.0, 0.5 * (c + right) * root * pltpu.roll(root, CX - 1, 0))
        cy[z] = jnp.where(lane == CY - 1, 0.0, 0.5 * (c + ahead) * root * pltpu.roll(root, CY - 1, 1))
        if z:
            cz[z - 1] = 0.5 * (k[z - 1] + c) * s[z - 1] * root
    cz[CZ - 1] = jnp.zeros((CX, CY), F32)
    by[0:32, :] = flags[4] * 0.5 * (y_edge_lo + yl)
    by[32:64, :] = flags[5] * 0.5 * (y_edge_hi + yh)
    bounds_zx.send()
    bounds_y.send()
    rho = start_cg(lambda z: r[z], s, q)
    cg(raw(cz), raw(cx), raw(cy), raw(s), p, q, e, y, rho, local)


def solve1_body(ins, outs, p, q, e, y):
    scalars, r, image, s, cz, cx, cy = ins
    (local,) = outs
    alpha = full(scalars)[0:1, 0:1]
    rho = start_cg(lambda z: r[z] - alpha * image[z], s, q)
    cg(cz, cx, cy, raw(s), p, q, e, y, rho, local)


def combine_body(ins, outs, xs_lo, xs_hi, tile, wide, sems):
    got, zrow, label, factor, local, *_ = ins
    out, kept, *faces = outs
    lane, sub = iota((CX, LANES), 1), iota((CX, LANES), 0)
    wide[...] = got[...].astype(F32)
    _, key = slots(full(zrow)[...])
    columns = label_columns(label, tile)
    factor = full(factor)
    flipped = wide[part_rows(EXTRA), :].T
    u = flipped[0:32, :] + flipped[32:64, :]
    acc = jnp.zeros((KC, LANES), F32)
    for t in range(32):
        acc = acc + factor[:, t * LANES : (t + 1) * LANES] * u[t : t + 1, :]
    coef_col = jnp.sum(acc, axis=1, keepdims=True)
    coef = jnp.sum(jnp.where(sub == lane, coef_col, 0.0), axis=0, keepdims=True)
    coef = jnp.broadcast_to(coef, (CX, LANES))
    back = jnp.concatenate(
        [
            jnp.concatenate([wide[part_rows(k), :], wide[part_rows(CAP + k), :]], axis=1)
            for k in range(CAP)
        ],
        axis=0,
    ).astype(BF16)
    take = jnp.where(iota((ZN, CAP * ZN), 1) == key, 1.0, 0.0).astype(BF16)
    placed = jnp.dot(take, back, preferred_element_type=F32)
    kind = lane.astype(F32)
    order = {0: 0, 1: 1, CZ - 2: 2, CZ - 1: 3}
    for z in range(CZ):
        value = jnp.sum(
            jnp.where(columns[:, z : z + 1] == kind, coef, 0.0), axis=1, keepdims=True
        )
        plane = local[z] + value
        if z in order:
            at = order[z] * CX
            plane = plane + placed[at : at + CX, :]
        out[z] = plane
    keep = pltpu.make_async_copy(out, kept, sems)
    keep.start()
    face_store(lambda z: out[z], faces, xs_lo, xs_hi)
    keep.wait()


def apply_plane(z, v, sinv, cz, cx, cy, bounds, halos, masks):
    bzl, bzh, bxl, bxh, byl, byh = bounds
    hzl, hzh, hxl, hxh, hyl, hyh = halos
    first_row, last_row, first_lane, last_lane = masks
    inverse = sinv[z]
    scaled = minus_neighbours(
        v[z] * inverse,
        v[z - 1] * sinv[z - 1] if z else None,
        v[z + 1] * sinv[z + 1] if z + 1 < CZ else None,
        cz[z - 1] if z else None,
        cz[z] if z + 1 < CZ else None,
        cx[z],
        cy[z],
    )
    out = scaled * inverse
    out = out - jnp.where(first_row, bxl[z : z + 1, :] * hxl[z : z + 1, :], 0.0)
    out = out - jnp.where(last_row, bxh[z : z + 1, :] * hxh[z : z + 1, :], 0.0)
    low = pltpu.roll(byl * hyl, (LANES - z) % LANES, 1)
    high = pltpu.roll(byh * hyh, LANES - 1 - z, 1)
    out = out - jnp.where(first_lane, jnp.concatenate([low, low], axis=1), 0.0)
    out = out - jnp.where(last_lane, jnp.concatenate([high, high], axis=1), 0.0)
    if z == 0:
        out = out - bzl * hzl
    if z == CZ - 1:
        out = out - bzh * hzh
    return out


def apply_inputs(zx, by, halo_refs):
    halos = [full(h)[...].astype(F32) for h in halo_refs]
    zx, by = full(zx), full(by)
    bounds = (zx[0:32, :], zx[32:64, :], zx[64:80, :], zx[80:96, :], by[0:32, :], by[32:64, :])
    sub, lane = iota((CX, CY), 0), iota((CX, CY), 1)
    return bounds, halos, (sub == 0, sub == CX - 1, lane == 0, lane == CY - 1)


def apply0_body(ins, outs, tile, rows, wide):
    v, sinv, cz, cx, cy, zx, by, r, *halo_refs, label, zrow, factor = ins
    image, send = outs
    bounds, halos, masks = apply_inputs(zx, by, halo_refs)
    rz = jnp.zeros((8, LANES), F32)
    curvature = jnp.zeros((8, LANES), F32)
    lines = []
    for z in range(CZ):
        out = apply_plane(z, v, sinv, cz, cx, cy, bounds, halos, masks)
        image[z] = out
        lines.append(jnp.sum(out, axis=1, keepdims=True))
        rz = rz + fold(r[z] * v[z])
        curvature = curvature + fold(v[z] * out)
    columns = label_columns(label, tile)
    u_rows = coarse_rows(lambda z: lines[z], columns, factor, rows)
    sums = (total(rz), total(curvature))
    store_send(raw(send), face_blocks(image), full(zrow)[...], u_rows, sums, tile, wide)


def apply1_body(ins, outs):
    v, sinv, cz, cx, cy, zx, by, r, image0, *halo_refs, scalars = ins
    image, sums = outs
    bounds, halos, masks = apply_inputs(zx, by, halo_refs)
    alpha = full(scalars)[0:1, 0:1]
    sums3 = [jnp.zeros((8, LANES), F32) for _ in range(3)]
    for z in range(CZ):
        out = apply_plane(z, v, sinv, cz, cx, cy, bounds, halos, masks)
        image[z] = out
        at = v[z]
        sums3[0] = sums3[0] + fold((r[z] - alpha * image0[z]) * at)
        sums3[1] = sums3[1] + fold(at * out)
        sums3[2] = sums3[2] + fold(at * image0[z])
    lane = iota((ZN, LANES), 1)
    row = jnp.zeros((ZN, LANES), F32)
    for i in range(3):
        row = jnp.where(lane == i, total(sums3[i]), row)
    sums[...] = row


def final_body(ins, outs):
    scalars, got, d, v, r, image0, image1 = ins
    solution, residual = outs
    scalars = full(scalars)
    sums = jnp.sum(got[...], axis=0, keepdims=True)
    alpha0, rz0, curvature0 = scalars[0:1, 0:1], scalars[1:2, 0:1], scalars[2:3, 0:1]
    rz1, vav, vad = sums[:, 0:1], sums[:, 1:2], sums[:, 2:3]
    beta = rz1 / rz0
    alpha1 = rz1 / (vav + 2.0 * beta * vad + beta * beta * curvature0)
    mix = alpha0 + alpha1 * beta
    for z in range(CZ):
        solution[z] = mix * d[z] + alpha1 * v[z]
        residual[z] = r[z] - mix * image0[z] - alpha1 * image1[z]


FIELD = sds((CZ, CX, CY))
FIELD_SCRATCH = pltpu.VMEM((CZ, CX, CY), F32)
PACKED = sds((ZN * PARTS, LANES), BF16)
WIDE = pltpu.VMEM((ZN * PARTS, LANES), F32)
TILE = pltpu.VMEM((LANES, LANES), F32)
ROWS = pltpu.VMEM((KC, LANES), F32)


def swap(x):
    return lax.all_to_all(x, AX, split_axis=0, concat_axis=0, tiled=True)


def swap_packed(x):
    return swap(x.reshape(ZN, PARTS // 2, 2, LANES)).reshape(ZN * PARTS, LANES)


def each(mode, *arrays):
    return [(mode, a) for a in arrays]


def per_device(r, storage, k, label, zone_of_block, factor, zone_factor):
    zrow = zone_of_block.reshape(1, ZN)
    label = label.reshape(CZ, CX)
    flags = jnp.stack(
        [
            (lax.axis_index(axis) != edge).astype(F32)
            for axis in ("gz", "gx", "gy")
            for edge in (0, lax.axis_size(axis) - 1)
        ]
    )
    send0, *k_faces = run(
        pack_body,
        each("h", label, zrow) + each("c", r) + each("h", factor) + each("c", k),
        each("h", PACKED, *FACE_OUTS),
        (TILE, ROWS, WIDE) + FACE_SCRATCH,
    )
    got0 = swap_packed(send0)
    k_halos = exchange(k_faces)
    got0, *k_halos = lax.optimization_barrier((got0, *k_halos))
    back0, got0 = run(
        lift0_body,
        each("v", got0) + each("h", zone_factor),
        each("c", PACKED) + each("o", PACKED),
        (WIDE, pltpu.SemaphoreType.DMA),
    )
    back0 = swap_packed(back0)
    local, s, sinv, cz, cx, cy, *bounds = run(
        solve0_body,
        each("s", flags) + each("a", *k_halos) + each("c", k, storage, r),
        each("c", *(FIELD,) * 6) + each("h", sds((96, CY)), sds((64, LANES))),
        (FIELD_SCRATCH,) * 4,
        ((7, 8, 9),),
    )
    matrix = (sinv, cz, cx, cy, *bounds)

    def combine(local, back, more):
        field, kept, *rest = run(
            combine_body,
            each("v", back)
            + each("h", zrow, label, factor)
            + each("c", local)
            + each("p", *matrix, *more),
            each("v", FIELD) + each("o", FIELD) + each("v", *FACE_OUTS),
            FACE_SCRATCH + (TILE, WIDE, pltpu.SemaphoreType.DMA),
        )
        return field, kept, exchange(rest[:6]), rest[6:]

    field, d, halos, passed = combine(local, back0, (r,))
    image0, send1 = run(
        apply0_body,
        each("v", field, *passed, *halos) + each("h", label, zrow, factor),
        each("c", FIELD) + each("h", PACKED),
        (TILE, ROWS, WIDE),
    )
    got1 = swap_packed(send1)
    back1, scalars = run(
        lift1_body,
        each("h", zone_factor, got0) + each("v", got1),
        each("c", PACKED) + each("h", sds((8, LANES))),
        (WIDE,),
    )
    back1 = swap_packed(back1)
    (local,) = run(
        solve1_body,
        each("h", scalars) + each("c", r, image0, s, cz, cx, cy),
        each("c", FIELD),
        (FIELD_SCRATCH,) * 4,
        ((1, 2, 3), (4, 5, 6)),
    )
    field, v, halos, passed = combine(local, back1, (r, image0))
    image1, sums = run(
        apply1_body,
        each("v", field, *passed, *halos) + each("h", scalars),
        each("c", FIELD) + each("v", sds((ZN, LANES))),
    )
    return run(
        final_body,
        each("h", scalars) + each("v", swap(sums)) + each("c", d, v, r, image0, image1),
        each("c", FIELD, FIELD),
        (),
        ((2, 3, 4, 5, 6),),
    )


def solution(mesh):
    field = P("gz", "gx", "gy")
    in_specs = (field, field, field, field, P(AX, None), P(AX, None), P(AX, None, None))
    return jax.shard_map(
        per_device, mesh=mesh, in_specs=in_specs, out_specs=(field, field), check_vma=False
    )
```

time: 174 us -> 139 us (0.80)
  local copies, waits for them, and re-layouts: 40.5 us -> 0.13 us
  blocking collectives: 59.2 us -> 37.5 us
  Pallas kernels: 25.5 us -> 44.9 us
  starting transfers between devices: 35 us -> 45 us
  other arithmetic: 6.36 us -> 0.01 us
  waiting for transfers between devices: 5.35 us -> 9.51 us
    unnamed x116 -> x12, local copies, waits for them, and re-layouts: 39.8 us -> 0.03 us
    all_to_all x3 -> x2, blocking collectives: 59.2 us -> 37.5 us  [swap(): return lax.all_to_all(x, AX, split_axis=0, concat_axis=0, tiled=True)]
    pallas_call x11 -> x10, Pallas kernels: 25.5 us -> 44.9 us  [run(): pl.pallas_call(kernel, out_shape=tuple((pltpu.HBM(a.shape, a.dtype) if m...]
    all_to_all x2 -> x3, starting transfers between devices: 11.4 us -> 23.2 us  [swap(): return lax.all_to_all(x, AX, split_axis=0, concat_axis=0, tiled=True)]
    all_to_all x4 -> x0, other arithmetic: 6.35 us -> none  [swap(): return lax.all_to_all(x, AX, split_axis=0, concat_axis=0, tiled=True)]
    all_to_all x2 -> x3, waiting for transfers between devices: 2.48 us -> 6.09 us  [swap(): return lax.all_to_all(x, AX, split_axis=0, concat_axis=0, tiled=True)]
  transfers between devices with their start and end apart: 20 -> 21, of which waited for: 5 -> 9; matrix products, arithmetic and copies ran while one was open for 0% -> 0% of each run, Pallas kernels for 9% -> 14%
where the time goes in v2:
time: 139 us; the launch traced here: 138 us
  starting transfers between devices  45 us (32%)
  Pallas kernels  44.9 us (32%)
  blocking collectives  37.5 us (27%)
  waiting for transfers between devices  9.51 us (7%)
    pallas_call x10, Pallas kernels, run(): pl.pallas_call(kernel, out_shape=tuple((pltpu.HBM(a.shape, a.dtype) if m...  44.9 us
    all_to_all x2, blocking collectives, swap(): return lax.all_to_all(x, AX, split_axis=0, concat_axis=0, tiled=True)  37.5 us
    all_to_all x3, starting transfers between devices, swap(): return lax.all_to_all(x, AX, split_axis=0, concat_axis=0, tiled=True)  23.2 us
    ppermute x9, starting transfers between devices, exchange(): out.append(lax.ppermute(low, axis, backward))  12.1 us
    ppermute x9, starting transfers between devices, exchange(): out.append(lax.ppermute(high, axis, forward))  9.62 us
    all_to_all x3, waiting for transfers between devices, swap(): return lax.all_to_all(x, AX, split_axis=0, concat_axis=0, tiled=True)  6.09 us
  transfers between devices with their start and end apart: 21, of which 9 were waited for; matrix products, arithmetic and copies ran while one was open for 0% of the time, Pallas kernels for 14%

profile of v2, /device:TPU:1, one launch (start us, length us, event | category | flops | bytes accessed | tf_op | source)
XLA Modules:
  0.0 138.1 jit_solution(10794567582261280000)
XLA Ops:
  0.6 3.6 %shard_map.86 = (bf16[1280,128]{1,0:T(8,128)(2,1)}, bf16[32,256]{1,0:T(8,128)(2,1)}, bf16[32,256]{1,0:T(8,128)(2,1)}, bf16[16,256]{1,0:T(8,128)(2,1)}, bf16[16,2...) custom-call(s32[16,32]{1,0:T(8,128)} %bitcast.30, s32[1,128]{1,0:T(1,128)} %bitcast.34, ...), custom_call_target="tpu_custom_call" | custom-call | tf_op jit(solution)/shard_map/pallas_call | solution.py:144
  4.2 0.0 copy-start.5
  4.2 0.0 copy-start.1
  4.3 0.0 copy-start
  4.3 0.0 copy-start.4
  4.3 0.0 copy-start.3
  4.3 11.5 %all-to-all-start = ((bf16[128,5,2,128]{3,2,1,0:T(2,128)(2,1)}), bf16[128,5,2,128]{3,2,1,0:T(2,128)(2,1)S(1)}, u32[]{:S(2)}, u32[]{:S(2)}) async-start(bf16[128,5,2,128]{3,2,1,0:T(2,128)(2,1)} %bitcast.27), calls=%async_computation | async-start | bytes 655360 | tf_op jit(solution)/shard_map/all_to_all | solution.py:653
  15.8 0.0 copy-start.2
  15.8 0.0 copy-done.5
  15.8 1.8 %collective-permute-start.2 = (bf16[16,256]{1,0:T(8,128)(2,1)S(1)}, bf16[16,256]{1,0:T(8,128)(2,1)S(1)}, u32[]{:S(2)}, u32[]{:S(2)}) collective-permute-start(bf16[16,256]{1,0:T(8,128)(2,1)S(1)} %copy-done.5), channel_id=1, source_target_pairs={{0,16},{16,32},{32,48},{48,64},{64,80},{80,96},{96,112},{112,0},{1... | collective-permute-start | bytes 24584 | tf_op jit(solution)/shard_map/ppermute | solution.py:223
  17.6 0.0 copy-done.1
  17.6 1.2 collective-permute-start
  18.8 1.4 %collective-permute-start.1 = (bf16[32,256]{1,0:T(8,128)(2,1)S(1)}, bf16[32,256]{1,0:T(8,128)(2,1)S(1)}, u32[]{:S(2)}, u32[]{:S(2)}) collective-permute-start(bf16[32,256]{1,0:T(8,128)(2,1)S(1)} %copy-done), channel_id=1, source_target_pairs={{1,0},{2,1},{3,2},{0,3},{5,4},{6,5},{7,6},{4,7},{9,8},{10,9},{11,1... | collective-permute-start | bytes 49160 | tf_op jit(solution)/shard_map/ppermute | solution.py:224
  20.3 0.0 collective-permute-start.3
  20.3 0.0 copy-done.3
  20.3 1.3 collective-permute-start.4
  21.6 0.0 collective-permute-done.2.refs_3_
  21.6 1.5 %collective-permute-start.5 = (bf16[32,128]{1,0:T(8,128)(2,1)S(1)}, bf16[32,128]{1,0:T(8,128)(2,1)S(1)}, u32[]{:S(2)}, u32[]{:S(2)}) collective-permute-start(bf16[32,128]{1,0:T(8,128)(2,1)S(1)} %copy-done.2), channel_id=1, source_target_pairs={{4,0},{8,4},{12,8},{0,12},{5,1},{9,5},{13,9},{1,13},{6,2},{10,6},{... | collective-permute-start | bytes 24584 | tf_op jit(solution)/shard_map/ppermute | solution.py:224
  23.0 0.6 collective-permute-done.3.refs_4_
  23.7 0.7 collective-permute-done.4.refs_5_
  24.4 0.0 collective-permute-done.5.refs_6_
  24.4 0.0 collective-permute-done.refs_1_
  24.4 0.0 collective-permute-done.1.refs_2_
  24.4 2.8 %all-to-all-done = bf16[128,5,2,128]{3,2,1,0:T(2,128)(2,1)S(1)} async-done(((bf16[128,5,2,128]{3,2,1,0:T(2,128)(2,1)}), bf16[128,5,2,128]{3,2,1,0:T(2,128)(2,1)S(1)}, u32[]{:S(2)}, u32[]{:S(2)}) %all-to-all-start) | async-done | bytes 327712 | tf_op jit(solution)/shard_map/all_to_all | solution.py:653
  27.2 2.2 %shard_map.87 = (bf16[1280,128]{1,0:T(8,128)(2,1)}, bf16[1280,128]{1,0:T(8,128)(2,1)}) custom-call(bf16[1280,128]{1,0:T(8,128)(2,1)S(1)} %bitcast.22, bf16[1,256,256]{2,1,0:T(8,128)(2,1)} %refs_0_.1), custom_call_target="tpu_custom_call" | custom-call | tf_op jit(solution)/shard_map/pallas_call | solution.py:144
  29.4 7.0 %all-to-all-start.1 = ((bf16[128,5,2,128]{3,2,1,0:T(2,128)(2,1)}), bf16[128,5,2,128]{3,2,1,0:T(2,128)(2,1)S(1)}, u32[]{:S(2)}, u32[]{:S(2)}) async-start(bf16[128,5,2,128]{3,2,1,0:T(2,128)(2,1)} %bitcast.26), calls=%async_computation.1 | async-start | bytes 655360 | tf_op jit(solution)/shard_map/all_to_all | solution.py:653
  36.5 0.1 stack.35
  36.6 10.6 %shard_map.88 = (f32[16,32,256]{2,1,0:T(8,128)}, f32[16,32,256]{2,1,0:T(8,128)}, f32[16,32,256]{2,1,0:T(8,128)}, f32[16,32,256]{2,1,0:T(8,128)}, f32[16,32,256]{...) custom-call(f32[6]{0:T(128)S(1)} %stack.36.refs_0_, ...), custom_call_target="tpu_custom_call" | custom-call | tf_op jit(solution)/shard_map/pallas_call | solution.py:144
  47.2 0.6 all-to-all-done.1
  47.8 4.2 %shard_map.89 = (f32[16,32,256]{2,1,0:T(8,128)S(1)}, f32[16,32,256]{2,1,0:T(8,128)}, bf16[32,256]{1,0:T(8,128)(2,1)S(1)}, bf16[32,256]{1,0:T(8,128)(2,1)S(1)}, b...) custom-call(bf16[1280,128]{1,0:T(8,128)(2,1)S(1)} %bitcast.20, ...), custom_call_target="tpu_custom_call" | custom-call | tf_op jit(solution)/shard_map/pallas_call | solution.py:144
  52.0 1.7 %collective-permute-start.8 = (bf16[16,256]{1,0:T(8,128)(2,1)S(1)}, bf16[16,256]{1,0:T(8,128)(2,1)S(1)}, u32[]{:S(2)}, u32[]{:S(2)}) collective-permute-start(bf16[16,256]{1,0:T(8,128)(2,1)S(1)} %get-tuple-element.96), channel_id=1, source_target_pairs={{0,16},{16,32},{32,48},{48,64},{64,80},{80,96},{96,112},{112,0},{1... | collective-permute-start | bytes 24584 | tf_op jit(solution)/shard_map/ppermute | solution.py:223
  53.7 0.7 collective-permute-start.6
  54.5 1.9 %collective-permute-start.7 = (bf16[32,256]{1,0:T(8,128)(2,1)S(1)}, bf16[32,256]{1,0:T(8,128)(2,1)S(1)}, u32[]{:S(2)}, u32[]{:S(2)}) collective-permute-start(bf16[32,256]{1,0:T(8,128)(2,1)S(1)} %get-tuple-element.95), channel_id=1, source_target_pairs={{1,0},{2,1},{3,2},{0,3},{5,4},{6,5},{7,6},{4,7},{9,8},{10,9},{11,1... | collective-permute-start | bytes 49160 | tf_op jit(solution)/shard_map/ppermute | solution.py:224
  56.4 0.2 collective-permute-start.9
  56.6 0.5 collective-permute-start.10
  57.1 0.0 collective-permute-done.8.refs_10_
  57.1 2.2 %collective-permute-start.11 = (bf16[32,128]{1,0:T(8,128)(2,1)S(1)}, bf16[32,128]{1,0:T(8,128)(2,1)S(1)}, u32[]{:S(2)}, u32[]{:S(2)}) collective-permute-start(bf16[32,128]{1,0:T(8,128)(2,1)S(1)} %get-tuple-element.99), channel_id=1, source_target_pairs={{4,0},{8,4},{12,8},{0,12},{5,1},{9,5},{13,9},{1,13},{6,2},{10,6},{... | collective-permute-start | bytes 24584 | tf_op jit(solution)/shard_map/ppermute | solution.py:224
  59.3 0.2 collective-permute-done.9.refs_11_
  59.5 0.8 collective-permute-done.10.refs_12_
  60.3 0.0 collective-permute-done.11.refs_13_
  60.3 0.0 collective-permute-done.6.refs_8_
  60.3 0.0 collective-permute-done.7.refs_9_
  60.4 3.8 %shard_map.90 = (f32[16,32,256]{2,1,0:T(8,128)}, bf16[1280,128]{1,0:T(8,128)(2,1)}) custom-call(f32[16,32,256]{2,1,0:T(8,128)S(1)} %get-tuple-element.86.refs_0_, f32[16,32,256]{2,1,0:T(8,128)S(1)} %get-tuple-element.87.refs_1_, f32[16,32,256]{2,1,0:T(8,128)S(1)} %get-tuple-element.88.refs_2_, f32[16,32,256]{2,1,0:T(8,128)S(1)} %get-tuple-element.89.refs_3_, ...), custom_call_target="tpu_custom_call" | custom-call | tf_op jit(solution)/shard_map/pallas_call | solution.py:144
  64.2 20.6 %all_to_all.31 = bf16[128,5,2,128]{3,2,1,0:T(2,128)(2,1)S(1)} all-to-all(bf16[128,5,2,128]{3,2,1,0:T(2,128)(2,1)} %bitcast.28), channel_id=1, replica_groups=mesh['gx'=8,'gy'=4,'gz'=4] {'gx','gy','gz'}, dimensions={0} | all-to-all | bytes 655360 | tf_op jit(solution)/shard_map/all_to_all | solution.py:653
  84.7 2.3 %shard_map.91 = (bf16[1280,128]{1,0:T(8,128)(2,1)}, f32[8,128]{1,0:T(8,128)}) custom-call(bf16[1,256,256]{2,1,0:T(8,128)(2,1)} %refs_0_.1, bf16[1280,128]{1,0:T(8,128)(2,1)} %get-tuple-element.71.refs_1_, bf16[1280,128]{1,0:T(8,128)(2,1)S(1)} %bitcast.23), custom_call_target="tpu_custom_call" | custom-call | tf_op jit(solution)/shard_map/pallas_call | solution.py:144
  87.1 4.7 %all-to-all-start.3 = ((bf16[128,5,2,128]{3,2,1,0:T(2,128)(2,1)}), bf16[128,5,2,128]{3,2,1,0:T(2,128)(2,1)S(1)}, u32[]{:S(2)}, u32[]{:S(2)}) async-start(bf16[128,5,2,128]{3,2,1,0:T(2,128)(2,1)} %bitcast.29), calls=%async_computation.3 | async-start | bytes 655360 | tf_op jit(solution)/shard_map/all_to_all | solution.py:653
  91.8 8.8 %shard_map.92.refs_4_ = f32[16,32,256]{2,1,0:T(8,128)} custom-call(f32[8,128]{1,0:T(8,128)} %get-tuple-element.101.refs_0_.refs_15_, f32[16,32,256]{2,1,0:T(8,128)} %refs_4_.3, f32[16,32,256]{2,1,0:T(8,128)} %get-tuple-element.103.refs_2_.refs_12_.refs_5_, f32[16,32,256]{2,1,0:T(8,128)} %get-tuple-element.104.refs_3_, ...), custom_call_target="tpu_custom_call" | custom-call | tf_op jit(solution)/shard_map/pallas_call | solution.py:144
  100.6 2.7 %all-to-all-done.3 = bf16[128,5,2,128]{3,2,1,0:T(2,128)(2,1)S(1)} async-done(((bf16[128,5,2,128]{3,2,1,0:T(2,128)(2,1)}), bf16[128,5,2,128]{3,2,1,0:T(2,128)(2,1)S(1)}, u32[]{:S(2)}, u32[]{:S(2)}) %all-to-all-start.3) | async-done | bytes 327712 | tf_op jit(solution)/shard_map/all_to_all | solution.py:653
  103.3 4.4 %shard_map.93 = (f32[16,32,256]{2,1,0:T(8,128)S(1)}, f32[16,32,256]{2,1,0:T(8,128)}, bf16[32,256]{1,0:T(8,128)(2,1)S(1)}, bf16[32,256]{1,0:T(8,128)(2,1)S(1)}, b...) custom-call(bf16[1280,128]{1,0:T(8,128)(2,1)S(1)} %bitcast.21, ...), custom_call_target="tpu_custom_call" | custom-call | tf_op jit(solution)/shard_map/pallas_call | solution.py:144
  107.7 1.7 %collective-permute-start.14 = (bf16[16,256]{1,0:T(8,128)(2,1)S(1)}, bf16[16,256]{1,0:T(8,128)(2,1)S(1)}, u32[]{:S(2)}, u32[]{:S(2)}) collective-permute-start(bf16[16,256]{1,0:T(8,128)(2,1)S(1)} %get-tuple-element.116), channel_id=1, source_target_pairs={{0,16},{16,32},{32,48},{48,64},{64,80},{80,96},{96,112},{112,0},{1... | collective-permute-start | bytes 24584 | tf_op jit(solution)/shard_map/ppermute | solution.py:223
  109.4 0.4 collective-permute-start.12
  109.8 2.3 %collective-permute-start.13 = (bf16[32,256]{1,0:T(8,128)(2,1)S(1)}, bf16[32,256]{1,0:T(8,128)(2,1)S(1)}, u32[]{:S(2)}, u32[]{:S(2)}) collective-permute-start(bf16[32,256]{1,0:T(8,128)(2,1)S(1)} %get-tuple-element.115), channel_id=1, source_target_pairs={{1,0},{2,1},{3,2},{0,3},{5,4},{6,5},{7,6},{4,7},{9,8},{10,9},{11,1... | collective-permute-start | bytes 49160 | tf_op jit(solution)/shard_map/ppermute | solution.py:224
  112.1 0.2 collective-permute-start.15
  112.3 0.3 collective-permute-start.16
  112.6 0.0 collective-permute-done.14.refs_11_
  112.6 2.4 %collective-permute-start.17 = (bf16[32,128]{1,0:T(8,128)(2,1)S(1)}, bf16[32,128]{1,0:T(8,128)(2,1)S(1)}, u32[]{:S(2)}, u32[]{:S(2)}) collective-permute-start(bf16[32,128]{1,0:T(8,128)(2,1)S(1)} %get-tuple-element.119), channel_id=1, source_target_pairs={{4,0},{8,4},{12,8},{0,12},{5,1},{9,5},{13,9},{1,13},{6,2},{10,6},{... | collective-permute-start | bytes 24584 | tf_op jit(solution)/shard_map/ppermute | solution.py:224
  115.0 0.2 collective-permute-done.15.refs_12_
  115.1 0.8 collective-permute-done.16.refs_13_
  116.0 0.0 collective-permute-done.17.refs_14_
  116.0 0.0 collective-permute-done.12.refs_9_
  116.0 0.0 collective-permute-done.13.refs_10_
  116.0 2.1 %shard_map.94 = (f32[16,32,256]{2,1,0:T(8,128)}, f32[128,128]{1,0:T(8,128)S(1)}) custom-call(f32[16,32,256]{2,1,0:T(8,128)S(1)} %get-tuple-element.105.refs_0_, f32[16,32,256]{2,1,0:T(8,128)S(1)} %get-tuple-element.106.refs_1_, f32[16,32,256]{2,1,0:T(8,128)S(1)} %get-tuple-element.107.refs_2_, f32[16,32,256]{2,1,0:T(8,128)S(1)} %get-tuple-element.108.refs_3_, ...), custom_call_target="tpu_custom_call" | custom-call | tf_op jit(solution)/shard_map/pallas_call | solution.py:144
  118.1 16.9 %all_to_all.32 = f32[128,1,128]{2,1,0:T(1,128)S(1)} all-to-all(f32[128,1,128]{2,1,0:T(1,128)S(1)} %bitcast.25), channel_id=1, replica_groups=mesh['gx'=8,'gy'=4,'gz'=4] {'gx','gy','gz'}, dimensions={0} | all-to-all | bytes 131072 | tf_op jit(solution)/shard_map/all_to_all | solution.py:653
  135.0 2.9 %shard_map.95 = (f32[16,32,256]{2,1,0:T(8,128)}, f32[16,32,256]{2,1,0:T(8,128)}) custom-call(f32[8,128]{1,0:T(8,128)} %get-tuple-element.101.refs_0_.refs_15_, f32[128,128]{1,0:T(8,128)S(1)} %bitcast.24, f32[16,32,256]{2,1,0:T(8,128)} %get-tuple-element.121.refs_2_, f32[16,32,256]{2,1,0:T(8,128)} %get-tuple-element.122.refs_3_, f32[16,32,256]{2,1,0:T(8,128)} %refs_4_.3, ...), custom_call_target="tpu_custom_call" | custom-call | tf_op jit(solution)/shard_map/pallas_call | solution.py:144
  (4 shorter events, 0.0 us)
Async XLA Ops:
  4.2 11.6 %copy-start.5 = (bf16[16,256]{1,0:T(8,128)(2,1)S(1)}, bf16[16,256]{1,0:T(8,128)(2,1)}, u32[]{:S(2)}) copy-start(bf16[16,256]{1,0:T(8,128)(2,1)} %get-tuple-element.66) | copy-start | bytes 24580
  4.2 13.3 %copy-start.1 = (bf16[32,256]{1,0:T(8,128)(2,1)S(1)}, bf16[32,256]{1,0:T(8,128)(2,1)}, u32[]{:S(2)}) copy-start(bf16[32,256]{1,0:T(8,128)(2,1)} %get-tuple-element.64) | copy-start | bytes 49156
  4.3 14.6 %copy-start = (bf16[32,256]{1,0:T(8,128)(2,1)S(1)}, bf16[32,256]{1,0:T(8,128)(2,1)}, u32[]{:S(2)}) copy-start(bf16[32,256]{1,0:T(8,128)(2,1)} %get-tuple-element.65) | copy-start | bytes 49156
  4.3 16.0 %copy-start.4 = (bf16[16,256]{1,0:T(8,128)(2,1)S(1)}, bf16[16,256]{1,0:T(8,128)(2,1)}, u32[]{:S(2)}) copy-start(bf16[16,256]{1,0:T(8,128)(2,1)} %get-tuple-element.67) | copy-start | bytes 24580
  4.3 16.0 %copy-start.3 = (bf16[32,128]{1,0:T(8,128)(2,1)S(1)}, bf16[32,128]{1,0:T(8,128)(2,1)}, u32[]{:S(2)}) copy-start(bf16[32,128]{1,0:T(8,128)(2,1)} %get-tuple-element.68) | copy-start | bytes 24580
  4.3 22.9 %all-to-all-start = ((bf16[128,5,2,128]{3,2,1,0:T(2,128)(2,1)}), bf16[128,5,2,128]{3,2,1,0:T(2,128)(2,1)S(1)}, u32[]{:S(2)}, u32[]{:S(2)}) async-start(bf16[128,5,2,128]{3,2,1,0:T(2,128)(2,1)} %bitcast.27), calls=%async_computation | async-start | bytes 655360 | tf_op jit(solution)/shard_map/all_to_all | solution.py:653
  15.8 5.8 %copy-start.2 = (bf16[32,128]{1,0:T(8,128)(2,1)S(1)}, bf16[32,128]{1,0:T(8,128)(2,1)}, u32[]{:S(2)}) copy-start(bf16[32,128]{1,0:T(8,128)(2,1)} %get-tuple-element.69) | copy-start | bytes 24580
  15.8 5.7 %collective-permute-start.2 = (bf16[16,256]{1,0:T(8,128)(2,1)S(1)}, bf16[16,256]{1,0:T(8,128)(2,1)S(1)}, u32[]{:S(2)}, u32[]{:S(2)}) collective-permute-start(bf16[16,256]{1,0:T(8,128)(2,1)S(1)} %copy-done.5), channel_id=1, source_target_pairs={{0,16},{16,32},{32,48},{48,64},{64,80},{80,96},{96,112},{112,0},{1... | collective-permute-start | bytes 24584 | tf_op jit(solution)/shard_map/ppermute | solution.py:223
  17.6 6.8 %collective-permute-start = (bf16[32,256]{1,0:T(8,128)(2,1)S(1)}, bf16[32,256]{1,0:T(8,128)(2,1)S(1)}, u32[]{:S(2)}, u32[]{:S(2)}) collective-permute-start(bf16[32,256]{1,0:T(8,128)(2,1)S(1)} %copy-done.1), channel_id=1, source_target_pairs={{0,1},{1,2},{2,3},{3,0},{4,5},{5,6},{6,7},{7,4},{8,9},{9,10},{10,1... | collective-permute-start | bytes 49160 | tf_op jit(solution)/shard_map/ppermute | solution.py:223
  18.8 5.5 %collective-permute-start.1 = (bf16[32,256]{1,0:T(8,128)(2,1)S(1)}, bf16[32,256]{1,0:T(8,128)(2,1)S(1)}, u32[]{:S(2)}, u32[]{:S(2)}) collective-permute-start(bf16[32,256]{1,0:T(8,128)(2,1)S(1)} %copy-done), channel_id=1, source_target_pairs={{1,0},{2,1},{3,2},{0,3},{5,4},{6,5},{7,6},{4,7},{9,8},{10,9},{11,1... | collective-permute-start | bytes 49160 | tf_op jit(solution)/shard_map/ppermute | solution.py:224
  20.3 3.4 %collective-permute-start.3 = (bf16[16,256]{1,0:T(8,128)(2,1)S(1)}, bf16[16,256]{1,0:T(8,128)(2,1)S(1)}, u32[]{:S(2)}, u32[]{:S(2)}) collective-permute-start(bf16[16,256]{1,0:T(8,128)(2,1)S(1)} %copy-done.4), channel_id=1, source_target_pairs={{16,0},{32,16},{48,32},{64,48},{80,64},{96,80},{112,96},{0,112},{1... | collective-permute-start | bytes 24584 | tf_op jit(solution)/shard_map/ppermute | solution.py:224
  20.3 4.1 %collective-permute-start.4 = (bf16[32,128]{1,0:T(8,128)(2,1)S(1)}, bf16[32,128]{1,0:T(8,128)(2,1)S(1)}, u32[]{:S(2)}, u32[]{:S(2)}) collective-permute-start(bf16[32,128]{1,0:T(8,128)(2,1)S(1)} %copy-done.3), channel_id=1, source_target_pairs={{0,4},{4,8},{8,12},{12,0},{1,5},{5,9},{9,13},{13,1},{2,6},{6,10},{... | collective-permute-start | bytes 24584 | tf_op jit(solution)/shard_map/ppermute | solution.py:223
  21.6 2.8 %collective-permute-start.5 = (bf16[32,128]{1,0:T(8,128)(2,1)S(1)}, bf16[32,128]{1,0:T(8,128)(2,1)S(1)}, u32[]{:S(2)}, u32[]{:S(2)}) collective-permute-start(bf16[32,128]{1,0:T(8,128)(2,1)S(1)} %copy-done.2), channel_id=1, source_target_pairs={{4,0},{8,4},{12,8},{0,12},{5,1},{9,5},{13,9},{1,13},{6,2},{10,6},{... | collective-permute-start | bytes 24584 | tf_op jit(solution)/shard_map/ppermute | solution.py:224
  29.4 18.4 %all-to-all-start.1 = ((bf16[128,5,2,128]{3,2,1,0:T(2,128)(2,1)}), bf16[128,5,2,128]{3,2,1,0:T(2,128)(2,1)S(1)}, u32[]{:S(2)}, u32[]{:S(2)}) async-start(bf16[128,5,2,128]{3,2,1,0:T(2,128)(2,1)} %bitcast.26), calls=%async_computation.1 | async-start | bytes 655360 | tf_op jit(solution)/shard_map/all_to_all | solution.py:653
  52.0 5.1 %collective-permute-start.8 = (bf16[16,256]{1,0:T(8,128)(2,1)S(1)}, bf16[16,256]{1,0:T(8,128)(2,1)S(1)}, u32[]{:S(2)}, u32[]{:S(2)}) collective-permute-start(bf16[16,256]{1,0:T(8,128)(2,1)S(1)} %get-tuple-element.96), channel_id=1, source_target_pairs={{0,16},{16,32},{32,48},{48,64},{64,80},{80,96},{96,112},{112,0},{1... | collective-permute-start | bytes 24584 | tf_op jit(solution)/shard_map/ppermute | solution.py:223
  53.7 6.6 %collective-permute-start.6 = (bf16[32,256]{1,0:T(8,128)(2,1)S(1)}, bf16[32,256]{1,0:T(8,128)(2,1)S(1)}, u32[]{:S(2)}, u32[]{:S(2)}) collective-permute-start(bf16[32,256]{1,0:T(8,128)(2,1)S(1)} %get-tuple-element.94), channel_id=1, source_target_pairs={{0,1},{1,2},{2,3},{3,0},{4,5},{5,6},{6,7},{7,4},{8,9},{9,10},{10,1... | collective-permute-start | bytes 49160 | tf_op jit(solution)/shard_map/ppermute | solution.py:223
  54.5 5.9 %collective-permute-start.7 = (bf16[32,256]{1,0:T(8,128)(2,1)S(1)}, bf16[32,256]{1,0:T(8,128)(2,1)S(1)}, u32[]{:S(2)}, u32[]{:S(2)}) collective-permute-start(bf16[32,256]{1,0:T(8,128)(2,1)S(1)} %get-tuple-element.95), channel_id=1, source_target_pairs={{1,0},{2,1},{3,2},{0,3},{5,4},{6,5},{7,6},{4,7},{9,8},{10,9},{11,1... | collective-permute-start | bytes 49160 | tf_op jit(solution)/shard_map/ppermute | solution.py:224
  56.4 3.1 %collective-permute-start.9 = (bf16[16,256]{1,0:T(8,128)(2,1)S(1)}, bf16[16,256]{1,0:T(8,128)(2,1)S(1)}, u32[]{:S(2)}, u32[]{:S(2)}) collective-permute-start(bf16[16,256]{1,0:T(8,128)(2,1)S(1)} %get-tuple-element.97), channel_id=1, source_target_pairs={{16,0},{32,16},{48,32},{64,48},{80,64},{96,80},{112,96},{0,112},{1... | collective-permute-start | bytes 24584 | tf_op jit(solution)/shard_map/ppermute | solution.py:224
  56.6 3.7 %collective-permute-start.10 = (bf16[32,128]{1,0:T(8,128)(2,1)S(1)}, bf16[32,128]{1,0:T(8,128)(2,1)S(1)}, u32[]{:S(2)}, u32[]{:S(2)}) collective-permute-start(bf16[32,128]{1,0:T(8,128)(2,1)S(1)} %get-tuple-element.98), channel_id=1, source_target_pairs={{0,4},{4,8},{8,12},{12,0},{1,5},{5,9},{9,13},{13,1},{2,6},{6,10},{... | collective-permute-start | bytes 24584 | tf_op jit(solution)/shard_map/ppermute | solution.py:223
  57.1 3.2 %collective-permute-start.11 = (bf16[32,128]{1,0:T(8,128)(2,1)S(1)}, bf16[32,128]{1,0:T(8,128)(2,1)S(1)}, u32[]{:S(2)}, u32[]{:S(2)}) collective-permute-start(bf16[32,128]{1,0:T(8,128)(2,1)S(1)} %get-tuple-element.99), channel_id=1, source_target_pairs={{4,0},{8,4},{12,8},{0,12},{5,1},{9,5},{13,9},{1,13},{6,2},{10,6},{... | collective-permute-start | bytes 24584 | tf_op jit(solution)/shard_map/ppermute | solution.py:224
  87.1 16.2 %all-to-all-start.3 = ((bf16[128,5,2,128]{3,2,1,0:T(2,128)(2,1)}), bf16[128,5,2,128]{3,2,1,0:T(2,128)(2,1)S(1)}, u32[]{:S(2)}, u32[]{:S(2)}) async-start(bf16[128,5,2,128]{3,2,1,0:T(2,128)(2,1)} %bitcast.29), calls=%async_computation.3 | async-start | bytes 655360 | tf_op jit(solution)/shard_map/all_to_all | solution.py:653
  107.7 4.9 %collective-permute-start.14 = (bf16[16,256]{1,0:T(8,128)(2,1)S(1)}, bf16[16,256]{1,0:T(8,128)(2,1)S(1)}, u32[]{:S(2)}, u32[]{:S(2)}) collective-permute-start(bf16[16,256]{1,0:T(8,128)(2,1)S(1)} %get-tuple-element.116), channel_id=1, source_target_pairs={{0,16},{16,32},{32,48},{48,64},{64,80},{80,96},{96,112},{112,0},{1... | collective-permute-start | bytes 24584 | tf_op jit(solution)/shard_map/ppermute | solution.py:223
  109.4 6.6 %collective-permute-start.12 = (bf16[32,256]{1,0:T(8,128)(2,1)S(1)}, bf16[32,256]{1,0:T(8,128)(2,1)S(1)}, u32[]{:S(2)}, u32[]{:S(2)}) collective-permute-start(bf16[32,256]{1,0:T(8,128)(2,1)S(1)} %get-tuple-element.114), channel_id=1, source_target_pairs={{0,1},{1,2},{2,3},{3,0},{4,5},{5,6},{6,7},{7,4},{8,9},{9,10},{10,1... | collective-permute-start | bytes 49160 | tf_op jit(solution)/shard_map/ppermute | solution.py:223
  109.8 6.2 %collective-permute-start.13 = (bf16[32,256]{1,0:T(8,128)(2,1)S(1)}, bf16[32,256]{1,0:T(8,128)(2,1)S(1)}, u32[]{:S(2)}, u32[]{:S(2)}) collective-permute-start(bf16[32,256]{1,0:T(8,128)(2,1)S(1)} %get-tuple-element.115), channel_id=1, source_target_pairs={{1,0},{2,1},{3,2},{0,3},{5,4},{6,5},{7,6},{4,7},{9,8},{10,9},{11,1... | collective-permute-start | bytes 49160 | tf_op jit(solution)/shard_map/ppermute | solution.py:224
  112.1 3.1 %collective-permute-start.15 = (bf16[16,256]{1,0:T(8,128)(2,1)S(1)}, bf16[16,256]{1,0:T(8,128)(2,1)S(1)}, u32[]{:S(2)}, u32[]{:S(2)}) collective-permute-start(bf16[16,256]{1,0:T(8,128)(2,1)S(1)} %get-tuple-element.117), channel_id=1, source_target_pairs={{16,0},{32,16},{48,32},{64,48},{80,64},{96,80},{112,96},{0,112},{1... | collective-permute-start | bytes 24584 | tf_op jit(solution)/shard_map/ppermute | solution.py:224
  112.3 3.7 %collective-permute-start.16 = (bf16[32,128]{1,0:T(8,128)(2,1)S(1)}, bf16[32,128]{1,0:T(8,128)(2,1)S(1)}, u32[]{:S(2)}, u32[]{:S(2)}) collective-permute-start(bf16[32,128]{1,0:T(8,128)(2,1)S(1)} %get-tuple-element.118), channel_id=1, source_target_pairs={{0,4},{4,8},{8,12},{12,0},{1,5},{5,9},{9,13},{13,1},{2,6},{6,10},{... | collective-permute-start | bytes 24584 | tf_op jit(solution)/shard_map/ppermute | solution.py:223
  112.6 3.4 %collective-permute-start.17 = (bf16[32,128]{1,0:T(8,128)(2,1)S(1)}, bf16[32,128]{1,0:T(8,128)(2,1)S(1)}, u32[]{:S(2)}, u32[]{:S(2)}) collective-permute-start(bf16[32,128]{1,0:T(8,128)(2,1)S(1)} %get-tuple-element.119), channel_id=1, source_target_pairs={{4,0},{8,4},{12,8},{0,12},{5,1},{9,5},{13,9},{1,13},{6,2},{10,6},{... | collective-permute-start | bytes 24584 | tf_op jit(solution)/shard_map/ppermute | solution.py:224

commit v3 on v2

--- a/solution.py
+++ b/solution.py
@@ -16,6 +16,7 @@
 EXTRA = 2 * CAP
 PARTS = EXTRA + 2
 LANES = 128
+LINES = CZ * CX
 AX = ("gx", "gy", "gz")
 F32 = jnp.float32
 BF16 = jnp.bfloat16
@@ -89,13 +90,17 @@
 CHUNKS = 4
 
 
+def chunks_of(mode, array):
+    return CHUNKS if mode in "cp" and array.shape[0] > 8 else 1
+
+
 def spec(mode):
     return pl.BlockSpec(memory_space=SPACE[mode])
 
 
 def run(body, ins, outs, scratch=(), mixed=()):
     moved = [(m, a) for side in (ins, outs) for m, a in side if m in COPIED]
-    n_chunks = [1 if m in "ha" else CHUNKS for m, _ in moved]
+    n_chunks = [chunks_of(m, a) for m, a in moved]
     buffers = [pltpu.VMEM(a.shape, a.dtype) for m, a in moved if m != "p"]
     sems = [pltpu.SemaphoreType.DMA((n,)) for n in n_chunks]
     passed = [sds(a.shape, a.dtype) for m, a in ins if m == "p"]
@@ -115,13 +120,13 @@
         for (m, _), ref in zip(ins, in_refs):
             if m in COPIED:
                 buf = pass_refs.pop(0) if m == "p" else bufs.pop(0)
-                given.append(Load(ref, buf, refs.pop(0), 1 if m in "ha" else CHUNKS))
+                given.append(Load(ref, buf, refs.pop(0), chunks_of(m, buf)))
                 loads.append(given[-1])
             else:
                 given.append(ref)
         for (m, _), ref in zip(outs, out_refs):
             if m in COPIED:
-                made.append(Store(ref, bufs.pop(0), refs.pop(0), 1 if m in "ha" else CHUNKS))
+                made.append(Store(ref, bufs[0], refs.pop(0), chunks_of(m, bufs.pop(0))))
                 stores.append(made[-1])
             else:
                 made.append(ref)
@@ -182,25 +187,46 @@
     return high, mid, rest - mid
 
 
-def face_store(plane_of, refs, xs_lo, xs_hi):
-    zlo, zhi, xlo, xhi, ylo, yhi = (raw(x) for x in refs)
-    lane = iota((CX, LANES), 1)
-    acc_lo = jnp.zeros((CX, LANES), F32)
-    acc_hi = jnp.zeros((CX, LANES), F32)
+def choose(even, first, second):
+    return even * first + (1.0 - even) * second
+
+
+def edge_rows(flat):
+    shape = (8, CY)
+    sub, lane = iota(shape, 0), iota(shape, 1)
+    hit = ((sub == 0) & (lane == 0)) | ((sub == 1) & (lane == CY - 1))
+    pick = jnp.where(hit, 1.0, 0.0).astype(BF16)
+    return lax.dot_general(pick, flat, (((1,), (1,)), ((), ())), preferred_element_type=F32)
+
+
+def edge_field(rows):
+    high, mid, low = split3(rows)
+    sub = iota(rows.shape, 0)
+    stack = jnp.where(
+        sub < 2, high, jnp.where(sub < 4, pltpu.roll(mid, 2, 0), pltpu.roll(low, 4, 0))
+    )
+    shape = (8, CY)
+    sub, lane = iota(shape, 0), iota(shape, 1)
+    hit = ((sub % 2 == 0) & (lane == 0)) | ((sub % 2 == 1) & (lane == CY - 1))
+    put = jnp.where(hit & (sub < 6), 1.0, 0.0).astype(BF16)
+    stack = jnp.where(iota(rows.shape, 0) < 6, stack, 0.0)
+    return jnp.dot(stack.T.astype(BF16), put, preferred_element_type=F32)
+
+
+def face_store(plane_of, flags, refs, xs_lo, xs_hi):
+    za, zb, xa, xb, ys = (raw(x) for x in refs)
+    low, high = plane_of(0), plane_of(CZ - 1)
+    za[...] = choose(flags[6], high, low).astype(BF16)
+    zb[...] = choose(flags[6], low, high).astype(BF16)
+    planes = []
     for z in range(CZ):
         plane = plane_of(z)
-        if z == 0:
-            zlo[...] = plane.astype(BF16)
-        if z == CZ - 1:
-            zhi[...] = plane.astype(BF16)
         xs_lo[z : z + 1, :] = plane[0:1, :]
         xs_hi[z : z + 1, :] = plane[CX - 1 : CX, :]
-        acc_lo = jnp.where(lane == z, plane[:, 0:1], acc_lo)
-        acc_hi = jnp.where(lane == z, plane[:, CY - 1 : CY], acc_hi)
-    xlo[...] = xs_lo[...].astype(BF16)
-    xhi[...] = xs_hi[...].astype(BF16)
-    ylo[...] = acc_lo.astype(BF16)
-    yhi[...] = acc_hi.astype(BF16)
+        planes.append(plane.astype(BF16))
+    xa[...] = choose(flags[7], xs_hi[...], xs_lo[...]).astype(BF16)
+    xb[...] = choose(flags[7], xs_lo[...], xs_hi[...]).astype(BF16)
+    ys[...] = edge_rows(jnp.concatenate(planes, axis=0)).astype(BF16)
 
 
 FACE_OUTS = (
@@ -208,21 +234,40 @@
     sds((CX, CY), BF16),
     sds((CZ, CY), BF16),
     sds((CZ, CY), BF16),
-    sds((CX, LANES), BF16),
-    sds((CX, LANES), BF16),
+    sds((8, LINES), BF16),
 )
 FACE_SCRATCH = (pltpu.VMEM((CZ, CY), F32), pltpu.VMEM((CZ, CY), F32))
 
 
 def exchange(faces):
+    za, zb, xa, xb, ys = faces
     out = []
-    for axis, (low, high) in zip(("gz", "gx", "gy"), (faces[0:2], faces[2:4], faces[4:6])):
+    for axis, first, second in (("gz", za, zb), ("gx", xa, xb), ("gy", ys, ys)):
         n = lax.axis_size(axis)
-        forward = [(i, (i + 1) % n) for i in range(n)]
-        backward = [((i + 1) % n, i) for i in range(n)]
-        out.append(lax.ppermute(high, axis, forward))
-        out.append(lax.ppermute(low, axis, backward))
+        out.append(lax.ppermute(first, axis, [(i, i ^ 1) for i in range(n)]))
+        out.append(
+            lax.ppermute(second, axis, [(i, (i + 1 if i % 2 else i - 1) % n) for i in range(n)])
+        )
     return out
+
+
+def halo_values(flags, got):
+    za, zb, xa, xb, ya, yb = (full(x)[...].astype(F32) for x in got)
+    low, high = choose(flags[8], yb, ya), choose(flags[8], ya, yb)
+    shape = (8, LINES)
+    sub = iota(shape, 0)
+    rows = jnp.where(
+        sub == 0,
+        jnp.broadcast_to(low[1:2, :], shape),
+        jnp.where(sub == 1, jnp.broadcast_to(high[0:1, :], shape), 0.0),
+    )
+    return (
+        choose(flags[6], zb, za),
+        choose(flags[6], za, zb),
+        choose(flags[7], xb, xa),
+        choose(flags[7], xa, xb),
+        rows,
+    )
 
 
 def slots(zrow):
@@ -240,9 +285,14 @@
     return pl.ds(first * PARTS + part, count, stride=PARTS)
 
 
-def store_send(send, blocks, zrow, u_rows, scalars, tile, wide):
-    key, _ = slots(zrow)
-    put = jnp.where(iota((CAP * ZN, ZN), 0) == key, 1.0, 0.0).astype(BF16)
+def zone_hits(zrow):
+    row, col = slots(zrow)
+    put = jnp.where(iota((CAP * ZN, ZN), 0) == row, 1.0, 0.0).astype(BF16)
+    take = jnp.where(iota((ZN, CAP * ZN), 1) == col, 1.0, 0.0).astype(BF16)
+    return put, take
+
+
+def store_send(send, blocks, put, u_rows, scalars, tile, wide):
     placed = jnp.dot(put, blocks, preferred_element_type=F32)
     for k in range(CAP):
         rows = placed[k * ZN : (k + 1) * ZN, :]
@@ -261,19 +311,23 @@
     send[...] = wide[...].astype(BF16)
 
 
-def label_columns(label, tile):
+def label_hits(label, tile, hits):
     tile[...] = jnp.zeros((LANES, LANES), F32)
     tile[0:CZ, 0:CX] = full(label)[...].astype(F32)
-    return tile[...].T[0:CX, :]
-
-
-def coarse_rows(line_of, columns, factor, rows):
+    columns = tile[...].T[0:CX, :]
     lane = iota((CX, LANES), 1)
-    kind = lane.astype(F32)
+    kind = jnp.where(lane < 3 * KC, lane % KC, -1).astype(F32)
+    for z in range(CZ):
+        hit = jnp.where(columns[:, z : z + 1] == kind, 1.0, 0.0)
+        hits[z * CX : (z + 1) * CX, :] = hit.astype(BF16)
+
+
+def coarse_rows(line_of, hits, factor, rows):
+    lane = iota((CX, LANES), 1)
     sub = iota((CX, LANES), 0)
     acc = jnp.zeros((CX, LANES), F32)
     for z in range(CZ):
-        acc = acc + jnp.where(columns[:, z : z + 1] == kind, line_of(z), 0.0)
+        acc = acc + hits[z * CX : (z + 1) * CX, :].astype(F32) * line_of(z)
     g_row = jnp.broadcast_to(jnp.sum(acc, axis=0, keepdims=True), (CX, LANES))
     g_col = jnp.sum(jnp.where(sub == lane, g_row, 0.0), axis=1, keepdims=True)
     g = jnp.broadcast_to(g_col, (KC, LANES))
@@ -290,15 +344,18 @@
 
 
 def pack_body(ins, outs, tile, rows, wide, xs_lo, xs_hi):
-    label, zrow, r, factor, k = ins
-    send, *faces = outs
-    columns = label_columns(label, tile)
+    flags, label, zrow, r, factor, k = ins
+    send, hits, put, take, *faces = outs
+    label_hits(label, tile, raw(hits))
+    raw(put)[...], raw(take)[...] = zone_hits(full(zrow)[...])
+    for x in (hits, put, take):
+        x.send()
     u_rows = coarse_rows(
-        lambda z: jnp.sum(r[z], axis=1, keepdims=True), columns, factor, rows
-    )
-    store_send(raw(send), face_blocks(r), full(zrow)[...], u_rows, (), tile, wide)
+        lambda z: jnp.sum(r[z], axis=1, keepdims=True), raw(hits), factor, rows
+    )
+    store_send(raw(send), face_blocks(r), raw(put)[...], u_rows, (), tile, wide)
     send.send()
-    face_store(lambda z: k[z], faces, xs_lo, xs_hi)
+    face_store(lambda z: k[z], flags, faces, xs_lo, xs_hi)
 
 
 def lift_store(out, wide, tail, zone):
@@ -383,106 +440,98 @@
     return out
 
 
-def apply_scaled(p_of, cz, cx, cy, e):
-    acc = jnp.zeros((8, LANES), F32)
-    below, now = None, p_of(0)
-    for z in range(CZ):
-        above = p_of(z + 1) if z + 1 < CZ else None
-        image = minus_neighbours(
-            now,
-            below,
-            above,
-            cz[z - 1] if z else None,
-            cz[z] if z + 1 < CZ else None,
-            cx[z],
-            cy[z],
-        )
-        e[z] = image
-        acc = acc + fold(now * image)
-        below, now = now, above
-    return total(acc)
-
-
-def cg(cz, cx, cy, s, p, q, e, y, rho, local):
-    def first_of(z):
-        p[z] = q[z]
-        return q[z]
-
-    a = rho / apply_scaled(first_of, cz, cx, cy, e)
-
-    def move(a, started):
-        acc = jnp.zeros((8, LANES), F32)
+def cg(cz, cx, cy, s, p, q, e, y, first, local):
+    def sweep(next_of, cz, cx, cy):
+        rho = jnp.zeros((8, LANES), F32)
+        pe, ee = rho, rho
+        below, (now, left) = None, next_of(0)
         for z in range(CZ):
-            y[z] = y[z] + a * p[z] if started else a * p[z]
+            rho = rho + fold(left * left)
+            above = None
+            if z + 1 < CZ:
+                above, left = next_of(z + 1)
+            image = minus_neighbours(
+                now,
+                below,
+                above,
+                cz[z - 1] if z else None,
+                cz[z] if z + 1 < CZ else None,
+                cx[z],
+                cy[z],
+            )
+            e[z] = image
+            pe = pe + fold(now * image)
+            ee = ee + fold(image * image)
+            below, now = now, above
+        rho, pe, ee = total(rho), total(pe), total(ee)
+        a = rho / pe
+        return a, a * a * ee / rho - 1.0
+
+    def begin(z):
+        value = first(z)
+        q[z] = value
+        p[z] = value
+        return value, value
+
+    def second(a, beta):
+        def next_of(z):
+            old = p[z]
+            y[z] = a * old
             left = q[z] - a * e[z]
             q[z] = left
-            acc = acc + fold(left * left)
-        return total(acc)
-
-    new = move(a, False)
-    carry = (new, new / rho)
-    cz, cx, cy = raw(cz), raw(cx), raw(cy)
-
-    def advance(beta):
+            new = left + beta * old
+            p[z] = new
+            return new, left
+
+        return next_of
+
+    def later(a, beta):
         def next_of(z):
-            value = q[z] + beta * p[z]
-            p[z] = value
-            return value
-
-        return apply_scaled(next_of, cz, cx, cy, e)
-
-    def step(_, carry):
-        rho, beta = carry
-        new = move(rho / advance(beta), True)
-        return new, new / rho
-
-    rho, beta = lax.fori_loop(0, INNER - 2, step, carry)
-    a = rho / advance(beta)
+            old = p[z]
+            y[z] = y[z] + a * old
+            left = q[z] - a * e[z]
+            q[z] = left
+            new = left + beta * old
+            p[z] = new
+            return new, left
+
+        return next_of
+
+    carry = sweep(begin, cz, cx, cy)
+    cz, cx, cy = full(cz), full(cx), full(cy)
+    carry = sweep(second(*carry), cz, cx, cy)
+    carry = lax.fori_loop(0, INNER - 2, lambda _, c: sweep(later(*c), cz, cx, cy), carry)
+    a = carry[0]
     for z in range(CZ):
         local[z] = s[z] * (y[z] + a * p[z])
 
 
-def start_cg(r_of, s, q):
-    acc = jnp.zeros((8, LANES), F32)
-    for z in range(CZ):
-        left = s[z] * r_of(z)
-        q[z] = left
-        acc = acc + fold(left * left)
-    return total(acc)
-
-
-def solve0_body(ins, outs, p, q, e, y):
+def solve0_body(ins, outs, p, q, e, y, ky):
     flags, *halos, k, storage, r = ins
     local, s, sinv, cz, cx, cy, bounds_zx, bounds_y = outs
-    kzl, kzh, kxl, kxh, kyl, kyh = (full(h) for h in halos)
+    sub, lane = iota((CX, CY), 0), iota((CX, CY), 1)
+    zl, zh, xl, xh, y_rows = halo_values(flags, halos)
+    zl, zh, xl, xh = flags[0] * zl, flags[1] * zh, flags[2] * xl, flags[3] * xh
+    y_flags = jnp.where(iota((8, LINES), 0) == 0, flags[4], flags[5])
+    y_rows = y_flags * y_rows
+    ky[...] = edge_field(y_rows)
     zx, by = raw(bounds_zx), raw(bounds_y)
-    sub, lane = iota((CX, CY), 0), iota((CX, CY), 1)
-    zl, zh = flags[0] * kzl[...].astype(F32), flags[1] * kzh[...].astype(F32)
-    xl, xh = flags[2] * kxl[...].astype(F32), flags[3] * kxh[...].astype(F32)
-    yl, yh = flags[4] * kyl[...].astype(F32), flags[5] * kyh[...].astype(F32)
     zx[0:32, :] = flags[0] * 0.5 * (k[0] + zl)
-    zx[32:64, :] = flags[1] * 0.5 * (k[CZ - 1] + zh)
-    lane_half = iota((CX, LANES), 1)
-    y_edge_lo = jnp.zeros((CX, LANES), F32)
-    y_edge_hi = jnp.zeros((CX, LANES), F32)
+    planes = []
     for z in range(CZ):
         c = k[z]
+        planes.append(c.astype(BF16))
         x_row_lo, x_row_hi = xl[z : z + 1, :], xh[z : z + 1, :]
         zx[64 + z : 65 + z, :] = flags[2] * 0.5 * (c[0:1, :] + x_row_lo)
         zx[80 + z : 81 + z, :] = flags[3] * 0.5 * (c[CX - 1 : CX, :] + x_row_hi)
-        y_edge_lo = jnp.where(lane_half == z, c[:, 0:1], y_edge_lo)
-        y_edge_hi = jnp.where(lane_half == z, c[:, CY - 1 : CY], y_edge_hi)
         around = (k[z - 1] if z else zl) + (k[z + 1] if z + 1 < CZ else zh)
         right = pltpu.roll(c, CX - 1, 0)
         around = around + jnp.where(sub == CX - 1, x_row_hi, right)
         around = around + jnp.where(sub == 0, x_row_lo, pltpu.roll(c, 1, 0))
         ahead = pltpu.roll(c, CY - 1, 1)
-        end = pltpu.roll(yh, LANES - 1 - z, 1)
-        around = around + jnp.where(lane == CY - 1, jnp.concatenate([end, end], axis=1), ahead)
-        begin = pltpu.roll(yl, (LANES - z) % LANES, 1)
-        around = around + jnp.where(
-            lane == 0, jnp.concatenate([begin, begin], axis=1), pltpu.roll(c, 1, 1)
-        )
+        beyond = ky[z * CX : (z + 1) * CX, :]
+        around = around + jnp.where(lane == CY - 1, beyond, ahead)
+        around = around + jnp.where(lane == 0, beyond, pltpu.roll(c, 1, 1))
         diagonal = storage[z] + 3.0 * c + 0.5 * around
         root = lax.rsqrt(diagonal)
         root = root * (1.5 - 0.5 * diagonal * root * root)
@@ -493,29 +542,24 @@
         if z:
             cz[z - 1] = 0.5 * (k[z - 1] + c) * s[z - 1] * root
     cz[CZ - 1] = jnp.zeros((CX, CY), F32)
-    by[0:32, :] = flags[4] * 0.5 * (y_edge_lo + yl)
-    by[32:64, :] = flags[5] * 0.5 * (y_edge_hi + yh)
+    zx[32:64, :] = flags[1] * 0.5 * (k[CZ - 1] + zh)
+    by[...] = y_flags * 0.5 * (edge_rows(jnp.concatenate(planes, axis=0)) + y_rows)
     bounds_zx.send()
     bounds_y.send()
-    rho = start_cg(lambda z: r[z], s, q)
-    cg(raw(cz), raw(cx), raw(cy), raw(s), p, q, e, y, rho, local)
+    cg(raw(cz), raw(cx), raw(cy), raw(s), p, q, e, y, lambda z: s[z] * r[z], local)
 
 
 def solve1_body(ins, outs, p, q, e, y):
     scalars, r, image, s, cz, cx, cy = ins
     (local,) = outs
     alpha = full(scalars)[0:1, 0:1]
-    rho = start_cg(lambda z: r[z] - alpha * image[z], s, q)
-    cg(cz, cx, cy, raw(s), p, q, e, y, rho, local)
-
-
-def combine_body(ins, outs, xs_lo, xs_hi, tile, wide, sems):
-    got, zrow, label, factor, local, *_ = ins
+    cg(cz, cx, cy, s, p, q, e, y, lambda z: s[z] * (r[z] - alpha * image[z]), local)
+
+
+def combine_body(ins, outs, xs_lo, xs_hi, wide, lines, sems):
+    flags, got, hits, take, factor, local, *_ = ins
     out, kept, *faces = outs
-    lane, sub = iota((CX, LANES), 1), iota((CX, LANES), 0)
     wide[...] = got[...].astype(F32)
-    _, key = slots(full(zrow)[...])
-    columns = label_columns(label, tile)
     factor = full(factor)
     flipped = wide[part_rows(EXTRA), :].T
     u = flipped[0:32, :] + flipped[32:64, :]
@@ -523,8 +567,9 @@
     for t in range(32):
         acc = acc + factor[:, t * LANES : (t + 1) * LANES] * u[t : t + 1, :]
     coef_col = jnp.sum(acc, axis=1, keepdims=True)
-    coef = jnp.sum(jnp.where(sub == lane, coef_col, 0.0), axis=0, keepdims=True)
-    coef = jnp.broadcast_to(coef, (CX, LANES))
+    pieces = split3(jnp.broadcast_to(coef_col, (KC, CY)))
+    coef = jnp.concatenate([*pieces, jnp.zeros((LANES - 3 * KC, CY), F32)], axis=0)
+    lines[...] = jnp.dot(full(hits)[...], coef.astype(BF16), preferred_element_type=F32)
     back = jnp.concatenate(
         [
             jnp.concatenate([wide[part_rows(k), :], wide[part_rows(CAP + k), :]], axis=1)
@@ -532,88 +577,71 @@
         ],
         axis=0,
     ).astype(BF16)
-    take = jnp.where(iota((ZN, CAP * ZN), 1) == key, 1.0, 0.0).astype(BF16)
-    placed = jnp.dot(take, back, preferred_element_type=F32)
-    kind = lane.astype(F32)
+    placed = jnp.dot(full(take)[...], back, preferred_element_type=F32)
     order = {0: 0, 1: 1, CZ - 2: 2, CZ - 1: 3}
     for z in range(CZ):
-        value = jnp.sum(
-            jnp.where(columns[:, z : z + 1] == kind, coef, 0.0), axis=1, keepdims=True
-        )
-        plane = local[z] + value
+        plane = local[z] + lines[z * CX : (z + 1) * CX, :]
         if z in order:
             at = order[z] * CX
             plane = plane + placed[at : at + CX, :]
         out[z] = plane
     keep = pltpu.make_async_copy(out, kept, sems)
     keep.start()
-    face_store(lambda z: out[z], faces, xs_lo, xs_hi)
+    face_store(lambda z: out[z], flags, faces, xs_lo, xs_hi)
     keep.wait()
 
 
-def apply_plane(z, v, sinv, cz, cx, cy, bounds, halos, masks):
-    bzl, bzh, bxl, bxh, byl, byh = bounds
-    hzl, hzh, hxl, hxh, hyl, hyh = halos
-    first_row, last_row, first_lane, last_lane = masks
-    inverse = sinv[z]
-    scaled = minus_neighbours(
-        v[z] * inverse,
-        v[z - 1] * sinv[z - 1] if z else None,
-        v[z + 1] * sinv[z + 1] if z + 1 < CZ else None,
-        cz[z - 1] if z else None,
-        cz[z] if z + 1 < CZ else None,
-        cx[z],
-        cy[z],
-    )
-    out = scaled * inverse
-    out = out - jnp.where(first_row, bxl[z : z + 1, :] * hxl[z : z + 1, :], 0.0)
-    out = out - jnp.where(last_row, bxh[z : z + 1, :] * hxh[z : z + 1, :], 0.0)
-    low = pltpu.roll(byl * hyl, (LANES - z) % LANES, 1)
-    high = pltpu.roll(byh * hyh, LANES - 1 - z, 1)
-    out = out - jnp.where(first_lane, jnp.concatenate([low, low], axis=1), 0.0)
-    out = out - jnp.where(last_lane, jnp.concatenate([high, high], axis=1), 0.0)
-    if z == 0:
-        out = out - bzl * hzl
-    if z == CZ - 1:
-        out = out - bzh * hzh
-    return out
-
-
-def apply_inputs(zx, by, halo_refs):
-    halos = [full(h)[...].astype(F32) for h in halo_refs]
-    zx, by = full(zx), full(by)
-    bounds = (zx[0:32, :], zx[32:64, :], zx[64:80, :], zx[80:96, :], by[0:32, :], by[32:64, :])
-    sub, lane = iota((CX, CY), 0), iota((CX, CY), 1)
-    return bounds, halos, (sub == 0, sub == CX - 1, lane == 0, lane == CY - 1)
-
-
-def apply0_body(ins, outs, tile, rows, wide):
-    v, sinv, cz, cx, cy, zx, by, r, *halo_refs, label, zrow, factor = ins
+def apply_layers(v, sinv, cz, cx, cy, zx, by, flags, halos, beyond):
+    zl, zh, xl, xh, y_rows = halo_values(flags, halos)
+    beyond[...] = edge_field(by[...] * y_rows)
+    xl, xh = zx[64:80, :] * xl, zx[80:96, :] * xh
+    sub = iota((CX, CY), 0)
+    first_row, last_row = sub == 0, sub == CX - 1
+    below, now = None, v[0] * sinv[0]
+    for z in range(CZ):
+        above = v[z + 1] * sinv[z + 1] if z + 1 < CZ else None
+        scaled = minus_neighbours(
+            now,
+            below,
+            above,
+            cz[z - 1] if z else None,
+            cz[z] if z + 1 < CZ else None,
+            cx[z],
+            cy[z],
+        )
+        out = scaled * sinv[z] - beyond[z * CX : (z + 1) * CX, :]
+        row = jnp.where(first_row, xl[z : z + 1, :], 0.0)
+        out = out - jnp.where(last_row, xh[z : z + 1, :], row)
+        if z == 0:
+            out = out - zx[0:32, :] * zl
+        if z == CZ - 1:
+            out = out - zx[32:64, :] * zh
+        yield z, out
+        below, now = now, above
+
+
+def apply0_body(ins, outs, tile, rows, wide, beyond):
+    flags, v, sinv, cz, cx, cy, zx, by, r, *halos, hits, put, factor = ins
     image, send = outs
-    bounds, halos, masks = apply_inputs(zx, by, halo_refs)
     rz = jnp.zeros((8, LANES), F32)
     curvature = jnp.zeros((8, LANES), F32)
     lines = []
-    for z in range(CZ):
-        out = apply_plane(z, v, sinv, cz, cx, cy, bounds, halos, masks)
+    for z, out in apply_layers(v, sinv, cz, cx, cy, zx, by, flags, halos, beyond):
         image[z] = out
         lines.append(jnp.sum(out, axis=1, keepdims=True))
         rz = rz + fold(r[z] * v[z])
         curvature = curvature + fold(v[z] * out)
-    columns = label_columns(label, tile)
-    u_rows = coarse_rows(lambda z: lines[z], columns, factor, rows)
+    u_rows = coarse_rows(lambda z: lines[z], full(hits), factor, rows)
     sums = (total(rz), total(curvature))
-    store_send(raw(send), face_blocks(image), full(zrow)[...], u_rows, sums, tile, wide)
-
-
-def apply1_body(ins, outs):
-    v, sinv, cz, cx, cy, zx, by, r, image0, *halo_refs, scalars = ins
+    store_send(raw(send), face_blocks(image), full(put)[...], u_rows, sums, tile, wide)
+
+
+def apply1_body(ins, outs, beyond):
+    flags, v, sinv, cz, cx, cy, zx, by, r, image0, *halos, scalars = ins
     image, sums = outs
-    bounds, halos, masks = apply_inputs(zx, by, halo_refs)
     alpha = full(scalars)[0:1, 0:1]
     sums3 = [jnp.zeros((8, LANES), F32) for _ in range(3)]
-    for z in range(CZ):
-        out = apply_plane(z, v, sinv, cz, cx, cy, bounds, halos, masks)
+    for z, out in apply_layers(v, sinv, cz, cx, cy, zx, by, flags, halos, beyond):
         image[z] = out
         at = v[z]
         sums3[0] = sums3[0] + fold((r[z] - alpha * image0[z]) * at)
@@ -647,6 +675,10 @@
 WIDE = pltpu.VMEM((ZN * PARTS, LANES), F32)
 TILE = pltpu.VMEM((LANES, LANES), F32)
 ROWS = pltpu.VMEM((KC, LANES), F32)
+LINE_FIELD = pltpu.VMEM((LINES, CY), F32)
+HITS = sds((LINES, LANES), BF16)
+PUT = sds((CAP * ZN, ZN), BF16)
+TAKE = sds((ZN, CAP * ZN), BF16)
 
 
 def swap(x):
@@ -670,11 +702,12 @@
             for axis in ("gz", "gx", "gy")
             for edge in (0, lax.axis_size(axis) - 1)
         ]
-    )
-    send0, *k_faces = run(
+        + [(1 - lax.axis_index(axis) % 2).astype(F32) for axis in ("gz", "gx", "gy")]
+    )
+    send0, hits, put, take, *k_faces = run(
         pack_body,
-        each("h", label, zrow) + each("c", r) + each("h", factor) + each("c", k),
-        each("h", PACKED, *FACE_OUTS),
+        each("s", flags) + each("h", label, zrow) + each("c", r) + each("h", factor) + each("c", k),
+        each("h", PACKED, HITS, PUT, TAKE, *FACE_OUTS),
         (TILE, ROWS, WIDE) + FACE_SCRATCH,
     )
     got0 = swap_packed(send0)
@@ -690,8 +723,8 @@
     local, s, sinv, cz, cx, cy, *bounds = run(
         solve0_body,
         each("s", flags) + each("a", *k_halos) + each("c", k, storage, r),
-        each("c", *(FIELD,) * 6) + each("h", sds((96, CY)), sds((64, LANES))),
-        (FIELD_SCRATCH,) * 4,
+        each("c", *(FIELD,) * 6) + each("h", sds((96, CY)), sds((8, LINES))),
+        (FIELD_SCRATCH,) * 4 + (LINE_FIELD,),
         ((7, 8, 9),),
     )
     matrix = (sinv, cz, cx, cy, *bounds)
@@ -699,21 +732,22 @@
     def combine(local, back, more):
         field, kept, *rest = run(
             combine_body,
-            each("v", back)
-            + each("h", zrow, label, factor)
+            each("s", flags)
+            + each("v", back)
+            + each("h", hits, take, factor)
             + each("c", local)
             + each("p", *matrix, *more),
             each("v", FIELD) + each("o", FIELD) + each("v", *FACE_OUTS),
-            FACE_SCRATCH + (TILE, WIDE, pltpu.SemaphoreType.DMA),
+            FACE_SCRATCH + (WIDE, LINE_FIELD, pltpu.SemaphoreType.DMA),
         )
-        return field, kept, exchange(rest[:6]), rest[6:]
+        return field, kept, exchange(rest[:5]), rest[5:]
 
     field, d, halos, passed = combine(local, back0, (r,))
     image0, send1 = run(
         apply0_body,
-        each("v", field, *passed, *halos) + each("h", label, zrow, factor),
+        each("s", flags) + each("v", field, *passed, *halos) + each("h", hits, put, factor),
         each("c", FIELD) + each("h", PACKED),
-        (TILE, ROWS, WIDE),
+        (TILE, ROWS, WIDE, LINE_FIELD),
     )
     got1 = swap_packed(send1)
     back1, scalars = run(
@@ -733,8 +767,9 @@
     field, v, halos, passed = combine(local, back1, (r, image0))
     image1, sums = run(
         apply1_body,
-        each("v", field, *passed, *halos) + each("h", scalars),
+        each("s", flags) + each("v", field, *passed, *halos) + each("h", scalars),
         each("c", FIELD) + each("v", sds((ZN, LANES))),
+        (LINE_FIELD,),
     )
     return run(
         final_body,

time: 139 us -> 136 us (0.978)
  waiting for transfers between devices: 9.51 us -> 13.6 us
  starting transfers between devices: 45 us -> 41.2 us
  blocking collectives: 37.5 us -> 34.7 us
    ppermute x18, waiting for transfers between devices: 3.41 us -> 7.8 us  [the longest x9 4.62 us: exchange(): lax.ppermute(second, axis, [(i, (i + 1 if i % 2 else i - 1) % n) for i in...]
    all_to_all x2, blocking collectives: 37.5 us -> 34.7 us  [swap(): return lax.all_to_all(x, AX, split_axis=0, concat_axis=0, tiled=True)]
    ppermute x18, starting transfers between devices: 21.8 us -> 19.3 us  [the longest x9 13.9 us: exchange(): lax.ppermute(second, axis, [(i, (i + 1 if i % 2 else i - 1) % n) for i in...]
  transfers between devices with their start and end apart: 21 -> 21, of which waited for: 9 -> 9; matrix products, arithmetic and copies ran while one was open for 0% -> 0% of each run, Pallas kernels for 14% -> 13%
where the time goes in v3:
time: 136 us; the launch traced here: 135 us
  Pallas kernels  44.8 us (33%)
  starting transfers between devices  41.2 us (30%)
  blocking collectives  34.7 us (26%)
  waiting for transfers between devices  13.6 us (10%)
    pallas_call x10, Pallas kernels, run(): pl.pallas_call(kernel, out_shape=tuple((pltpu.HBM(a.shape, a.dtype) if m...  44.8 us
    all_to_all x2, blocking collectives, swap(): return lax.all_to_all(x, AX, split_axis=0, concat_axis=0, tiled=True)  34.7 us
    all_to_all x3, starting transfers between devices, swap(): return lax.all_to_all(x, AX, split_axis=0, concat_axis=0, tiled=True)  21.9 us
    ppermute x9, starting transfers between devices, exchange(): lax.ppermute(second, axis, [(i, (i + 1 if i % 2 else i - 1) % n) for i in...  13.9 us
    all_to_all x3, waiting for transfers between devices, swap(): return lax.all_to_all(x, AX, split_axis=0, concat_axis=0, tiled=True)  5.8 us
    ppermute x9, starting transfers between devices, exchange(): out.append(lax.ppermute(first, axis, [(i, i ^ 1) for i in range(n)]))  5.32 us
    ppermute x9, waiting for transfers between devices, exchange(): lax.ppermute(second, axis, [(i, (i + 1 if i % 2 else i - 1) % n) for i in...  4.62 us
    ppermute x9, waiting for transfers between devices, exchange(): out.append(lax.ppermute(first, axis, [(i, i ^ 1) for i in range(n)]))  3.18 us
  transfers between devices with their start and end apart: 21, of which 9 were waited for; matrix products, arithmetic and copies ran while one was open for 0% of the time, Pallas kernels for 13%

profile of v3, /device:TPU:1, one launch (start us, length us, event | category | flops | bytes accessed | tf_op | source)
XLA Modules:
  0.0 135.3 jit_solution(8799842830098851841)
XLA Ops:
  0.7 0.1 stack.63.refs_0_
  0.8 3.9 %shard_map.86 = (bf16[1280,128]{1,0:T(8,128)(2,1)}, bf16[512,128]{1,0:T(8,128)(2,1)}, bf16[512,128]{1,0:T(8,128)(2,1)}, bf16[128,512]{1,0:T(8,128)(2,1)}, bf16[3...) custom-call(f32[9]{0:T(128)S(1)} %stack.63.refs_0_, ...), custom_call_target="tpu_custom_call" | custom-call | tf_op jit(solution)/shard_map/pallas_call | solution.py:149
  4.6 0.0 copy-start.4
  4.7 0.0 copy-start.1
  4.7 0.0 copy-start
  4.7 0.0 copy-start.3
  4.7 11.5 %all-to-all-start = ((bf16[128,5,2,128]{3,2,1,0:T(2,128)(2,1)}), bf16[128,5,2,128]{3,2,1,0:T(2,128)(2,1)S(1)}, u32[]{:S(2)}, u32[]{:S(2)}) async-start(bf16[128,5,2,128]{3,2,1,0:T(2,128)(2,1)} %bitcast.29), calls=%async_computation | async-start | bytes 655360 | tf_op jit(solution)/shard_map/all_to_all | solution.py:685
  16.2 0.0 copy-start.2
  16.2 0.0 copy-done.4
  16.2 1.1 collective-permute-start.2
  17.4 0.0 copy-done.1
  17.4 0.7 collective-permute-start
  18.1 0.0 copy-done
  18.1 1.8 %collective-permute-start.1 = (bf16[32,256]{1,0:T(8,128)(2,1)S(1)}, bf16[32,256]{1,0:T(8,128)(2,1)S(1)}, u32[]{:S(2)}, u32[]{:S(2)}) collective-permute-start(bf16[32,256]{1,0:T(8,128)(2,1)S(1)} %copy-done), channel_id=1, source_target_pairs={{0,3},{1,2},{2,1},{3,0},{4,7},{5,6},{6,5},{7,4},{8,11},{9,10},{10,... | collective-permute-start | bytes 49160 | tf_op jit(solution)/shard_map/ppermute | solution.py:249
  19.8 0.0 copy-done.3
  19.9 2.0 %collective-permute-start.3 = (bf16[16,256]{1,0:T(8,128)(2,1)S(1)}, bf16[16,256]{1,0:T(8,128)(2,1)S(1)}, u32[]{:S(2)}, u32[]{:S(2)}) collective-permute-start(bf16[16,256]{1,0:T(8,128)(2,1)S(1)} %copy-done.3), channel_id=1, source_target_pairs={{0,112},{16,32},{32,16},{48,64},{64,48},{80,96},{96,80},{112,0},{1... | collective-permute-start | bytes 24584 | tf_op jit(solution)/shard_map/ppermute | solution.py:249
  21.9 2.4 %collective-permute-start.5 = (bf16[8,512]{1,0:T(8,128)(2,1)S(1)}, bf16[8,512]{1,0:T(8,128)(2,1)S(1)}, u32[]{:S(2)}, u32[]{:S(2)}) collective-permute-start(bf16[8,512]{1,0:T(8,128)(2,1)S(1)} %copy-done.2), channel_id=1, source_target_pairs={{0,12},{4,8},{8,4},{12,0},{1,13},{5,9},{9,5},{13,1},{2,14},{6,10},... | collective-permute-start | bytes 24584 | tf_op jit(solution)/shard_map/ppermute | solution.py:249
  24.3 0.0 collective-permute-done.2.refs_3_
  24.3 0.0 collective-permute-start.4
  24.3 0.0 collective-permute-done.3.refs_4_
  24.4 1.6 %collective-permute-done.5.refs_6_ = bf16[8,512]{1,0:T(8,128)(2,1)S(1)} collective-permute-done((bf16[8,512]{1,0:T(8,128)(2,1)S(1)}, bf16[8,512]{1,0:T(8,128)(2,1)S(1)}, u32[]{:S(2)}, u32[]{:S(2)}) %collective-permute-start.5) | collective-permute-done | bytes 8224 | tf_op jit(solution)/shard_map/ppermute | solution.py:249
  25.9 1.2 collective-permute-done.4.refs_5_
  27.1 0.0 collective-permute-done.refs_1_
  27.1 0.0 collective-permute-done.1.refs_2_
  27.1 0.4 all-to-all-done
  27.6 2.2 %shard_map.87 = (bf16[1280,128]{1,0:T(8,128)(2,1)}, bf16[1280,128]{1,0:T(8,128)(2,1)}) custom-call(bf16[1280,128]{1,0:T(8,128)(2,1)S(1)} %bitcast.25, bf16[1,256,256]{2,1,0:T(8,128)(2,1)} %refs_0_.1), custom_call_target="tpu_custom_call" | custom-call | tf_op jit(solution)/shard_map/pallas_call | solution.py:149
  29.8 5.7 %all-to-all-start.1 = ((bf16[128,5,2,128]{3,2,1,0:T(2,128)(2,1)}), bf16[128,5,2,128]{3,2,1,0:T(2,128)(2,1)S(1)}, u32[]{:S(2)}, u32[]{:S(2)}) async-start(bf16[128,5,2,128]{3,2,1,0:T(2,128)(2,1)} %bitcast.30), calls=%async_computation.1 | async-start | bytes 655360 | tf_op jit(solution)/shard_map/all_to_all | solution.py:685
  35.5 9.5 %shard_map.88 = (f32[16,32,256]{2,1,0:T(8,128)}, f32[16,32,256]{2,1,0:T(8,128)}, f32[16,32,256]{2,1,0:T(8,128)}, f32[16,32,256]{2,1,0:T(8,128)}, f32[16,32,256]{...) custom-call(f32[9]{0:T(128)S(1)} %stack.63.refs_0_, ...), custom_call_target="tpu_custom_call" | custom-call | tf_op jit(solution)/shard_map/pallas_call | solution.py:149
  45.0 2.0 %all-to-all-done.1 = bf16[128,5,2,128]{3,2,1,0:T(2,128)(2,1)S(1)} async-done(((bf16[128,5,2,128]{3,2,1,0:T(2,128)(2,1)}), bf16[128,5,2,128]{3,2,1,0:T(2,128)(2,1)S(1)}, u32[]{:S(2)}, u32[]{:S(2)}) %all-to-all-start.1) | async-done | bytes 327712 | tf_op jit(solution)/shard_map/all_to_all | solution.py:685
  47.0 4.5 %shard_map.89 = (f32[16,32,256]{2,1,0:T(8,128)S(1)}, f32[16,32,256]{2,1,0:T(8,128)}, bf16[32,256]{1,0:T(8,128)(2,1)S(1)}, bf16[32,256]{1,0:T(8,128)(2,1)S(1)}, b...) custom-call(f32[9]{0:T(128)S(1)} %stack.63.refs_0_, ...), custom_call_target="tpu_custom_call" | custom-call | tf_op jit(solution)/shard_map/pallas_call | solution.py:149
  51.5 1.4 collective-permute-start.8
  52.8 0.4 collective-permute-start.6
  53.2 0.1 collective-permute-start.7
  53.3 2.1 %collective-permute-start.9 = (bf16[16,256]{1,0:T(8,128)(2,1)S(1)}, bf16[16,256]{1,0:T(8,128)(2,1)S(1)}, u32[]{:S(2)}, u32[]{:S(2)}) collective-permute-start(bf16[16,256]{1,0:T(8,128)(2,1)S(1)} %get-tuple-element.98), channel_id=1, source_target_pairs={{0,112},{16,32},{32,16},{48,64},{64,48},{80,96},{96,80},{112,0},{1... | collective-permute-start | bytes 24584 | tf_op jit(solution)/shard_map/ppermute | solution.py:249
  55.3 2.4 %collective-permute-start.11 = (bf16[8,512]{1,0:T(8,128)(2,1)S(1)}, bf16[8,512]{1,0:T(8,128)(2,1)S(1)}, u32[]{:S(2)}, u32[]{:S(2)}) collective-permute-start(bf16[8,512]{1,0:T(8,128)(2,1)S(1)} %get-tuple-element.99), channel_id=1, source_target_pairs={{0,12},{4,8},{8,4},{12,0},{1,13},{5,9},{9,5},{13,1},{2,14},{6,10},... | collective-permute-start | bytes 24584 | tf_op jit(solution)/shard_map/ppermute | solution.py:249
  57.8 0.0 collective-permute-done.8.refs_11_
  57.8 0.0 collective-permute-start.10
  57.8 0.0 collective-permute-done.9.refs_12_
  57.8 1.3 collective-permute-done.11.refs_14_
  59.1 1.2 collective-permute-done.10.refs_13_
  60.3 0.0 collective-permute-done.6.refs_9_
  60.3 0.0 collective-permute-done.7.refs_10_
  60.3 4.1 %shard_map.90 = (f32[16,32,256]{2,1,0:T(8,128)}, bf16[1280,128]{1,0:T(8,128)(2,1)}) custom-call(f32[9]{0:T(128)S(1)} %stack.63.refs_0_, f32[16,32,256]{2,1,0:T(8,128)S(1)} %get-tuple-element.87.refs_1_, f32[16,32,256]{2,1,0:T(8,128)S(1)} %get-tuple-element.88.refs_2_, f32[16,32,256]{2,1,0:T(8,128)S(1)} %get-tuple-element.89.refs_3_, ...), custom_call_target="tpu_custom_call" | custom-call | tf_op jit(solution)/shard_map/pallas_call | solution.py:149
  64.4 18.1 %all_to_all.31 = bf16[128,5,2,128]{3,2,1,0:T(2,128)(2,1)S(1)} all-to-all(bf16[128,5,2,128]{3,2,1,0:T(2,128)(2,1)} %bitcast.31), channel_id=1, replica_groups=mesh['gx'=8,'gy'=4,'gz'=4] {'gx','gy','gz'}, dimensions={0} | all-to-all | bytes 655360 | tf_op jit(solution)/shard_map/all_to_all | solution.py:685
  82.5 2.3 %shard_map.91 = (bf16[1280,128]{1,0:T(8,128)(2,1)}, f32[8,128]{1,0:T(8,128)}) custom-call(bf16[1,256,256]{2,1,0:T(8,128)(2,1)} %refs_0_.1, bf16[1280,128]{1,0:T(8,128)(2,1)} %get-tuple-element.70.refs_1_, bf16[1280,128]{1,0:T(8,128)(2,1)S(1)} %bitcast.26), custom_call_target="tpu_custom_call" | custom-call | tf_op jit(solution)/shard_map/pallas_call | solution.py:149
  84.8 4.7 %all-to-all-start.3 = ((bf16[128,5,2,128]{3,2,1,0:T(2,128)(2,1)}), bf16[128,5,2,128]{3,2,1,0:T(2,128)(2,1)S(1)}, u32[]{:S(2)}, u32[]{:S(2)}) async-start(bf16[128,5,2,128]{3,2,1,0:T(2,128)(2,1)} %bitcast.32), calls=%async_computation.3 | async-start | bytes 655360 | tf_op jit(solution)/shard_map/all_to_all | solution.py:685
  89.6 8.1 %shard_map.92.refs_5_ = f32[16,32,256]{2,1,0:T(8,128)} custom-call(f32[8,128]{1,0:T(8,128)} %get-tuple-element.102.refs_0_.refs_16_, f32[16,32,256]{2,1,0:T(8,128)} %refs_4_.7, f32[16,32,256]{2,1,0:T(8,128)} %get-tuple-element.104.refs_2_.refs_13_.refs_5_, f32[16,32,256]{2,1,0:T(8,128)} %get-tuple-element.105.refs_3_, ...), custom_call_target="tpu_custom_call" | custom-call | tf_op jit(solution)/shard_map/pallas_call | solution.py:149
  97.6 3.4 %all-to-all-done.3 = bf16[128,5,2,128]{3,2,1,0:T(2,128)(2,1)S(1)} async-done(((bf16[128,5,2,128]{3,2,1,0:T(2,128)(2,1)}), bf16[128,5,2,128]{3,2,1,0:T(2,128)(2,1)S(1)}, u32[]{:S(2)}, u32[]{:S(2)}) %all-to-all-start.3) | async-done | bytes 327712 | tf_op jit(solution)/shard_map/all_to_all | solution.py:685
  101.0 4.5 %shard_map.93 = (f32[16,32,256]{2,1,0:T(8,128)S(1)}, f32[16,32,256]{2,1,0:T(8,128)}, bf16[32,256]{1,0:T(8,128)(2,1)S(1)}, bf16[32,256]{1,0:T(8,128)(2,1)S(1)}, b...) custom-call(f32[9]{0:T(128)S(1)} %stack.63.refs_0_, ...), custom_call_target="tpu_custom_call" | custom-call | tf_op jit(solution)/shard_map/pallas_call | solution.py:149
  105.6 1.4 collective-permute-start.14
  106.9 0.4 collective-permute-start.12
  107.3 0.0 collective-permute-start.13
  107.3 1.2 collective-permute-start.15
  108.5 1.9 %collective-permute-start.17 = (bf16[8,512]{1,0:T(8,128)(2,1)S(1)}, bf16[8,512]{1,0:T(8,128)(2,1)S(1)}, u32[]{:S(2)}, u32[]{:S(2)}) collective-permute-start(bf16[8,512]{1,0:T(8,128)(2,1)S(1)} %get-tuple-element.119), channel_id=1, source_target_pairs={{0,12},{4,8},{8,4},{12,0},{1,13},{5,9},{9,5},{13,1},{2,14},{6,10},... | collective-permute-start | bytes 24584 | tf_op jit(solution)/shard_map/ppermute | solution.py:249
  110.4 0.0 collective-permute-done.14.refs_12_
  110.4 0.0 collective-permute-start.16
  110.4 0.0 collective-permute-done.15.refs_13_
  110.4 1.8 %collective-permute-done.17.refs_15_ = bf16[8,512]{1,0:T(8,128)(2,1)S(1)} collective-permute-done((bf16[8,512]{1,0:T(8,128)(2,1)S(1)}, bf16[8,512]{1,0:T(8,128)(2,1)S(1)}, u32[]{:S(2)}, u32[]{:S(2)}) %collective-permute-start.17) | collective-permute-done | bytes 8224 | tf_op jit(solution)/shard_map/ppermute | solution.py:249
  112.2 0.7 collective-permute-done.16.refs_14_
  112.9 0.0 collective-permute-done.12.refs_10_
  112.9 0.0 collective-permute-done.13.refs_11_
  112.9 2.8 %shard_map.94 = (f32[16,32,256]{2,1,0:T(8,128)}, f32[128,128]{1,0:T(8,128)S(1)}) custom-call(f32[9]{0:T(128)S(1)} %stack.63.refs_0_, f32[16,32,256]{2,1,0:T(8,128)S(1)} %get-tuple-element.106.refs_1_, f32[16,32,256]{2,1,0:T(8,128)S(1)} %get-tuple-element.107.refs_2_, f32[16,32,256]{2,1,0:T(8,128)S(1)} %get-tuple-element.108.refs_3_, ...), custom_call_target="tpu_custom_call" | custom-call | tf_op jit(solution)/shard_map/pallas_call | solution.py:149
  115.7 16.6 %all_to_all.32 = f32[128,1,128]{2,1,0:T(1,128)S(1)} all-to-all(f32[128,1,128]{2,1,0:T(1,128)S(1)} %bitcast.28), channel_id=1, replica_groups=mesh['gx'=8,'gy'=4,'gz'=4] {'gx','gy','gz'}, dimensions={0} | all-to-all | bytes 131072 | tf_op jit(solution)/shard_map/all_to_all | solution.py:685
  132.3 2.9 %shard_map.95 = (f32[16,32,256]{2,1,0:T(8,128)}, f32[16,32,256]{2,1,0:T(8,128)}) custom-call(f32[8,128]{1,0:T(8,128)} %get-tuple-element.102.refs_0_.refs_16_, f32[128,128]{1,0:T(8,128)S(1)} %bitcast.27, f32[16,32,256]{2,1,0:T(8,128)} %get-tuple-element.121.refs_2_, f32[16,32,256]{2,1,0:T(8,128)} %get-tuple-element.122.refs_3_, f32[16,32,256]{2,1,0:T(8,128)} %refs_4_.7, ...), custom_call_target="tpu_custom_call" | custom-call | tf_op jit(solution)/shard_map/pallas_call | solution.py:149
  (1 shorter events, 0.0 us)
Async XLA Ops:
  4.6 11.6 %copy-start.4 = (bf16[16,256]{1,0:T(8,128)(2,1)S(1)}, bf16[16,256]{1,0:T(8,128)(2,1)}, u32[]{:S(2)}) copy-start(bf16[16,256]{1,0:T(8,128)(2,1)} %get-tuple-element.66) | copy-start | bytes 24580
  4.7 12.7 %copy-start.1 = (bf16[32,256]{1,0:T(8,128)(2,1)S(1)}, bf16[32,256]{1,0:T(8,128)(2,1)}, u32[]{:S(2)}) copy-start(bf16[32,256]{1,0:T(8,128)(2,1)} %get-tuple-element.64) | copy-start | bytes 49156
  4.7 13.4 %copy-start = (bf16[32,256]{1,0:T(8,128)(2,1)S(1)}, bf16[32,256]{1,0:T(8,128)(2,1)}, u32[]{:S(2)}) copy-start(bf16[32,256]{1,0:T(8,128)(2,1)} %get-tuple-element.65) | copy-start | bytes 49156
  4.7 15.2 %copy-start.3 = (bf16[16,256]{1,0:T(8,128)(2,1)S(1)}, bf16[16,256]{1,0:T(8,128)(2,1)}, u32[]{:S(2)}) copy-start(bf16[16,256]{1,0:T(8,128)(2,1)} %get-tuple-element.67) | copy-start | bytes 24580
  4.7 22.9 %all-to-all-start = ((bf16[128,5,2,128]{3,2,1,0:T(2,128)(2,1)}), bf16[128,5,2,128]{3,2,1,0:T(2,128)(2,1)S(1)}, u32[]{:S(2)}, u32[]{:S(2)}) async-start(bf16[128,5,2,128]{3,2,1,0:T(2,128)(2,1)} %bitcast.29), calls=%async_computation | async-start | bytes 655360 | tf_op jit(solution)/shard_map/all_to_all | solution.py:685
  16.2 5.7 %copy-start.2 = (bf16[8,512]{1,0:T(8,128)(2,1)S(1)}, bf16[8,512]{1,0:T(8,128)(2,1)}, u32[]{:S(2)}) copy-start(bf16[8,512]{1,0:T(8,128)(2,1)} %get-tuple-element.68) | copy-start | bytes 24580
  16.2 8.1 %collective-permute-start.2 = (bf16[16,256]{1,0:T(8,128)(2,1)S(1)}, bf16[16,256]{1,0:T(8,128)(2,1)S(1)}, u32[]{:S(2)}, u32[]{:S(2)}) collective-permute-start(bf16[16,256]{1,0:T(8,128)(2,1)S(1)} %copy-done.4), channel_id=1, source_target_pairs={{0,16},{16,0},{32,48},{48,32},{64,80},{80,64},{96,112},{112,96},{1... | collective-permute-start | bytes 24584 | tf_op jit(solution)/shard_map/ppermute | solution.py:247
  17.4 9.8 %collective-permute-start = (bf16[32,256]{1,0:T(8,128)(2,1)S(1)}, bf16[32,256]{1,0:T(8,128)(2,1)S(1)}, u32[]{:S(2)}, u32[]{:S(2)}) collective-permute-start(bf16[32,256]{1,0:T(8,128)(2,1)S(1)} %copy-done.1), channel_id=1, source_target_pairs={{0,1},{1,0},{2,3},{3,2},{4,5},{5,4},{6,7},{7,6},{8,9},{9,8},{10,11... | collective-permute-start | bytes 49160 | tf_op jit(solution)/shard_map/ppermute | solution.py:247
  18.1 9.1 %collective-permute-start.1 = (bf16[32,256]{1,0:T(8,128)(2,1)S(1)}, bf16[32,256]{1,0:T(8,128)(2,1)S(1)}, u32[]{:S(2)}, u32[]{:S(2)}) collective-permute-start(bf16[32,256]{1,0:T(8,128)(2,1)S(1)} %copy-done), channel_id=1, source_target_pairs={{0,3},{1,2},{2,1},{3,0},{4,7},{5,6},{6,5},{7,4},{8,11},{9,10},{10,... | collective-permute-start | bytes 49160 | tf_op jit(solution)/shard_map/ppermute | solution.py:249
  19.9 4.5 %collective-permute-start.3 = (bf16[16,256]{1,0:T(8,128)(2,1)S(1)}, bf16[16,256]{1,0:T(8,128)(2,1)S(1)}, u32[]{:S(2)}, u32[]{:S(2)}) collective-permute-start(bf16[16,256]{1,0:T(8,128)(2,1)S(1)} %copy-done.3), channel_id=1, source_target_pairs={{0,112},{16,32},{32,16},{48,64},{64,48},{80,96},{96,80},{112,0},{1... | collective-permute-start | bytes 24584 | tf_op jit(solution)/shard_map/ppermute | solution.py:249
  21.9 4.0 %collective-permute-start.5 = (bf16[8,512]{1,0:T(8,128)(2,1)S(1)}, bf16[8,512]{1,0:T(8,128)(2,1)S(1)}, u32[]{:S(2)}, u32[]{:S(2)}) collective-permute-start(bf16[8,512]{1,0:T(8,128)(2,1)S(1)} %copy-done.2), channel_id=1, source_target_pairs={{0,12},{4,8},{8,4},{12,0},{1,13},{5,9},{9,5},{13,1},{2,14},{6,10},... | collective-permute-start | bytes 24584 | tf_op jit(solution)/shard_map/ppermute | solution.py:249
  24.3 2.8 %collective-permute-start.4 = (bf16[8,512]{1,0:T(8,128)(2,1)S(1)}, bf16[8,512]{1,0:T(8,128)(2,1)S(1)}, u32[]{:S(2)}, u32[]{:S(2)}) collective-permute-start(bf16[8,512]{1,0:T(8,128)(2,1)S(1)} %copy-done.2), channel_id=1, source_target_pairs={{0,4},{4,0},{8,12},{12,8},{1,5},{5,1},{9,13},{13,9},{2,6},{6,2},{1... | collective-permute-start | bytes 24584 | tf_op jit(solution)/shard_map/ppermute | solution.py:247
  29.8 17.2 %all-to-all-start.1 = ((bf16[128,5,2,128]{3,2,1,0:T(2,128)(2,1)}), bf16[128,5,2,128]{3,2,1,0:T(2,128)(2,1)S(1)}, u32[]{:S(2)}, u32[]{:S(2)}) async-start(bf16[128,5,2,128]{3,2,1,0:T(2,128)(2,1)} %bitcast.30), calls=%async_computation.1 | async-start | bytes 655360 | tf_op jit(solution)/shard_map/all_to_all | solution.py:685
  51.5 6.3 %collective-permute-start.8 = (bf16[16,256]{1,0:T(8,128)(2,1)S(1)}, bf16[16,256]{1,0:T(8,128)(2,1)S(1)}, u32[]{:S(2)}, u32[]{:S(2)}) collective-permute-start(bf16[16,256]{1,0:T(8,128)(2,1)S(1)} %get-tuple-element.97), channel_id=1, source_target_pairs={{0,16},{16,0},{32,48},{48,32},{64,80},{80,64},{96,112},{112,96},{1... | collective-permute-start | bytes 24584 | tf_op jit(solution)/shard_map/ppermute | solution.py:247
  52.8 7.5 %collective-permute-start.6 = (bf16[32,256]{1,0:T(8,128)(2,1)S(1)}, bf16[32,256]{1,0:T(8,128)(2,1)S(1)}, u32[]{:S(2)}, u32[]{:S(2)}) collective-permute-start(bf16[32,256]{1,0:T(8,128)(2,1)S(1)} %get-tuple-element.95), channel_id=1, source_target_pairs={{0,1},{1,0},{2,3},{3,2},{4,5},{5,4},{6,7},{7,6},{8,9},{9,8},{10,11... | collective-permute-start | bytes 49160 | tf_op jit(solution)/shard_map/ppermute | solution.py:247
  53.2 7.1 %collective-permute-start.7 = (bf16[32,256]{1,0:T(8,128)(2,1)S(1)}, bf16[32,256]{1,0:T(8,128)(2,1)S(1)}, u32[]{:S(2)}, u32[]{:S(2)}) collective-permute-start(bf16[32,256]{1,0:T(8,128)(2,1)S(1)} %get-tuple-element.96), channel_id=1, source_target_pairs={{0,3},{1,2},{2,1},{3,0},{4,7},{5,6},{6,5},{7,4},{8,11},{9,10},{10,... | collective-permute-start | bytes 49160 | tf_op jit(solution)/shard_map/ppermute | solution.py:249
  53.3 4.5 %collective-permute-start.9 = (bf16[16,256]{1,0:T(8,128)(2,1)S(1)}, bf16[16,256]{1,0:T(8,128)(2,1)S(1)}, u32[]{:S(2)}, u32[]{:S(2)}) collective-permute-start(bf16[16,256]{1,0:T(8,128)(2,1)S(1)} %get-tuple-element.98), channel_id=1, source_target_pairs={{0,112},{16,32},{32,16},{48,64},{64,48},{80,96},{96,80},{112,0},{1... | collective-permute-start | bytes 24584 | tf_op jit(solution)/shard_map/ppermute | solution.py:249
  55.3 3.7 %collective-permute-start.11 = (bf16[8,512]{1,0:T(8,128)(2,1)S(1)}, bf16[8,512]{1,0:T(8,128)(2,1)S(1)}, u32[]{:S(2)}, u32[]{:S(2)}) collective-permute-start(bf16[8,512]{1,0:T(8,128)(2,1)S(1)} %get-tuple-element.99), channel_id=1, source_target_pairs={{0,12},{4,8},{8,4},{12,0},{1,13},{5,9},{9,5},{13,1},{2,14},{6,10},... | collective-permute-start | bytes 24584 | tf_op jit(solution)/shard_map/ppermute | solution.py:249
  57.8 2.5 %collective-permute-start.10 = (bf16[8,512]{1,0:T(8,128)(2,1)S(1)}, bf16[8,512]{1,0:T(8,128)(2,1)S(1)}, u32[]{:S(2)}, u32[]{:S(2)}) collective-permute-start(bf16[8,512]{1,0:T(8,128)(2,1)S(1)} %get-tuple-element.99), channel_id=1, source_target_pairs={{0,4},{4,0},{8,12},{12,8},{1,5},{5,1},{9,13},{13,9},{2,6},{6,2},{1... | collective-permute-start | bytes 24584 | tf_op jit(solution)/shard_map/ppermute | solution.py:247
  84.8 16.2 %all-to-all-start.3 = ((bf16[128,5,2,128]{3,2,1,0:T(2,128)(2,1)}), bf16[128,5,2,128]{3,2,1,0:T(2,128)(2,1)S(1)}, u32[]{:S(2)}, u32[]{:S(2)}) async-start(bf16[128,5,2,128]{3,2,1,0:T(2,128)(2,1)} %bitcast.32), calls=%async_computation.3 | async-start | bytes 655360 | tf_op jit(solution)/shard_map/all_to_all | solution.py:685
  105.6 4.8 %collective-permute-start.14 = (bf16[16,256]{1,0:T(8,128)(2,1)S(1)}, bf16[16,256]{1,0:T(8,128)(2,1)S(1)}, u32[]{:S(2)}, u32[]{:S(2)}) collective-permute-start(bf16[16,256]{1,0:T(8,128)(2,1)S(1)} %get-tuple-element.117), channel_id=1, source_target_pairs={{0,16},{16,0},{32,48},{48,32},{64,80},{80,64},{96,112},{112,96},{1... | collective-permute-start | bytes 24584 | tf_op jit(solution)/shard_map/ppermute | solution.py:247
  106.9 6.0 %collective-permute-start.12 = (bf16[32,256]{1,0:T(8,128)(2,1)S(1)}, bf16[32,256]{1,0:T(8,128)(2,1)S(1)}, u32[]{:S(2)}, u32[]{:S(2)}) collective-permute-start(bf16[32,256]{1,0:T(8,128)(2,1)S(1)} %get-tuple-element.115), channel_id=1, source_target_pairs={{0,1},{1,0},{2,3},{3,2},{4,5},{5,4},{6,7},{7,6},{8,9},{9,8},{10,11... | collective-permute-start | bytes 49160 | tf_op jit(solution)/shard_map/ppermute | solution.py:247
  107.3 5.6 %collective-permute-start.13 = (bf16[32,256]{1,0:T(8,128)(2,1)S(1)}, bf16[32,256]{1,0:T(8,128)(2,1)S(1)}, u32[]{:S(2)}, u32[]{:S(2)}) collective-permute-start(bf16[32,256]{1,0:T(8,128)(2,1)S(1)} %get-tuple-element.116), channel_id=1, source_target_pairs={{0,3},{1,2},{2,1},{3,0},{4,7},{5,6},{6,5},{7,4},{8,11},{9,10},{10,... | collective-permute-start | bytes 49160 | tf_op jit(solution)/shard_map/ppermute | solution.py:249
  107.3 3.1 %collective-permute-start.15 = (bf16[16,256]{1,0:T(8,128)(2,1)S(1)}, bf16[16,256]{1,0:T(8,128)(2,1)S(1)}, u32[]{:S(2)}, u32[]{:S(2)}) collective-permute-start(bf16[16,256]{1,0:T(8,128)(2,1)S(1)} %get-tuple-element.118), channel_id=1, source_target_pairs={{0,112},{16,32},{32,16},{48,64},{64,48},{80,96},{96,80},{112,0},{1... | collective-permute-start | bytes 24584 | tf_op jit(solution)/shard_map/ppermute | solution.py:249
  108.5 3.7 %collective-permute-start.17 = (bf16[8,512]{1,0:T(8,128)(2,1)S(1)}, bf16[8,512]{1,0:T(8,128)(2,1)S(1)}, u32[]{:S(2)}, u32[]{:S(2)}) collective-permute-start(bf16[8,512]{1,0:T(8,128)(2,1)S(1)} %get-tuple-element.119), channel_id=1, source_target_pairs={{0,12},{4,8},{8,4},{12,0},{1,13},{5,9},{9,5},{13,1},{2,14},{6,10},... | collective-permute-start | bytes 24584 | tf_op jit(solution)/shard_map/ppermute | solution.py:249
  110.4 2.5 %collective-permute-start.16 = (bf16[8,512]{1,0:T(8,128)(2,1)S(1)}, bf16[8,512]{1,0:T(8,128)(2,1)S(1)}, u32[]{:S(2)}, u32[]{:S(2)}) collective-permute-start(bf16[8,512]{1,0:T(8,128)(2,1)S(1)} %get-tuple-element.119), channel_id=1, source_target_pairs={{0,4},{4,0},{8,12},{12,8},{1,5},{5,1},{9,13},{13,9},{2,6},{6,2},{1... | collective-permute-start | bytes 24584 | tf_op jit(solution)/shard_map/ppermute | solution.py:247

commit v4 on v3

--- a/solution.py
+++ b/solution.py
@@ -239,16 +239,16 @@
 FACE_SCRATCH = (pltpu.VMEM((CZ, CY), F32), pltpu.VMEM((CZ, CY), F32))
 
 
+def pair(axis, first, second):
+    n = lax.axis_size(axis)
+    even = [(i, i ^ 1) for i in range(n)]
+    odd = [(i, (i + 1 if i % 2 else i - 1) % n) for i in range(n)]
+    return [lax.ppermute(first, axis, even), lax.ppermute(second, axis, odd)]
+
+
 def exchange(faces):
     za, zb, xa, xb, ys = faces
-    out = []
-    for axis, first, second in (("gz", za, zb), ("gx", xa, xb), ("gy", ys, ys)):
-        n = lax.axis_size(axis)
-        out.append(lax.ppermute(first, axis, [(i, i ^ 1) for i in range(n)]))
-        out.append(
-            lax.ppermute(second, axis, [(i, (i + 1 if i % 2 else i - 1) % n) for i in range(n)])
-        )
-    return out
+    return pair("gz", za, zb) + pair("gx", xa, xb) + pair("gy", ys, ys)
 
 
 def halo_values(flags, got):
@@ -311,25 +311,31 @@
     send[...] = wide[...].astype(BF16)
 
 
-def label_hits(label, tile, hits):
+def label_hits(label, tile, hits, flipped):
     tile[...] = jnp.zeros((LANES, LANES), F32)
     tile[0:CZ, 0:CX] = full(label)[...].astype(F32)
     columns = tile[...].T[0:CX, :]
     lane = iota((CX, LANES), 1)
     kind = jnp.where(lane < 3 * KC, lane % KC, -1).astype(F32)
+    columns_of = []
     for z in range(CZ):
         hit = jnp.where(columns[:, z : z + 1] == kind, 1.0, 0.0)
         hits[z * CX : (z + 1) * CX, :] = hit.astype(BF16)
-
-
-def coarse_rows(line_of, hits, factor, rows):
-    lane = iota((CX, LANES), 1)
-    sub = iota((CX, LANES), 0)
-    acc = jnp.zeros((CX, LANES), F32)
-    for z in range(CZ):
-        acc = acc + hits[z * CX : (z + 1) * CX, :].astype(F32) * line_of(z)
-    g_row = jnp.broadcast_to(jnp.sum(acc, axis=0, keepdims=True), (CX, LANES))
-    g_col = jnp.sum(jnp.where(sub == lane, g_row, 0.0), axis=1, keepdims=True)
+        columns_of.append(hit)
+    flipped[...] = jnp.concatenate(columns_of, axis=0).T[0:KC, :].astype(BF16)
+
+
+def store_split(plane, z, high, low):
+    top = plane.astype(BF16)
+    high[z * CX : (z + 1) * CX, :] = top
+    low[z * CX : (z + 1) * CX, :] = (plane - top.astype(F32)).astype(BF16)
+
+
+def coarse_rows(high, low, flipped, factor, rows):
+    hits = flipped[0:KC, :]
+    sums = jnp.dot(hits, high[...], preferred_element_type=F32)
+    sums = sums + jnp.dot(hits, low[...], preferred_element_type=F32)
+    g_col = jnp.sum(sums[:, :LANES] + sums[:, LANES:], axis=1, keepdims=True)
     g = jnp.broadcast_to(g_col, (KC, LANES))
     factor = full(factor)
     for t in range(32):
@@ -343,16 +349,16 @@
     return jnp.concatenate([field[0], field[1], field[CZ - 2], field[CZ - 1]], axis=0).astype(BF16)
 
 
-def pack_body(ins, outs, tile, rows, wide, xs_lo, xs_hi):
+def pack_body(ins, outs, tile, rows, wide, xs_lo, xs_hi, fhigh, flow):
     flags, label, zrow, r, factor, k = ins
-    send, hits, put, take, *faces = outs
-    label_hits(label, tile, raw(hits))
+    send, hits, flipped, put, take, *faces = outs
+    label_hits(label, tile, raw(hits), raw(flipped))
     raw(put)[...], raw(take)[...] = zone_hits(full(zrow)[...])
-    for x in (hits, put, take):
+    for x in (hits, flipped, put, take):
         x.send()
-    u_rows = coarse_rows(
-        lambda z: jnp.sum(r[z], axis=1, keepdims=True), raw(hits), factor, rows
-    )
+    for z in range(CZ):
+        store_split(r[z], z, fhigh, flow)
+    u_rows = coarse_rows(fhigh, flow, raw(flipped), factor, rows)
     store_send(raw(send), face_blocks(r), raw(put)[...], u_rows, (), tile, wide)
     send.send()
     face_store(lambda z: k[z], flags, faces, xs_lo, xs_hi)
@@ -556,9 +562,9 @@
     cg(cz, cx, cy, s, p, q, e, y, lambda z: s[z] * (r[z] - alpha * image[z]), local)
 
 
-def combine_body(ins, outs, xs_lo, xs_hi, wide, lines, sems):
+def combine_body(ins, outs, xs_lo, xs_hi, wide, lines):
     flags, got, hits, take, factor, local, *_ = ins
-    out, kept, *faces = outs
+    out, *faces = outs
     wide[...] = got[...].astype(F32)
     factor = full(factor)
     flipped = wide[part_rows(EXTRA), :].T
@@ -585,10 +591,7 @@
             at = order[z] * CX
             plane = plane + placed[at : at + CX, :]
         out[z] = plane
-    keep = pltpu.make_async_copy(out, kept, sems)
-    keep.start()
     face_store(lambda z: out[z], flags, faces, xs_lo, xs_hi)
-    keep.wait()
 
 
 def apply_layers(v, sinv, cz, cx, cy, zx, by, flags, halos, beyond):
@@ -620,31 +623,35 @@
         below, now = now, above
 
 
-def apply0_body(ins, outs, tile, rows, wide, beyond):
-    flags, v, sinv, cz, cx, cy, zx, by, r, *halos, hits, put, factor = ins
-    image, send = outs
+def apply0_body(ins, outs, tile, rows, wide, beyond, fhigh, flow, sem):
+    flags, v, sinv, cz, cx, cy, zx, by, r, *halos, flipped, put, factor = ins
+    image, send, kept = outs
+    keep = pltpu.make_async_copy(v, kept, sem)
+    keep.start()
     rz = jnp.zeros((8, LANES), F32)
     curvature = jnp.zeros((8, LANES), F32)
-    lines = []
     for z, out in apply_layers(v, sinv, cz, cx, cy, zx, by, flags, halos, beyond):
         image[z] = out
-        lines.append(jnp.sum(out, axis=1, keepdims=True))
+        store_split(out, z, fhigh, flow)
         rz = rz + fold(r[z] * v[z])
         curvature = curvature + fold(v[z] * out)
-    u_rows = coarse_rows(lambda z: lines[z], full(hits), factor, rows)
+    u_rows = coarse_rows(fhigh, flow, full(flipped), factor, rows)
     sums = (total(rz), total(curvature))
     store_send(raw(send), face_blocks(image), full(put)[...], u_rows, sums, tile, wide)
-
-
-def apply1_body(ins, outs, beyond):
-    flags, v, sinv, cz, cx, cy, zx, by, r, image0, *halos, scalars = ins
-    image, sums = outs
-    alpha = full(scalars)[0:1, 0:1]
+    send.send()
+    keep.wait()
+
+
+def apply1_body(ins, outs, beyond, sem):
+    flags, v, sinv, cz, cx, cy, zx, by, r, image0, *halos = ins
+    image, sums, kept = outs
+    keep = pltpu.make_async_copy(v, kept, sem)
+    keep.start()
     sums3 = [jnp.zeros((8, LANES), F32) for _ in range(3)]
     for z, out in apply_layers(v, sinv, cz, cx, cy, zx, by, flags, halos, beyond):
         image[z] = out
         at = v[z]
-        sums3[0] = sums3[0] + fold((r[z] - alpha * image0[z]) * at)
+        sums3[0] = sums3[0] + fold(r[z] * at)
         sums3[1] = sums3[1] + fold(at * out)
         sums3[2] = sums3[2] + fold(at * image0[z])
     lane = iota((ZN, LANES), 1)
@@ -652,6 +659,7 @@
     for i in range(3):
         row = jnp.where(lane == i, total(sums3[i]), row)
     sums[...] = row
+    keep.wait()
 
 
 def final_body(ins, outs):
@@ -660,7 +668,8 @@
     scalars = full(scalars)
     sums = jnp.sum(got[...], axis=0, keepdims=True)
     alpha0, rz0, curvature0 = scalars[0:1, 0:1], scalars[1:2, 0:1], scalars[2:3, 0:1]
-    rz1, vav, vad = sums[:, 0:1], sums[:, 1:2], sums[:, 2:3]
+    rv, vav, vad = sums[:, 0:1], sums[:, 1:2], sums[:, 2:3]
+    rz1 = rv - alpha0 * vad
     beta = rz1 / rz0
     alpha1 = rz1 / (vav + 2.0 * beta * vad + beta * beta * curvature0)
     mix = alpha0 + alpha1 * beta
@@ -677,6 +686,8 @@
 ROWS = pltpu.VMEM((KC, LANES), F32)
 LINE_FIELD = pltpu.VMEM((LINES, CY), F32)
 HITS = sds((LINES, LANES), BF16)
+FLIPPED = sds((KC, LINES), BF16)
+FLAT = pltpu.VMEM((LINES, CY), BF16)
 PUT = sds((CAP * ZN, ZN), BF16)
 TAKE = sds((ZN, CAP * ZN), BF16)
 
@@ -704,11 +715,11 @@
         ]
         + [(1 - lax.axis_index(axis) % 2).astype(F32) for axis in ("gz", "gx", "gy")]
     )
-    send0, hits, put, take, *k_faces = run(
+    send0, hits, flipped, put, take, *k_faces = run(
         pack_body,
         each("s", flags) + each("h", label, zrow) + each("c", r) + each("h", factor) + each("c", k),
-        each("h", PACKED, HITS, PUT, TAKE, *FACE_OUTS),
-        (TILE, ROWS, WIDE) + FACE_SCRATCH,
+        each("h", PACKED, HITS, FLIPPED, PUT, TAKE, *FACE_OUTS),
+        (TILE, ROWS, WIDE) + FACE_SCRATCH + (FLAT, FLAT),
     )
     got0 = swap_packed(send0)
     k_halos = exchange(k_faces)
@@ -730,24 +741,24 @@
     matrix = (sinv, cz, cx, cy, *bounds)
 
     def combine(local, back, more):
-        field, kept, *rest = run(
+        field, *rest = run(
             combine_body,
             each("s", flags)
             + each("v", back)
             + each("h", hits, take, factor)
             + each("c", local)
             + each("p", *matrix, *more),
-            each("v", FIELD) + each("o", FIELD) + each("v", *FACE_OUTS),
-            FACE_SCRATCH + (WIDE, LINE_FIELD, pltpu.SemaphoreType.DMA),
+            each("v", FIELD, *FACE_OUTS),
+            FACE_SCRATCH + (WIDE, LINE_FIELD),
         )
-        return field, kept, exchange(rest[:5]), rest[5:]
-
-    field, d, halos, passed = combine(local, back0, (r,))
-    image0, send1 = run(
+        return field, exchange(rest[:5]), rest[5:]
+
+    field, halos, passed = combine(local, back0, (r,))
+    image0, send1, d = run(
         apply0_body,
-        each("s", flags) + each("v", field, *passed, *halos) + each("h", hits, put, factor),
-        each("c", FIELD) + each("h", PACKED),
-        (TILE, ROWS, WIDE, LINE_FIELD),
+        each("s", flags) + each("v", field, *passed, *halos) + each("h", flipped, put, factor),
+        each("c", FIELD) + each("h", PACKED) + each("o", FIELD),
+        (TILE, ROWS, WIDE, LINE_FIELD, FLAT, FLAT, pltpu.SemaphoreType.DMA),
     )
     got1 = swap_packed(send1)
     back1, scalars = run(
@@ -764,12 +775,12 @@
         (FIELD_SCRATCH,) * 4,
         ((1, 2, 3), (4, 5, 6)),
     )
-    field, v, halos, passed = combine(local, back1, (r, image0))
-    image1, sums = run(
+    field, halos, passed = combine(local, back1, (r, image0))
+    image1, sums, v = run(
         apply1_body,
-        each("s", flags) + each("v", field, *passed, *halos) + each("h", scalars),
-        each("c", FIELD) + each("v", sds((ZN, LANES))),
-        (LINE_FIELD,),
+        each("s", flags) + each("v", field, *passed, *halos),
+        each("c", FIELD) + each("v", sds((ZN, LANES))) + each("o", FIELD),
+        (LINE_FIELD, pltpu.SemaphoreType.DMA),
     )
     return run(
         final_body,

time: 136 us -> 133 us (0.978)
  Pallas kernels: 44.8 us -> 42.1 us
    pallas_call x10, Pallas kernels: 44.8 us -> 42.1 us  [run(): pl.pallas_call(kernel, out_shape=tuple((pltpu.HBM(a.shape, a.dtype) if m...]
where the time goes in v4:
time: 133 us
  Pallas kernels  42.1 us (32%)
  starting transfers between devices  41.1 us (31%)
  blocking collectives  34.7 us (26%)
  waiting for transfers between devices  13.6 us (10%)
    pallas_call x10, Pallas kernels, run(): pl.pallas_call(kernel, out_shape=tuple((pltpu.HBM(a.shape, a.dtype) if m...  42.1 us
    all_to_all x2, blocking collectives, swap(): return lax.all_to_all(x, AX, split_axis=0, concat_axis=0, tiled=True)  34.7 us
    all_to_all x3, starting transfers between devices, swap(): return lax.all_to_all(x, AX, split_axis=0, concat_axis=0, tiled=True)  21.9 us
    ppermute x18, starting transfers between devices, pair(): return [lax.ppermute(first, axis, even), lax.ppermute(second, axis, odd)]  19.3 us
    ppermute x18, waiting for transfers between devices, pair(): return [lax.ppermute(first, axis, even), lax.ppermute(second, axis, odd)]  7.8 us
    all_to_all x3, waiting for transfers between devices, swap(): return lax.all_to_all(x, AX, split_axis=0, concat_axis=0, tiled=True)  5.8 us
  transfers between devices with their start and end apart: 21, of which 9 were waited for; matrix products, arithmetic and copies ran while one was open for 0% of the time, Pallas kernels for 13%

profile of v4, /device:TPU:1, one launch (start us, length us, event | category | flops | bytes accessed | tf_op | source)
XLA Modules:
  0.0 132.6 jit_solution(5035925465865785621)
XLA Ops:
  0.7 0.1 stack.63.refs_0_
  0.8 3.8 %shard_map.86 = (bf16[1280,128]{1,0:T(8,128)(2,1)}, bf16[512,128]{1,0:T(8,128)(2,1)}, bf16[32,512]{1,0:T(8,128)(2,1)}, bf16[512,128]{1,0:T(8,128)(2,1)}, bf16[12...) custom-call(f32[9]{0:T(128)S(1)} %stack.63.refs_0_, ...), custom_call_target="tpu_custom_call" | custom-call | tf_op jit(solution)/shard_map/pallas_call | solution.py:149
  4.5 0.0 copy-start.4
  4.5 0.0 copy-start.1
  4.6 0.0 copy-start
  4.6 0.0 copy-start.3
  4.6 11.5 %all-to-all-start = ((bf16[128,5,2,128]{3,2,1,0:T(2,128)(2,1)}), bf16[128,5,2,128]{3,2,1,0:T(2,128)(2,1)S(1)}, u32[]{:S(2)}, u32[]{:S(2)}) async-start(bf16[128,5,2,128]{3,2,1,0:T(2,128)(2,1)} %bitcast.29), calls=%async_computation | async-start | bytes 655360 | tf_op jit(solution)/shard_map/all_to_all | solution.py:696
  16.1 0.0 copy-start.2
  16.1 0.0 copy-done.4
  16.1 1.1 collective-permute-start.2
  17.3 0.0 copy-done.1
  17.3 0.7 collective-permute-start
  17.9 0.0 copy-done
  17.9 1.8 %collective-permute-start.1 = (bf16[32,256]{1,0:T(8,128)(2,1)S(1)}, bf16[32,256]{1,0:T(8,128)(2,1)S(1)}, u32[]{:S(2)}, u32[]{:S(2)}) collective-permute-start(bf16[32,256]{1,0:T(8,128)(2,1)S(1)} %copy-done), channel_id=1, source_target_pairs={{0,3},{1,2},{2,1},{3,0},{4,7},{5,6},{6,5},{7,4},{8,11},{9,10},{10,... | collective-permute-start | bytes 49160 | tf_op jit(solution)/shard_map/ppermute | solution.py:246
  19.7 0.0 copy-done.3
  19.7 2.0 %collective-permute-start.3 = (bf16[16,256]{1,0:T(8,128)(2,1)S(1)}, bf16[16,256]{1,0:T(8,128)(2,1)S(1)}, u32[]{:S(2)}, u32[]{:S(2)}) collective-permute-start(bf16[16,256]{1,0:T(8,128)(2,1)S(1)} %copy-done.3), channel_id=1, source_target_pairs={{0,112},{16,32},{32,16},{48,64},{64,48},{80,96},{96,80},{112,0},{1... | collective-permute-start | bytes 24584 | tf_op jit(solution)/shard_map/ppermute | solution.py:246
  21.8 2.4 %collective-permute-start.5 = (bf16[8,512]{1,0:T(8,128)(2,1)S(1)}, bf16[8,512]{1,0:T(8,128)(2,1)S(1)}, u32[]{:S(2)}, u32[]{:S(2)}) collective-permute-start(bf16[8,512]{1,0:T(8,128)(2,1)S(1)} %copy-done.2), channel_id=1, source_target_pairs={{0,12},{4,8},{8,4},{12,0},{1,13},{5,9},{9,5},{13,1},{2,14},{6,10},... | collective-permute-start | bytes 24584 | tf_op jit(solution)/shard_map/ppermute | solution.py:246
  24.2 0.0 collective-permute-done.2.refs_3_
  24.2 0.0 collective-permute-start.4
  24.2 0.0 collective-permute-done.3.refs_4_
  24.2 1.6 %collective-permute-done.5.refs_6_ = bf16[8,512]{1,0:T(8,128)(2,1)S(1)} collective-permute-done((bf16[8,512]{1,0:T(8,128)(2,1)S(1)}, bf16[8,512]{1,0:T(8,128)(2,1)S(1)}, u32[]{:S(2)}, u32[]{:S(2)}) %collective-permute-start.5) | collective-permute-done | bytes 8224 | tf_op jit(solution)/shard_map/ppermute | solution.py:246
  25.8 1.2 collective-permute-done.4.refs_5_
  27.0 0.0 collective-permute-done.refs_1_
  27.0 0.0 collective-permute-done.1.refs_2_
  27.0 0.4 all-to-all-done
  27.5 2.2 %shard_map.87 = (bf16[1280,128]{1,0:T(8,128)(2,1)}, bf16[1280,128]{1,0:T(8,128)(2,1)}) custom-call(bf16[1280,128]{1,0:T(8,128)(2,1)S(1)} %bitcast.25, bf16[1,256,256]{2,1,0:T(8,128)(2,1)} %refs_0_.1), custom_call_target="tpu_custom_call" | custom-call | tf_op jit(solution)/shard_map/pallas_call | solution.py:149
  29.7 5.7 %all-to-all-start.1 = ((bf16[128,5,2,128]{3,2,1,0:T(2,128)(2,1)}), bf16[128,5,2,128]{3,2,1,0:T(2,128)(2,1)S(1)}, u32[]{:S(2)}, u32[]{:S(2)}) async-start(bf16[128,5,2,128]{3,2,1,0:T(2,128)(2,1)} %bitcast.30), calls=%async_computation.1 | async-start | bytes 655360 | tf_op jit(solution)/shard_map/all_to_all | solution.py:696
  35.4 9.5 %shard_map.88 = (f32[16,32,256]{2,1,0:T(8,128)}, f32[16,32,256]{2,1,0:T(8,128)}, f32[16,32,256]{2,1,0:T(8,128)}, f32[16,32,256]{2,1,0:T(8,128)}, f32[16,32,256]{...) custom-call(f32[9]{0:T(128)S(1)} %stack.63.refs_0_, ...), custom_call_target="tpu_custom_call" | custom-call | tf_op jit(solution)/shard_map/pallas_call | solution.py:149
  44.9 2.0 %all-to-all-done.1 = bf16[128,5,2,128]{3,2,1,0:T(2,128)(2,1)S(1)} async-done(((bf16[128,5,2,128]{3,2,1,0:T(2,128)(2,1)}), bf16[128,5,2,128]{3,2,1,0:T(2,128)(2,1)S(1)}, u32[]{:S(2)}, u32[]{:S(2)}) %all-to-all-start.1) | async-done | bytes 327712 | tf_op jit(solution)/shard_map/all_to_all | solution.py:696
  46.9 3.8 %shard_map.89 = (f32[16,32,256]{2,1,0:T(8,128)S(1)}, bf16[32,256]{1,0:T(8,128)(2,1)S(1)}, bf16[32,256]{1,0:T(8,128)(2,1)S(1)}, bf16[16,256]{1,0:T(8,128)(2,1)S(1...) custom-call(f32[9]{0:T(128)S(1)} %stack.63.refs_0_, ...), custom_call_target="tpu_custom_call" | custom-call | tf_op jit(solution)/shard_map/pallas_call | solution.py:149
  50.7 1.4 %collective-permute-start.8 = (bf16[16,256]{1,0:T(8,128)(2,1)S(1)}, bf16[16,256]{1,0:T(8,128)(2,1)S(1)}, u32[]{:S(2)}, u32[]{:S(2)}) collective-permute-start(bf16[16,256]{1,0:T(8,128)(2,1)S(1)} %get-tuple-element.98), channel_id=1, source_target_pairs={{0,16},{16,0},{32,48},{48,32},{64,80},{80,64},{96,112},{112,96},{1... | collective-permute-start | bytes 24584 | tf_op jit(solution)/shard_map/ppermute | solution.py:246
  52.1 0.4 collective-permute-start.6
  52.5 0.1 collective-permute-start.7
  52.5 2.1 %collective-permute-start.9 = (bf16[16,256]{1,0:T(8,128)(2,1)S(1)}, bf16[16,256]{1,0:T(8,128)(2,1)S(1)}, u32[]{:S(2)}, u32[]{:S(2)}) collective-permute-start(bf16[16,256]{1,0:T(8,128)(2,1)S(1)} %get-tuple-element.99), channel_id=1, source_target_pairs={{0,112},{16,32},{32,16},{48,64},{64,48},{80,96},{96,80},{112,0},{1... | collective-permute-start | bytes 24584 | tf_op jit(solution)/shard_map/ppermute | solution.py:246
  54.6 2.4 %collective-permute-start.11 = (bf16[8,512]{1,0:T(8,128)(2,1)S(1)}, bf16[8,512]{1,0:T(8,128)(2,1)S(1)}, u32[]{:S(2)}, u32[]{:S(2)}) collective-permute-start(bf16[8,512]{1,0:T(8,128)(2,1)S(1)} %get-tuple-element.100), channel_id=1, source_target_pairs={{0,12},{4,8},{8,4},{12,0},{1,13},{5,9},{9,5},{13,1},{2,14},{6,10},... | collective-permute-start | bytes 24584 | tf_op jit(solution)/shard_map/ppermute | solution.py:246
  57.0 0.0 collective-permute-done.8.refs_11_
  57.1 0.0 collective-permute-start.10
  57.1 0.0 collective-permute-done.9.refs_12_
  57.1 1.3 collective-permute-done.11.refs_14_
  58.3 1.2 collective-permute-done.10.refs_13_
  59.6 0.0 collective-permute-done.6.refs_9_
  59.6 0.0 collective-permute-done.7.refs_10_
  59.6 3.4 %shard_map.90 = (f32[16,32,256]{2,1,0:T(8,128)}, bf16[1280,128]{1,0:T(8,128)(2,1)}, f32[16,32,256]{2,1,0:T(8,128)}) custom-call(f32[9]{0:T(128)S(1)} %stack.63.refs_0_, f32[16,32,256]{2,1,0:T(8,128)S(1)} %get-tuple-element.88.refs_1_, f32[16,32,256]{2,1,0:T(8,128)S(1)} %get-tuple-element.89.refs_2_, f32[16,32,256]{2,1,0:T(8,128)S(1)} %get-tuple-element.90.refs_3_, ...), custom_call_target="tpu_custom_call" | custom-call | tf_op jit(solution)/shard_map/pallas_call | solution.py:149
  62.9 18.1 %all_to_all.31 = bf16[128,5,2,128]{3,2,1,0:T(2,128)(2,1)S(1)} all-to-all(bf16[128,5,2,128]{3,2,1,0:T(2,128)(2,1)} %bitcast.31), channel_id=1, replica_groups=mesh['gx'=8,'gy'=4,'gz'=4] {'gx','gy','gz'}, dimensions={0} | all-to-all | bytes 655360 | tf_op jit(solution)/shard_map/all_to_all | solution.py:696
  81.0 2.3 %shard_map.91 = (bf16[1280,128]{1,0:T(8,128)(2,1)}, f32[8,128]{1,0:T(8,128)}) custom-call(bf16[1,256,256]{2,1,0:T(8,128)(2,1)} %refs_0_.1, bf16[1280,128]{1,0:T(8,128)(2,1)} %get-tuple-element.71.refs_1_, bf16[1280,128]{1,0:T(8,128)(2,1)S(1)} %bitcast.26), custom_call_target="tpu_custom_call" | custom-call | tf_op jit(solution)/shard_map/pallas_call | solution.py:149
  83.4 4.7 %all-to-all-start.3 = ((bf16[128,5,2,128]{3,2,1,0:T(2,128)(2,1)}), bf16[128,5,2,128]{3,2,1,0:T(2,128)(2,1)S(1)}, u32[]{:S(2)}, u32[]{:S(2)}) async-start(bf16[128,5,2,128]{3,2,1,0:T(2,128)(2,1)} %bitcast.32), calls=%async_computation.3 | async-start | bytes 655360 | tf_op jit(solution)/shard_map/all_to_all | solution.py:696
  88.1 8.1 %shard_map.92.refs_5_ = f32[16,32,256]{2,1,0:T(8,128)} custom-call(f32[8,128]{1,0:T(8,128)} %get-tuple-element.104.refs_0_, f32[16,32,256]{2,1,0:T(8,128)} %refs_4_.7, f32[16,32,256]{2,1,0:T(8,128)} %get-tuple-element.106.refs_2_.refs_13_.refs_5_, f32[16,32,256]{2,1,0:T(8,128)} %get-tuple-element.107.refs_3_, ...), custom_call_target="tpu_custom_call" | custom-call | tf_op jit(solution)/shard_map/pallas_call | solution.py:149
  96.2 3.4 %all-to-all-done.3 = bf16[128,5,2,128]{3,2,1,0:T(2,128)(2,1)S(1)} async-done(((bf16[128,5,2,128]{3,2,1,0:T(2,128)(2,1)}), bf16[128,5,2,128]{3,2,1,0:T(2,128)(2,1)S(1)}, u32[]{:S(2)}, u32[]{:S(2)}) %all-to-all-start.3) | async-done | bytes 327712 | tf_op jit(solution)/shard_map/all_to_all | solution.py:696
  99.6 3.9 %shard_map.93 = (f32[16,32,256]{2,1,0:T(8,128)S(1)}, bf16[32,256]{1,0:T(8,128)(2,1)S(1)}, bf16[32,256]{1,0:T(8,128)(2,1)S(1)}, bf16[16,256]{1,0:T(8,128)(2,1)S(1...) custom-call(f32[9]{0:T(128)S(1)} %stack.63.refs_0_, ...), custom_call_target="tpu_custom_call" | custom-call | tf_op jit(solution)/shard_map/pallas_call | solution.py:149
  103.5 1.4 %collective-permute-start.14 = (bf16[16,256]{1,0:T(8,128)(2,1)S(1)}, bf16[16,256]{1,0:T(8,128)(2,1)S(1)}, u32[]{:S(2)}, u32[]{:S(2)}) collective-permute-start(bf16[16,256]{1,0:T(8,128)(2,1)S(1)} %get-tuple-element.119), channel_id=1, source_target_pairs={{0,16},{16,0},{32,48},{48,32},{64,80},{80,64},{96,112},{112,96},{1... | collective-permute-start | bytes 24584 | tf_op jit(solution)/shard_map/ppermute | solution.py:246
  104.9 0.4 collective-permute-start.12
  105.3 0.0 collective-permute-start.13
  105.3 1.2 collective-permute-start.15
  106.5 1.9 %collective-permute-start.17 = (bf16[8,512]{1,0:T(8,128)(2,1)S(1)}, bf16[8,512]{1,0:T(8,128)(2,1)S(1)}, u32[]{:S(2)}, u32[]{:S(2)}) collective-permute-start(bf16[8,512]{1,0:T(8,128)(2,1)S(1)} %get-tuple-element.121), channel_id=1, source_target_pairs={{0,12},{4,8},{8,4},{12,0},{1,13},{5,9},{9,5},{13,1},{2,14},{6,10},... | collective-permute-start | bytes 24584 | tf_op jit(solution)/shard_map/ppermute | solution.py:246
  108.4 0.0 collective-permute-done.14.refs_12_
  108.4 0.0 collective-permute-start.16
  108.4 0.0 collective-permute-done.15.refs_13_
  108.4 1.8 %collective-permute-done.17.refs_15_ = bf16[8,512]{1,0:T(8,128)(2,1)S(1)} collective-permute-done((bf16[8,512]{1,0:T(8,128)(2,1)S(1)}, bf16[8,512]{1,0:T(8,128)(2,1)S(1)}, u32[]{:S(2)}, u32[]{:S(2)}) %collective-permute-start.17) | collective-permute-done | bytes 8224 | tf_op jit(solution)/shard_map/ppermute | solution.py:246
  110.2 0.7 collective-permute-done.16.refs_14_
  110.9 0.0 collective-permute-done.12.refs_10_
  110.9 0.0 collective-permute-done.13.refs_11_
  110.9 2.1 %shard_map.94 = (f32[16,32,256]{2,1,0:T(8,128)}, f32[128,128]{1,0:T(8,128)S(1)}, f32[16,32,256]{2,1,0:T(8,128)}) custom-call(f32[9]{0:T(128)S(1)} %stack.63.refs_0_, f32[16,32,256]{2,1,0:T(8,128)S(1)} %get-tuple-element.108.refs_1_, f32[16,32,256]{2,1,0:T(8,128)S(1)} %get-tuple-element.109.refs_2_, f32[16,32,256]{2,1,0:T(8,128)S(1)} %get-tuple-element.110.refs_3_, ...), custom_call_target="tpu_custom_call" | custom-call | tf_op jit(solution)/shard_map/pallas_call | solution.py:149
  113.0 16.6 %all_to_all.32 = f32[128,1,128]{2,1,0:T(1,128)S(1)} all-to-all(f32[128,1,128]{2,1,0:T(1,128)S(1)} %bitcast.28), channel_id=1, replica_groups=mesh['gx'=8,'gy'=4,'gz'=4] {'gx','gy','gz'}, dimensions={0} | all-to-all | bytes 131072 | tf_op jit(solution)/shard_map/all_to_all | solution.py:696
  129.6 2.9 %shard_map.95 = (f32[16,32,256]{2,1,0:T(8,128)}, f32[16,32,256]{2,1,0:T(8,128)}) custom-call(f32[8,128]{1,0:T(8,128)} %get-tuple-element.104.refs_0_, f32[128,128]{1,0:T(8,128)S(1)} %bitcast.27, f32[16,32,256]{2,1,0:T(8,128)} %get-tuple-element.123.refs_2_, f32[16,32,256]{2,1,0:T(8,128)} %get-tuple-element.124.refs_3_, f32[16,32,256]{2,1,0:T(8,128)} %refs_4_.7, ...), custom_call_target="tpu_custom_call" | custom-call | tf_op jit(solution)/shard_map/pallas_call | solution.py:149
  (1 shorter events, 0.0 us)
Async XLA Ops:
  4.5 11.6 %copy-start.4 = (bf16[16,256]{1,0:T(8,128)(2,1)S(1)}, bf16[16,256]{1,0:T(8,128)(2,1)}, u32[]{:S(2)}) copy-start(bf16[16,256]{1,0:T(8,128)(2,1)} %get-tuple-element.67) | copy-start | bytes 24580
  4.5 12.7 %copy-start.1 = (bf16[32,256]{1,0:T(8,128)(2,1)S(1)}, bf16[32,256]{1,0:T(8,128)(2,1)}, u32[]{:S(2)}) copy-start(bf16[32,256]{1,0:T(8,128)(2,1)} %get-tuple-element.65) | copy-start | bytes 49156
  4.6 13.4 %copy-start = (bf16[32,256]{1,0:T(8,128)(2,1)S(1)}, bf16[32,256]{1,0:T(8,128)(2,1)}, u32[]{:S(2)}) copy-start(bf16[32,256]{1,0:T(8,128)(2,1)} %get-tuple-element.66) | copy-start | bytes 49156
  4.6 15.2 %copy-start.3 = (bf16[16,256]{1,0:T(8,128)(2,1)S(1)}, bf16[16,256]{1,0:T(8,128)(2,1)}, u32[]{:S(2)}) copy-start(bf16[16,256]{1,0:T(8,128)(2,1)} %get-tuple-element.68) | copy-start | bytes 24580
  4.6 22.9 %all-to-all-start = ((bf16[128,5,2,128]{3,2,1,0:T(2,128)(2,1)}), bf16[128,5,2,128]{3,2,1,0:T(2,128)(2,1)S(1)}, u32[]{:S(2)}, u32[]{:S(2)}) async-start(bf16[128,5,2,128]{3,2,1,0:T(2,128)(2,1)} %bitcast.29), calls=%async_computation | async-start | bytes 655360 | tf_op jit(solution)/shard_map/all_to_all | solution.py:696
  16.1 5.7 %copy-start.2 = (bf16[8,512]{1,0:T(8,128)(2,1)S(1)}, bf16[8,512]{1,0:T(8,128)(2,1)}, u32[]{:S(2)}) copy-start(bf16[8,512]{1,0:T(8,128)(2,1)} %get-tuple-element.69) | copy-start | bytes 24580
  16.1 8.1 %collective-permute-start.2 = (bf16[16,256]{1,0:T(8,128)(2,1)S(1)}, bf16[16,256]{1,0:T(8,128)(2,1)S(1)}, u32[]{:S(2)}, u32[]{:S(2)}) collective-permute-start(bf16[16,256]{1,0:T(8,128)(2,1)S(1)} %copy-done.4), channel_id=1, source_target_pairs={{0,16},{16,0},{32,48},{48,32},{64,80},{80,64},{96,112},{112,96},{1... | collective-permute-start | bytes 24584 | tf_op jit(solution)/shard_map/ppermute | solution.py:246
  17.3 9.8 %collective-permute-start = (bf16[32,256]{1,0:T(8,128)(2,1)S(1)}, bf16[32,256]{1,0:T(8,128)(2,1)S(1)}, u32[]{:S(2)}, u32[]{:S(2)}) collective-permute-start(bf16[32,256]{1,0:T(8,128)(2,1)S(1)} %copy-done.1), channel_id=1, source_target_pairs={{0,1},{1,0},{2,3},{3,2},{4,5},{5,4},{6,7},{7,6},{8,9},{9,8},{10,11... | collective-permute-start | bytes 49160 | tf_op jit(solution)/shard_map/ppermute | solution.py:246
  17.9 9.1 %collective-permute-start.1 = (bf16[32,256]{1,0:T(8,128)(2,1)S(1)}, bf16[32,256]{1,0:T(8,128)(2,1)S(1)}, u32[]{:S(2)}, u32[]{:S(2)}) collective-permute-start(bf16[32,256]{1,0:T(8,128)(2,1)S(1)} %copy-done), channel_id=1, source_target_pairs={{0,3},{1,2},{2,1},{3,0},{4,7},{5,6},{6,5},{7,4},{8,11},{9,10},{10,... | collective-permute-start | bytes 49160 | tf_op jit(solution)/shard_map/ppermute | solution.py:246
  19.7 4.5 %collective-permute-start.3 = (bf16[16,256]{1,0:T(8,128)(2,1)S(1)}, bf16[16,256]{1,0:T(8,128)(2,1)S(1)}, u32[]{:S(2)}, u32[]{:S(2)}) collective-permute-start(bf16[16,256]{1,0:T(8,128)(2,1)S(1)} %copy-done.3), channel_id=1, source_target_pairs={{0,112},{16,32},{32,16},{48,64},{64,48},{80,96},{96,80},{112,0},{1... | collective-permute-start | bytes 24584 | tf_op jit(solution)/shard_map/ppermute | solution.py:246
  21.8 4.0 %collective-permute-start.5 = (bf16[8,512]{1,0:T(8,128)(2,1)S(1)}, bf16[8,512]{1,0:T(8,128)(2,1)S(1)}, u32[]{:S(2)}, u32[]{:S(2)}) collective-permute-start(bf16[8,512]{1,0:T(8,128)(2,1)S(1)} %copy-done.2), channel_id=1, source_target_pairs={{0,12},{4,8},{8,4},{12,0},{1,13},{5,9},{9,5},{13,1},{2,14},{6,10},... | collective-permute-start | bytes 24584 | tf_op jit(solution)/shard_map/ppermute | solution.py:246
  24.2 2.8 %collective-permute-start.4 = (bf16[8,512]{1,0:T(8,128)(2,1)S(1)}, bf16[8,512]{1,0:T(8,128)(2,1)S(1)}, u32[]{:S(2)}, u32[]{:S(2)}) collective-permute-start(bf16[8,512]{1,0:T(8,128)(2,1)S(1)} %copy-done.2), channel_id=1, source_target_pairs={{0,4},{4,0},{8,12},{12,8},{1,5},{5,1},{9,13},{13,9},{2,6},{6,2},{1... | collective-permute-start | bytes 24584 | tf_op jit(solution)/shard_map/ppermute | solution.py:246
  29.7 17.2 %all-to-all-start.1 = ((bf16[128,5,2,128]{3,2,1,0:T(2,128)(2,1)}), bf16[128,5,2,128]{3,2,1,0:T(2,128)(2,1)S(1)}, u32[]{:S(2)}, u32[]{:S(2)}) async-start(bf16[128,5,2,128]{3,2,1,0:T(2,128)(2,1)} %bitcast.30), calls=%async_computation.1 | async-start | bytes 655360 | tf_op jit(solution)/shard_map/all_to_all | solution.py:696
  50.7 6.3 %collective-permute-start.8 = (bf16[16,256]{1,0:T(8,128)(2,1)S(1)}, bf16[16,256]{1,0:T(8,128)(2,1)S(1)}, u32[]{:S(2)}, u32[]{:S(2)}) collective-permute-start(bf16[16,256]{1,0:T(8,128)(2,1)S(1)} %get-tuple-element.98), channel_id=1, source_target_pairs={{0,16},{16,0},{32,48},{48,32},{64,80},{80,64},{96,112},{112,96},{1... | collective-permute-start | bytes 24584 | tf_op jit(solution)/shard_map/ppermute | solution.py:246
  52.1 7.5 %collective-permute-start.6 = (bf16[32,256]{1,0:T(8,128)(2,1)S(1)}, bf16[32,256]{1,0:T(8,128)(2,1)S(1)}, u32[]{:S(2)}, u32[]{:S(2)}) collective-permute-start(bf16[32,256]{1,0:T(8,128)(2,1)S(1)} %get-tuple-element.96), channel_id=1, source_target_pairs={{0,1},{1,0},{2,3},{3,2},{4,5},{5,4},{6,7},{7,6},{8,9},{9,8},{10,11... | collective-permute-start | bytes 49160 | tf_op jit(solution)/shard_map/ppermute | solution.py:246
  52.5 7.1 %collective-permute-start.7 = (bf16[32,256]{1,0:T(8,128)(2,1)S(1)}, bf16[32,256]{1,0:T(8,128)(2,1)S(1)}, u32[]{:S(2)}, u32[]{:S(2)}) collective-permute-start(bf16[32,256]{1,0:T(8,128)(2,1)S(1)} %get-tuple-element.97), channel_id=1, source_target_pairs={{0,3},{1,2},{2,1},{3,0},{4,7},{5,6},{6,5},{7,4},{8,11},{9,10},{10,... | collective-permute-start | bytes 49160 | tf_op jit(solution)/shard_map/ppermute | solution.py:246
  52.5 4.5 %collective-permute-start.9 = (bf16[16,256]{1,0:T(8,128)(2,1)S(1)}, bf16[16,256]{1,0:T(8,128)(2,1)S(1)}, u32[]{:S(2)}, u32[]{:S(2)}) collective-permute-start(bf16[16,256]{1,0:T(8,128)(2,1)S(1)} %get-tuple-element.99), channel_id=1, source_target_pairs={{0,112},{16,32},{32,16},{48,64},{64,48},{80,96},{96,80},{112,0},{1... | collective-permute-start | bytes 24584 | tf_op jit(solution)/shard_map/ppermute | solution.py:246
  54.6 3.7 %collective-permute-start.11 = (bf16[8,512]{1,0:T(8,128)(2,1)S(1)}, bf16[8,512]{1,0:T(8,128)(2,1)S(1)}, u32[]{:S(2)}, u32[]{:S(2)}) collective-permute-start(bf16[8,512]{1,0:T(8,128)(2,1)S(1)} %get-tuple-element.100), channel_id=1, source_target_pairs={{0,12},{4,8},{8,4},{12,0},{1,13},{5,9},{9,5},{13,1},{2,14},{6,10},... | collective-permute-start | bytes 24584 | tf_op jit(solution)/shard_map/ppermute | solution.py:246
  57.1 2.5 %collective-permute-start.10 = (bf16[8,512]{1,0:T(8,128)(2,1)S(1)}, bf16[8,512]{1,0:T(8,128)(2,1)S(1)}, u32[]{:S(2)}, u32[]{:S(2)}) collective-permute-start(bf16[8,512]{1,0:T(8,128)(2,1)S(1)} %get-tuple-element.100), channel_id=1, source_target_pairs={{0,4},{4,0},{8,12},{12,8},{1,5},{5,1},{9,13},{13,9},{2,6},{6,2},{1... | collective-permute-start | bytes 24584 | tf_op jit(solution)/shard_map/ppermute | solution.py:246
  83.4 16.2 %all-to-all-start.3 = ((bf16[128,5,2,128]{3,2,1,0:T(2,128)(2,1)}), bf16[128,5,2,128]{3,2,1,0:T(2,128)(2,1)S(1)}, u32[]{:S(2)}, u32[]{:S(2)}) async-start(bf16[128,5,2,128]{3,2,1,0:T(2,128)(2,1)} %bitcast.32), calls=%async_computation.3 | async-start | bytes 655360 | tf_op jit(solution)/shard_map/all_to_all | solution.py:696
  103.5 4.8 %collective-permute-start.14 = (bf16[16,256]{1,0:T(8,128)(2,1)S(1)}, bf16[16,256]{1,0:T(8,128)(2,1)S(1)}, u32[]{:S(2)}, u32[]{:S(2)}) collective-permute-start(bf16[16,256]{1,0:T(8,128)(2,1)S(1)} %get-tuple-element.119), channel_id=1, source_target_pairs={{0,16},{16,0},{32,48},{48,32},{64,80},{80,64},{96,112},{112,96},{1... | collective-permute-start | bytes 24584 | tf_op jit(solution)/shard_map/ppermute | solution.py:246
  104.9 6.0 %collective-permute-start.12 = (bf16[32,256]{1,0:T(8,128)(2,1)S(1)}, bf16[32,256]{1,0:T(8,128)(2,1)S(1)}, u32[]{:S(2)}, u32[]{:S(2)}) collective-permute-start(bf16[32,256]{1,0:T(8,128)(2,1)S(1)} %get-tuple-element.117), channel_id=1, source_target_pairs={{0,1},{1,0},{2,3},{3,2},{4,5},{5,4},{6,7},{7,6},{8,9},{9,8},{10,11... | collective-permute-start | bytes 49160 | tf_op jit(solution)/shard_map/ppermute | solution.py:246
  105.3 5.6 %collective-permute-start.13 = (bf16[32,256]{1,0:T(8,128)(2,1)S(1)}, bf16[32,256]{1,0:T(8,128)(2,1)S(1)}, u32[]{:S(2)}, u32[]{:S(2)}) collective-permute-start(bf16[32,256]{1,0:T(8,128)(2,1)S(1)} %get-tuple-element.118), channel_id=1, source_target_pairs={{0,3},{1,2},{2,1},{3,0},{4,7},{5,6},{6,5},{7,4},{8,11},{9,10},{10,... | collective-permute-start | bytes 49160 | tf_op jit(solution)/shard_map/ppermute | solution.py:246
  105.3 3.1 %collective-permute-start.15 = (bf16[16,256]{1,0:T(8,128)(2,1)S(1)}, bf16[16,256]{1,0:T(8,128)(2,1)S(1)}, u32[]{:S(2)}, u32[]{:S(2)}) collective-permute-start(bf16[16,256]{1,0:T(8,128)(2,1)S(1)} %get-tuple-element.120), channel_id=1, source_target_pairs={{0,112},{16,32},{32,16},{48,64},{64,48},{80,96},{96,80},{112,0},{1... | collective-permute-start | bytes 24584 | tf_op jit(solution)/shard_map/ppermute | solution.py:246
  106.5 3.7 %collective-permute-start.17 = (bf16[8,512]{1,0:T(8,128)(2,1)S(1)}, bf16[8,512]{1,0:T(8,128)(2,1)S(1)}, u32[]{:S(2)}, u32[]{:S(2)}) collective-permute-start(bf16[8,512]{1,0:T(8,128)(2,1)S(1)} %get-tuple-element.121), channel_id=1, source_target_pairs={{0,12},{4,8},{8,4},{12,0},{1,13},{5,9},{9,5},{13,1},{2,14},{6,10},... | collective-permute-start | bytes 24584 | tf_op jit(solution)/shard_map/ppermute | solution.py:246
  108.4 2.5 %collective-permute-start.16 = (bf16[8,512]{1,0:T(8,128)(2,1)S(1)}, bf16[8,512]{1,0:T(8,128)(2,1)S(1)}, u32[]{:S(2)}, u32[]{:S(2)}) collective-permute-start(bf16[8,512]{1,0:T(8,128)(2,1)S(1)} %get-tuple-element.121), channel_id=1, source_target_pairs={{0,4},{4,0},{8,12},{12,8},{1,5},{5,1},{9,13},{13,9},{2,6},{6,2},{1... | collective-permute-start | bytes 24584 | tf_op jit(solution)/shard_map/ppermute | solution.py:246

commit v5 on v4

--- a/solution.py
+++ b/solution.py
@@ -85,13 +85,14 @@
             copy.wait()
 
 
-SPACE = {"a": pl.ANY, "o": pltpu.HBM, "s": pltpu.SMEM, "v": pltpu.VMEM, "h": pltpu.HBM, "c": pltpu.HBM, "p": pltpu.HBM}
-COPIED = "hcpa"
-CHUNKS = 4
+SPACE = {"a": pl.ANY, "o": pltpu.HBM, "s": pltpu.SMEM, "v": pltpu.VMEM, "h": pltpu.HBM, "c": pltpu.HBM, "p": pltpu.HBM, "w": pltpu.HBM}
+COPIED = "hcpaw"
+CHUNKS = 2
+WRITES = 2
 
 
 def chunks_of(mode, array):
-    return CHUNKS if mode in "cp" and array.shape[0] > 8 else 1
+    return {"c": CHUNKS, "w": WRITES}.get(mode, 1)
 
 
 def spec(mode):
@@ -149,7 +150,7 @@
     return pl.pallas_call(
         kernel,
         out_shape=tuple(
-            pltpu.HBM(a.shape, a.dtype) if m in "hco" else a for m, a in outs
+            pltpu.HBM(a.shape, a.dtype) if m in "hcow" else a for m, a in outs
         )
         + tuple(passed),
         in_specs=[spec(m) for m, _ in ins],
@@ -370,8 +371,8 @@
     u = jnp.where(lane < 32, tail + pltpu.roll(tail, LANES - 32, 1), 0.0)
     high = u.astype(BF16).astype(F32)
     both = high + pltpu.roll(u - high, 32, 1)
-    size = ZN // CHUNKS
-    for i in range(CHUNKS):
+    size = ZN // WRITES
+    for i in range(WRITES):
         at = i * size
         x = jnp.concatenate(
             [
@@ -470,8 +471,9 @@
             ee = ee + fold(image * image)
             below, now = now, above
         rho, pe, ee = total(rho), total(pe), total(ee)
-        a = rho / pe
-        return a, a * a * ee / rho - 1.0
+        inverse = 1.0 / pe
+        a = rho * inverse
+        return a, a * ee * inverse - 1.0
 
     def begin(z):
         value = first(z)
@@ -563,7 +565,7 @@
 
 
 def combine_body(ins, outs, xs_lo, xs_hi, wide, lines):
-    flags, got, hits, take, factor, local, *_ = ins
+    flags, got, factor, hits, take, local, *_ = ins
     out, *faces = outs
     wide[...] = got[...].astype(F32)
     factor = full(factor)
@@ -717,7 +719,7 @@
     )
     send0, hits, flipped, put, take, *k_faces = run(
         pack_body,
-        each("s", flags) + each("h", label, zrow) + each("c", r) + each("h", factor) + each("c", k),
+        each("s", flags) + each("h", label, zrow, r, factor, k),
         each("h", PACKED, HITS, FLIPPED, PUT, TAKE, *FACE_OUTS),
         (TILE, ROWS, WIDE) + FACE_SCRATCH + (FLAT, FLAT),
     )
@@ -727,14 +729,14 @@
     back0, got0 = run(
         lift0_body,
         each("v", got0) + each("h", zone_factor),
-        each("c", PACKED) + each("o", PACKED),
+        each("w", PACKED) + each("o", PACKED),
         (WIDE, pltpu.SemaphoreType.DMA),
     )
     back0 = swap_packed(back0)
     local, s, sinv, cz, cx, cy, *bounds = run(
         solve0_body,
         each("s", flags) + each("a", *k_halos) + each("c", k, storage, r),
-        each("c", *(FIELD,) * 6) + each("h", sds((96, CY)), sds((8, LINES))),
+        each("w", FIELD) + each("h", *(FIELD,) * 5, sds((96, CY)), sds((8, LINES))),
         (FIELD_SCRATCH,) * 4 + (LINE_FIELD,),
         ((7, 8, 9),),
     )
@@ -745,7 +747,7 @@
             combine_body,
             each("s", flags)
             + each("v", back)
-            + each("h", hits, take, factor)
+            + each("h", factor, hits, take)
             + each("c", local)
             + each("p", *matrix, *more),
             each("v", FIELD, *FACE_OUTS),
@@ -757,21 +759,21 @@
     image0, send1, d = run(
         apply0_body,
         each("s", flags) + each("v", field, *passed, *halos) + each("h", flipped, put, factor),
-        each("c", FIELD) + each("h", PACKED) + each("o", FIELD),
+        each("h", FIELD, PACKED) + each("o", FIELD),
         (TILE, ROWS, WIDE, LINE_FIELD, FLAT, FLAT, pltpu.SemaphoreType.DMA),
     )
     got1 = swap_packed(send1)
     back1, scalars = run(
         lift1_body,
         each("h", zone_factor, got0) + each("v", got1),
-        each("c", PACKED) + each("h", sds((8, LANES))),
+        each("w", PACKED) + each("h", sds((8, LANES))),
         (WIDE,),
     )
     back1 = swap_packed(back1)
     (local,) = run(
         solve1_body,
         each("h", scalars) + each("c", r, image0, s, cz, cx, cy),
-        each("c", FIELD),
+        each("w", FIELD),
         (FIELD_SCRATCH,) * 4,
         ((1, 2, 3), (4, 5, 6)),
     )
@@ -779,13 +781,13 @@
     image1, sums, v = run(
         apply1_body,
         each("s", flags) + each("v", field, *passed, *halos),
-        each("c", FIELD) + each("v", sds((ZN, LANES))) + each("o", FIELD),
+        each("w", FIELD) + each("v", sds((ZN, LANES))) + each("o", FIELD),
         (LINE_FIELD, pltpu.SemaphoreType.DMA),
     )
     return run(
         final_body,
         each("h", scalars) + each("v", swap(sums)) + each("c", d, v, r, image0, image1),
-        each("c", FIELD, FIELD),
+        each("w", FIELD, FIELD),
         (),
         ((2, 3, 4, 5, 6),),
     )

time: 133 us -> 129 us (0.970)
  Pallas kernels: 42.1 us -> 37.9 us
    pallas_call x10, Pallas kernels: 42.1 us -> 37.9 us  [run(): pl.pallas_call(kernel, out_shape=tuple((pltpu.HBM(a.shape, a.dtype) if m...]
  transfers between devices with their start and end apart: 21 -> 21, of which waited for: 9 -> 10; matrix products, arithmetic and copies ran while one was open for 0% -> 0% of each run, Pallas kernels for 13% -> 13%
where the time goes in v5:
time: 129 us
  starting transfers between devices  40 us (31%)
  Pallas kernels  37.9 us (29%)
  blocking collectives  35.1 us (27%)
  waiting for transfers between devices  14.7 us (11%)
    pallas_call x10, Pallas kernels, run(): pl.pallas_call(kernel, out_shape=tuple((pltpu.HBM(a.shape, a.dtype) if m...  37.9 us
    all_to_all x2, blocking collectives, swap(): return lax.all_to_all(x, AX, split_axis=0, concat_axis=0, tiled=True)  35.1 us
    all_to_all x3, starting transfers between devices, swap(): return lax.all_to_all(x, AX, split_axis=0, concat_axis=0, tiled=True)  21.9 us
    ppermute x18, starting transfers between devices, pair(): return [lax.ppermute(first, axis, even), lax.ppermute(second, axis, odd)]  18.1 us
    ppermute x18, waiting for transfers between devices, pair(): return [lax.ppermute(first, axis, even), lax.ppermute(second, axis, odd)]  7.81 us
    all_to_all x3, waiting for transfers between devices, swap(): return lax.all_to_all(x, AX, split_axis=0, concat_axis=0, tiled=True)  6.9 us
  transfers between devices with their start and end apart: 21, of which 10 were waited for; matrix products, arithmetic and copies ran while one was open for 0% of the time, Pallas kernels for 13%

profile of v5, /device:TPU:1, one launch (start us, length us, event | category | flops | bytes accessed | tf_op | source)
XLA Modules:
  0.0 128.8 jit_solution(11794010026295975745)
XLA Ops:
  0.7 0.1 stack.63.refs_0_
  0.8 3.3 %shard_map.86 = (bf16[1280,128]{1,0:T(8,128)(2,1)}, bf16[512,128]{1,0:T(8,128)(2,1)}, bf16[32,512]{1,0:T(8,128)(2,1)}, bf16[512,128]{1,0:T(8,128)(2,1)}, bf16[12...) custom-call(f32[9]{0:T(128)S(1)} %stack.63.refs_0_, ...), custom_call_target="tpu_custom_call" | custom-call | tf_op jit(solution)/shard_map/pallas_call | solution.py:150
  4.1 0.0 copy-start.4
  4.1 0.0 copy-start.1
  4.1 0.0 copy-start
  4.1 0.0 copy-start.3
  4.1 11.5 %all-to-all-start = ((bf16[128,5,2,128]{3,2,1,0:T(2,128)(2,1)}), bf16[128,5,2,128]{3,2,1,0:T(2,128)(2,1)S(1)}, u32[]{:S(2)}, u32[]{:S(2)}) async-start(bf16[128,5,2,128]{3,2,1,0:T(2,128)(2,1)} %bitcast.29), calls=%async_computation | async-start | bytes 655360 | tf_op jit(solution)/shard_map/all_to_all | solution.py:698
  15.6 0.0 copy-start.2
  15.6 0.0 copy-done.4
  15.7 1.1 collective-permute-start.2
  16.8 0.0 copy-done.1
  16.8 0.7 collective-permute-start
  17.5 0.0 copy-done
  17.5 1.8 %collective-permute-start.1 = (bf16[32,256]{1,0:T(8,128)(2,1)S(1)}, bf16[32,256]{1,0:T(8,128)(2,1)S(1)}, u32[]{:S(2)}, u32[]{:S(2)}) collective-permute-start(bf16[32,256]{1,0:T(8,128)(2,1)S(1)} %copy-done), channel_id=1, source_target_pairs={{0,3},{1,2},{2,1},{3,0},{4,7},{5,6},{6,5},{7,4},{8,11},{9,10},{10,... | collective-permute-start | bytes 49160 | tf_op jit(solution)/shard_map/ppermute | solution.py:247
  19.3 0.0 copy-done.3
  19.3 2.0 %collective-permute-start.3 = (bf16[16,256]{1,0:T(8,128)(2,1)S(1)}, bf16[16,256]{1,0:T(8,128)(2,1)S(1)}, u32[]{:S(2)}, u32[]{:S(2)}) collective-permute-start(bf16[16,256]{1,0:T(8,128)(2,1)S(1)} %copy-done.3), channel_id=1, source_target_pairs={{0,112},{16,32},{32,16},{48,64},{64,48},{80,96},{96,80},{112,0},{1... | collective-permute-start | bytes 24584 | tf_op jit(solution)/shard_map/ppermute | solution.py:247
  21.3 2.4 %collective-permute-start.5 = (bf16[8,512]{1,0:T(8,128)(2,1)S(1)}, bf16[8,512]{1,0:T(8,128)(2,1)S(1)}, u32[]{:S(2)}, u32[]{:S(2)}) collective-permute-start(bf16[8,512]{1,0:T(8,128)(2,1)S(1)} %copy-done.2), channel_id=1, source_target_pairs={{0,12},{4,8},{8,4},{12,0},{1,13},{5,9},{9,5},{13,1},{2,14},{6,10},... | collective-permute-start | bytes 24584 | tf_op jit(solution)/shard_map/ppermute | solution.py:247
  23.8 0.0 collective-permute-done.2.refs_3_
  23.8 0.0 collective-permute-start.4
  23.8 0.0 collective-permute-done.3.refs_4_
  23.8 1.6 %collective-permute-done.5.refs_6_ = bf16[8,512]{1,0:T(8,128)(2,1)S(1)} collective-permute-done((bf16[8,512]{1,0:T(8,128)(2,1)S(1)}, bf16[8,512]{1,0:T(8,128)(2,1)S(1)}, u32[]{:S(2)}, u32[]{:S(2)}) %collective-permute-start.5) | collective-permute-done | bytes 8224 | tf_op jit(solution)/shard_map/ppermute | solution.py:247
  25.3 1.2 collective-permute-done.4.refs_5_
  26.6 0.0 collective-permute-done.refs_1_
  26.6 0.0 collective-permute-done.1.refs_2_
  26.6 0.4 all-to-all-done
  27.0 2.1 %shard_map.87 = (bf16[1280,128]{1,0:T(8,128)(2,1)}, bf16[1280,128]{1,0:T(8,128)(2,1)}) custom-call(bf16[1280,128]{1,0:T(8,128)(2,1)S(1)} %bitcast.25, bf16[1,256,256]{2,1,0:T(8,128)(2,1)} %refs_0_.1), custom_call_target="tpu_custom_call" | custom-call | tf_op jit(solution)/shard_map/pallas_call | solution.py:150
  29.1 5.7 %all-to-all-start.1 = ((bf16[128,5,2,128]{3,2,1,0:T(2,128)(2,1)}), bf16[128,5,2,128]{3,2,1,0:T(2,128)(2,1)S(1)}, u32[]{:S(2)}, u32[]{:S(2)}) async-start(bf16[128,5,2,128]{3,2,1,0:T(2,128)(2,1)} %bitcast.30), calls=%async_computation.1 | async-start | bytes 655360 | tf_op jit(solution)/shard_map/all_to_all | solution.py:698
  34.8 8.8 %shard_map.88 = (f32[16,32,256]{2,1,0:T(8,128)}, f32[16,32,256]{2,1,0:T(8,128)}, f32[16,32,256]{2,1,0:T(8,128)}, f32[16,32,256]{2,1,0:T(8,128)}, f32[16,32,256]{...) custom-call(f32[9]{0:T(128)S(1)} %stack.63.refs_0_, ...), custom_call_target="tpu_custom_call" | custom-call | tf_op jit(solution)/shard_map/pallas_call | solution.py:150
  43.7 2.6 %all-to-all-done.1 = bf16[128,5,2,128]{3,2,1,0:T(2,128)(2,1)S(1)} async-done(((bf16[128,5,2,128]{3,2,1,0:T(2,128)(2,1)}), bf16[128,5,2,128]{3,2,1,0:T(2,128)(2,1)S(1)}, u32[]{:S(2)}, u32[]{:S(2)}) %all-to-all-start.1) | async-done | bytes 327712 | tf_op jit(solution)/shard_map/all_to_all | solution.py:698
  46.3 2.8 %shard_map.89 = (f32[16,32,256]{2,1,0:T(8,128)S(1)}, bf16[32,256]{1,0:T(8,128)(2,1)S(1)}, bf16[32,256]{1,0:T(8,128)(2,1)S(1)}, bf16[16,256]{1,0:T(8,128)(2,1)S(1...) custom-call(f32[9]{0:T(128)S(1)} %stack.63.refs_0_, ...), custom_call_target="tpu_custom_call" | custom-call | tf_op jit(solution)/shard_map/pallas_call | solution.py:150
  49.2 1.4 %collective-permute-start.8 = (bf16[16,256]{1,0:T(8,128)(2,1)S(1)}, bf16[16,256]{1,0:T(8,128)(2,1)S(1)}, u32[]{:S(2)}, u32[]{:S(2)}) collective-permute-start(bf16[16,256]{1,0:T(8,128)(2,1)S(1)} %get-tuple-element.98), channel_id=1, source_target_pairs={{0,16},{16,0},{32,48},{48,32},{64,80},{80,64},{96,112},{112,96},{1... | collective-permute-start | bytes 24584 | tf_op jit(solution)/shard_map/ppermute | solution.py:247
  50.5 0.4 collective-permute-start.6
  50.9 0.0 collective-permute-start.7
  50.9 1.4 %collective-permute-start.9 = (bf16[16,256]{1,0:T(8,128)(2,1)S(1)}, bf16[16,256]{1,0:T(8,128)(2,1)S(1)}, u32[]{:S(2)}, u32[]{:S(2)}) collective-permute-start(bf16[16,256]{1,0:T(8,128)(2,1)S(1)} %get-tuple-element.99), channel_id=1, source_target_pairs={{0,112},{16,32},{32,16},{48,64},{64,48},{80,96},{96,80},{112,0},{1... | collective-permute-start | bytes 24584 | tf_op jit(solution)/shard_map/ppermute | solution.py:247
  52.4 2.4 %collective-permute-start.11 = (bf16[8,512]{1,0:T(8,128)(2,1)S(1)}, bf16[8,512]{1,0:T(8,128)(2,1)S(1)}, u32[]{:S(2)}, u32[]{:S(2)}) collective-permute-start(bf16[8,512]{1,0:T(8,128)(2,1)S(1)} %get-tuple-element.100), channel_id=1, source_target_pairs={{0,12},{4,8},{8,4},{12,0},{1,13},{5,9},{9,5},{13,1},{2,14},{6,10},... | collective-permute-start | bytes 24584 | tf_op jit(solution)/shard_map/ppermute | solution.py:247
  54.8 0.0 collective-permute-done.8.refs_11_
  54.8 0.0 collective-permute-start.10
  54.8 0.0 collective-permute-done.9.refs_12_
  54.8 1.3 collective-permute-done.11.refs_14_
  56.1 1.2 collective-permute-done.10.refs_13_
  57.3 0.0 collective-permute-done.6.refs_9_
  57.3 0.0 collective-permute-done.7.refs_10_
  57.3 3.1 %shard_map.90 = (f32[16,32,256]{2,1,0:T(8,128)}, bf16[1280,128]{1,0:T(8,128)(2,1)}, f32[16,32,256]{2,1,0:T(8,128)}) custom-call(f32[9]{0:T(128)S(1)} %stack.63.refs_0_, f32[16,32,256]{2,1,0:T(8,128)S(1)} %get-tuple-element.88.refs_1_, f32[16,32,256]{2,1,0:T(8,128)S(1)} %get-tuple-element.89.refs_2_, f32[16,32,256]{2,1,0:T(8,128)S(1)} %get-tuple-element.90.refs_3_, ...), custom_call_target="tpu_custom_call" | custom-call | tf_op jit(solution)/shard_map/pallas_call | solution.py:150
  60.5 18.1 %all_to_all.31 = bf16[128,5,2,128]{3,2,1,0:T(2,128)(2,1)S(1)} all-to-all(bf16[128,5,2,128]{3,2,1,0:T(2,128)(2,1)} %bitcast.31), channel_id=1, replica_groups=mesh['gx'=8,'gy'=4,'gz'=4] {'gx','gy','gz'}, dimensions={0} | all-to-all | bytes 655360 | tf_op jit(solution)/shard_map/all_to_all | solution.py:698
  78.6 2.2 %shard_map.91 = (bf16[1280,128]{1,0:T(8,128)(2,1)}, f32[8,128]{1,0:T(8,128)}) custom-call(bf16[1,256,256]{2,1,0:T(8,128)(2,1)} %refs_0_.1, bf16[1280,128]{1,0:T(8,128)(2,1)} %get-tuple-element.71.refs_1_, bf16[1280,128]{1,0:T(8,128)(2,1)S(1)} %bitcast.26), custom_call_target="tpu_custom_call" | custom-call | tf_op jit(solution)/shard_map/pallas_call | solution.py:150
  80.8 4.7 %all-to-all-start.3 = ((bf16[128,5,2,128]{3,2,1,0:T(2,128)(2,1)}), bf16[128,5,2,128]{3,2,1,0:T(2,128)(2,1)S(1)}, u32[]{:S(2)}, u32[]{:S(2)}) async-start(bf16[128,5,2,128]{3,2,1,0:T(2,128)(2,1)} %bitcast.32), calls=%async_computation.3 | async-start | bytes 655360 | tf_op jit(solution)/shard_map/all_to_all | solution.py:698
  85.5 7.6 %shard_map.92.refs_5_ = f32[16,32,256]{2,1,0:T(8,128)} custom-call(f32[8,128]{1,0:T(8,128)} %get-tuple-element.104.refs_0_, f32[16,32,256]{2,1,0:T(8,128)} %refs_4_.3, f32[16,32,256]{2,1,0:T(8,128)} %get-tuple-element.106.refs_2_.refs_13_.refs_5_, f32[16,32,256]{2,1,0:T(8,128)} %get-tuple-element.107.refs_3_, ...), custom_call_target="tpu_custom_call" | custom-call | tf_op jit(solution)/shard_map/pallas_call | solution.py:150
  93.2 3.8 %all-to-all-done.3 = bf16[128,5,2,128]{3,2,1,0:T(2,128)(2,1)S(1)} async-done(((bf16[128,5,2,128]{3,2,1,0:T(2,128)(2,1)}), bf16[128,5,2,128]{3,2,1,0:T(2,128)(2,1)S(1)}, u32[]{:S(2)}, u32[]{:S(2)}) %all-to-all-start.3) | async-done | bytes 327712 | tf_op jit(solution)/shard_map/all_to_all | solution.py:698
  97.0 2.9 %shard_map.93 = (f32[16,32,256]{2,1,0:T(8,128)S(1)}, bf16[32,256]{1,0:T(8,128)(2,1)S(1)}, bf16[32,256]{1,0:T(8,128)(2,1)S(1)}, bf16[16,256]{1,0:T(8,128)(2,1)S(1...) custom-call(f32[9]{0:T(128)S(1)} %stack.63.refs_0_, ...), custom_call_target="tpu_custom_call" | custom-call | tf_op jit(solution)/shard_map/pallas_call | solution.py:150
  99.9 1.4 %collective-permute-start.14 = (bf16[16,256]{1,0:T(8,128)(2,1)S(1)}, bf16[16,256]{1,0:T(8,128)(2,1)S(1)}, u32[]{:S(2)}, u32[]{:S(2)}) collective-permute-start(bf16[16,256]{1,0:T(8,128)(2,1)S(1)} %get-tuple-element.119), channel_id=1, source_target_pairs={{0,16},{16,0},{32,48},{48,32},{64,80},{80,64},{96,112},{112,96},{1... | collective-permute-start | bytes 24584 | tf_op jit(solution)/shard_map/ppermute | solution.py:247
  101.3 0.4 collective-permute-start.12
  101.7 0.0 collective-permute-start.13
  101.7 1.2 collective-permute-start.15
  102.9 1.5 %collective-permute-start.17 = (bf16[8,512]{1,0:T(8,128)(2,1)S(1)}, bf16[8,512]{1,0:T(8,128)(2,1)S(1)}, u32[]{:S(2)}, u32[]{:S(2)}) collective-permute-start(bf16[8,512]{1,0:T(8,128)(2,1)S(1)} %get-tuple-element.121), channel_id=1, source_target_pairs={{0,12},{4,8},{8,4},{12,0},{1,13},{5,9},{9,5},{13,1},{2,14},{6,10},... | collective-permute-start | bytes 24584 | tf_op jit(solution)/shard_map/ppermute | solution.py:247
  104.4 0.0 collective-permute-done.14.refs_12_
  104.4 0.0 collective-permute-start.16
  104.4 0.4 collective-permute-done.15.refs_13_
  104.8 1.8 %collective-permute-done.17.refs_15_ = bf16[8,512]{1,0:T(8,128)(2,1)S(1)} collective-permute-done((bf16[8,512]{1,0:T(8,128)(2,1)S(1)}, bf16[8,512]{1,0:T(8,128)(2,1)S(1)}, u32[]{:S(2)}, u32[]{:S(2)}) %collective-permute-start.17) | collective-permute-done | bytes 8224 | tf_op jit(solution)/shard_map/ppermute | solution.py:247
  106.6 0.3 collective-permute-done.16.refs_14_
  106.9 0.0 collective-permute-done.12.refs_10_
  106.9 0.0 collective-permute-done.13.refs_11_
  106.9 2.2 %shard_map.94 = (f32[16,32,256]{2,1,0:T(8,128)}, f32[128,128]{1,0:T(8,128)S(1)}, f32[16,32,256]{2,1,0:T(8,128)}) custom-call(f32[9]{0:T(128)S(1)} %stack.63.refs_0_, f32[16,32,256]{2,1,0:T(8,128)S(1)} %get-tuple-element.108.refs_1_, f32[16,32,256]{2,1,0:T(8,128)S(1)} %get-tuple-element.109.refs_2_, f32[16,32,256]{2,1,0:T(8,128)S(1)} %get-tuple-element.110.refs_3_, ...), custom_call_target="tpu_custom_call" | custom-call | tf_op jit(solution)/shard_map/pallas_call | solution.py:150
  109.0 17.0 %all_to_all.32 = f32[128,1,128]{2,1,0:T(1,128)S(1)} all-to-all(f32[128,1,128]{2,1,0:T(1,128)S(1)} %bitcast.28), channel_id=1, replica_groups=mesh['gx'=8,'gy'=4,'gz'=4] {'gx','gy','gz'}, dimensions={0} | all-to-all | bytes 131072 | tf_op jit(solution)/shard_map/all_to_all | solution.py:698
  126.0 2.6 %shard_map.95 = (f32[16,32,256]{2,1,0:T(8,128)}, f32[16,32,256]{2,1,0:T(8,128)}) custom-call(f32[8,128]{1,0:T(8,128)} %get-tuple-element.104.refs_0_, f32[128,128]{1,0:T(8,128)S(1)} %bitcast.27, f32[16,32,256]{2,1,0:T(8,128)} %get-tuple-element.123.refs_2_, f32[16,32,256]{2,1,0:T(8,128)} %get-tuple-element.124.refs_3_, f32[16,32,256]{2,1,0:T(8,128)} %refs_4_.3, ...), custom_call_target="tpu_custom_call" | custom-call | tf_op jit(solution)/shard_map/pallas_call | solution.py:150
  (1 shorter events, 0.0 us)
Async XLA Ops:
  4.1 11.6 %copy-start.4 = (bf16[16,256]{1,0:T(8,128)(2,1)S(1)}, bf16[16,256]{1,0:T(8,128)(2,1)}, u32[]{:S(2)}) copy-start(bf16[16,256]{1,0:T(8,128)(2,1)} %get-tuple-element.67) | copy-start | bytes 24580
  4.1 12.7 %copy-start.1 = (bf16[32,256]{1,0:T(8,128)(2,1)S(1)}, bf16[32,256]{1,0:T(8,128)(2,1)}, u32[]{:S(2)}) copy-start(bf16[32,256]{1,0:T(8,128)(2,1)} %get-tuple-element.65) | copy-start | bytes 49156
  4.1 13.4 %copy-start = (bf16[32,256]{1,0:T(8,128)(2,1)S(1)}, bf16[32,256]{1,0:T(8,128)(2,1)}, u32[]{:S(2)}) copy-start(bf16[32,256]{1,0:T(8,128)(2,1)} %get-tuple-element.66) | copy-start | bytes 49156
  4.1 15.2 %copy-start.3 = (bf16[16,256]{1,0:T(8,128)(2,1)S(1)}, bf16[16,256]{1,0:T(8,128)(2,1)}, u32[]{:S(2)}) copy-start(bf16[16,256]{1,0:T(8,128)(2,1)} %get-tuple-element.68) | copy-start | bytes 24580
  4.1 22.9 %all-to-all-start = ((bf16[128,5,2,128]{3,2,1,0:T(2,128)(2,1)}), bf16[128,5,2,128]{3,2,1,0:T(2,128)(2,1)S(1)}, u32[]{:S(2)}, u32[]{:S(2)}) async-start(bf16[128,5,2,128]{3,2,1,0:T(2,128)(2,1)} %bitcast.29), calls=%async_computation | async-start | bytes 655360 | tf_op jit(solution)/shard_map/all_to_all | solution.py:698
  15.6 5.7 %copy-start.2 = (bf16[8,512]{1,0:T(8,128)(2,1)S(1)}, bf16[8,512]{1,0:T(8,128)(2,1)}, u32[]{:S(2)}) copy-start(bf16[8,512]{1,0:T(8,128)(2,1)} %get-tuple-element.69) | copy-start | bytes 24580
  15.7 8.1 %collective-permute-start.2 = (bf16[16,256]{1,0:T(8,128)(2,1)S(1)}, bf16[16,256]{1,0:T(8,128)(2,1)S(1)}, u32[]{:S(2)}, u32[]{:S(2)}) collective-permute-start(bf16[16,256]{1,0:T(8,128)(2,1)S(1)} %copy-done.4), channel_id=1, source_target_pairs={{0,16},{16,0},{32,48},{48,32},{64,80},{80,64},{96,112},{112,96},{1... | collective-permute-start | bytes 24584 | tf_op jit(solution)/shard_map/ppermute | solution.py:247
  16.8 9.8 %collective-permute-start = (bf16[32,256]{1,0:T(8,128)(2,1)S(1)}, bf16[32,256]{1,0:T(8,128)(2,1)S(1)}, u32[]{:S(2)}, u32[]{:S(2)}) collective-permute-start(bf16[32,256]{1,0:T(8,128)(2,1)S(1)} %copy-done.1), channel_id=1, source_target_pairs={{0,1},{1,0},{2,3},{3,2},{4,5},{5,4},{6,7},{7,6},{8,9},{9,8},{10,11... | collective-permute-start | bytes 49160 | tf_op jit(solution)/shard_map/ppermute | solution.py:247
  17.5 9.1 %collective-permute-start.1 = (bf16[32,256]{1,0:T(8,128)(2,1)S(1)}, bf16[32,256]{1,0:T(8,128)(2,1)S(1)}, u32[]{:S(2)}, u32[]{:S(2)}) collective-permute-start(bf16[32,256]{1,0:T(8,128)(2,1)S(1)} %copy-done), channel_id=1, source_target_pairs={{0,3},{1,2},{2,1},{3,0},{4,7},{5,6},{6,5},{7,4},{8,11},{9,10},{10,... | collective-permute-start | bytes 49160 | tf_op jit(solution)/shard_map/ppermute | solution.py:247
  19.3 4.5 %collective-permute-start.3 = (bf16[16,256]{1,0:T(8,128)(2,1)S(1)}, bf16[16,256]{1,0:T(8,128)(2,1)S(1)}, u32[]{:S(2)}, u32[]{:S(2)}) collective-permute-start(bf16[16,256]{1,0:T(8,128)(2,1)S(1)} %copy-done.3), channel_id=1, source_target_pairs={{0,112},{16,32},{32,16},{48,64},{64,48},{80,96},{96,80},{112,0},{1... | collective-permute-start | bytes 24584 | tf_op jit(solution)/shard_map/ppermute | solution.py:247
  21.3 4.0 %collective-permute-start.5 = (bf16[8,512]{1,0:T(8,128)(2,1)S(1)}, bf16[8,512]{1,0:T(8,128)(2,1)S(1)}, u32[]{:S(2)}, u32[]{:S(2)}) collective-permute-start(bf16[8,512]{1,0:T(8,128)(2,1)S(1)} %copy-done.2), channel_id=1, source_target_pairs={{0,12},{4,8},{8,4},{12,0},{1,13},{5,9},{9,5},{13,1},{2,14},{6,10},... | collective-permute-start | bytes 24584 | tf_op jit(solution)/shard_map/ppermute | solution.py:247
  23.8 2.8 %collective-permute-start.4 = (bf16[8,512]{1,0:T(8,128)(2,1)S(1)}, bf16[8,512]{1,0:T(8,128)(2,1)S(1)}, u32[]{:S(2)}, u32[]{:S(2)}) collective-permute-start(bf16[8,512]{1,0:T(8,128)(2,1)S(1)} %copy-done.2), channel_id=1, source_target_pairs={{0,4},{4,0},{8,12},{12,8},{1,5},{5,1},{9,13},{13,9},{2,6},{6,2},{1... | collective-permute-start | bytes 24584 | tf_op jit(solution)/shard_map/ppermute | solution.py:247
  29.1 17.2 %all-to-all-start.1 = ((bf16[128,5,2,128]{3,2,1,0:T(2,128)(2,1)}), bf16[128,5,2,128]{3,2,1,0:T(2,128)(2,1)S(1)}, u32[]{:S(2)}, u32[]{:S(2)}) async-start(bf16[128,5,2,128]{3,2,1,0:T(2,128)(2,1)} %bitcast.30), calls=%async_computation.1 | async-start | bytes 655360 | tf_op jit(solution)/shard_map/all_to_all | solution.py:698
  49.2 5.6 %collective-permute-start.8 = (bf16[16,256]{1,0:T(8,128)(2,1)S(1)}, bf16[16,256]{1,0:T(8,128)(2,1)S(1)}, u32[]{:S(2)}, u32[]{:S(2)}) collective-permute-start(bf16[16,256]{1,0:T(8,128)(2,1)S(1)} %get-tuple-element.98), channel_id=1, source_target_pairs={{0,16},{16,0},{32,48},{48,32},{64,80},{80,64},{96,112},{112,96},{1... | collective-permute-start | bytes 24584 | tf_op jit(solution)/shard_map/ppermute | solution.py:247
  50.5 6.8 %collective-permute-start.6 = (bf16[32,256]{1,0:T(8,128)(2,1)S(1)}, bf16[32,256]{1,0:T(8,128)(2,1)S(1)}, u32[]{:S(2)}, u32[]{:S(2)}) collective-permute-start(bf16[32,256]{1,0:T(8,128)(2,1)S(1)} %get-tuple-element.96), channel_id=1, source_target_pairs={{0,1},{1,0},{2,3},{3,2},{4,5},{5,4},{6,7},{7,6},{8,9},{9,8},{10,11... | collective-permute-start | bytes 49160 | tf_op jit(solution)/shard_map/ppermute | solution.py:247
  50.9 6.4 %collective-permute-start.7 = (bf16[32,256]{1,0:T(8,128)(2,1)S(1)}, bf16[32,256]{1,0:T(8,128)(2,1)S(1)}, u32[]{:S(2)}, u32[]{:S(2)}) collective-permute-start(bf16[32,256]{1,0:T(8,128)(2,1)S(1)} %get-tuple-element.97), channel_id=1, source_target_pairs={{0,3},{1,2},{2,1},{3,0},{4,7},{5,6},{6,5},{7,4},{8,11},{9,10},{10,... | collective-permute-start | bytes 49160 | tf_op jit(solution)/shard_map/ppermute | solution.py:247
  50.9 3.9 %collective-permute-start.9 = (bf16[16,256]{1,0:T(8,128)(2,1)S(1)}, bf16[16,256]{1,0:T(8,128)(2,1)S(1)}, u32[]{:S(2)}, u32[]{:S(2)}) collective-permute-start(bf16[16,256]{1,0:T(8,128)(2,1)S(1)} %get-tuple-element.99), channel_id=1, source_target_pairs={{0,112},{16,32},{32,16},{48,64},{64,48},{80,96},{96,80},{112,0},{1... | collective-permute-start | bytes 24584 | tf_op jit(solution)/shard_map/ppermute | solution.py:247
  52.4 3.7 %collective-permute-start.11 = (bf16[8,512]{1,0:T(8,128)(2,1)S(1)}, bf16[8,512]{1,0:T(8,128)(2,1)S(1)}, u32[]{:S(2)}, u32[]{:S(2)}) collective-permute-start(bf16[8,512]{1,0:T(8,128)(2,1)S(1)} %get-tuple-element.100), channel_id=1, source_target_pairs={{0,12},{4,8},{8,4},{12,0},{1,13},{5,9},{9,5},{13,1},{2,14},{6,10},... | collective-permute-start | bytes 24584 | tf_op jit(solution)/shard_map/ppermute | solution.py:247
  54.8 2.5 %collective-permute-start.10 = (bf16[8,512]{1,0:T(8,128)(2,1)S(1)}, bf16[8,512]{1,0:T(8,128)(2,1)S(1)}, u32[]{:S(2)}, u32[]{:S(2)}) collective-permute-start(bf16[8,512]{1,0:T(8,128)(2,1)S(1)} %get-tuple-element.100), channel_id=1, source_target_pairs={{0,4},{4,0},{8,12},{12,8},{1,5},{5,1},{9,13},{13,9},{2,6},{6,2},{1... | collective-permute-start | bytes 24584 | tf_op jit(solution)/shard_map/ppermute | solution.py:247
  80.8 16.2 %all-to-all-start.3 = ((bf16[128,5,2,128]{3,2,1,0:T(2,128)(2,1)}), bf16[128,5,2,128]{3,2,1,0:T(2,128)(2,1)S(1)}, u32[]{:S(2)}, u32[]{:S(2)}) async-start(bf16[128,5,2,128]{3,2,1,0:T(2,128)(2,1)} %bitcast.32), calls=%async_computation.3 | async-start | bytes 655360 | tf_op jit(solution)/shard_map/all_to_all | solution.py:698
  99.9 4.4 %collective-permute-start.14 = (bf16[16,256]{1,0:T(8,128)(2,1)S(1)}, bf16[16,256]{1,0:T(8,128)(2,1)S(1)}, u32[]{:S(2)}, u32[]{:S(2)}) collective-permute-start(bf16[16,256]{1,0:T(8,128)(2,1)S(1)} %get-tuple-element.119), channel_id=1, source_target_pairs={{0,16},{16,0},{32,48},{48,32},{64,80},{80,64},{96,112},{112,96},{1... | collective-permute-start | bytes 24584 | tf_op jit(solution)/shard_map/ppermute | solution.py:247
  101.3 5.6 %collective-permute-start.12 = (bf16[32,256]{1,0:T(8,128)(2,1)S(1)}, bf16[32,256]{1,0:T(8,128)(2,1)S(1)}, u32[]{:S(2)}, u32[]{:S(2)}) collective-permute-start(bf16[32,256]{1,0:T(8,128)(2,1)S(1)} %get-tuple-element.117), channel_id=1, source_target_pairs={{0,1},{1,0},{2,3},{3,2},{4,5},{5,4},{6,7},{7,6},{8,9},{9,8},{10,11... | collective-permute-start | bytes 49160 | tf_op jit(solution)/shard_map/ppermute | solution.py:247
  101.7 5.2 %collective-permute-start.13 = (bf16[32,256]{1,0:T(8,128)(2,1)S(1)}, bf16[32,256]{1,0:T(8,128)(2,1)S(1)}, u32[]{:S(2)}, u32[]{:S(2)}) collective-permute-start(bf16[32,256]{1,0:T(8,128)(2,1)S(1)} %get-tuple-element.118), channel_id=1, source_target_pairs={{0,3},{1,2},{2,1},{3,0},{4,7},{5,6},{6,5},{7,4},{8,11},{9,10},{10,... | collective-permute-start | bytes 49160 | tf_op jit(solution)/shard_map/ppermute | solution.py:247
  101.7 3.1 %collective-permute-start.15 = (bf16[16,256]{1,0:T(8,128)(2,1)S(1)}, bf16[16,256]{1,0:T(8,128)(2,1)S(1)}, u32[]{:S(2)}, u32[]{:S(2)}) collective-permute-start(bf16[16,256]{1,0:T(8,128)(2,1)S(1)} %get-tuple-element.120), channel_id=1, source_target_pairs={{0,112},{16,32},{32,16},{48,64},{64,48},{80,96},{96,80},{112,0},{1... | collective-permute-start | bytes 24584 | tf_op jit(solution)/shard_map/ppermute | solution.py:247
  102.9 3.7 %collective-permute-start.17 = (bf16[8,512]{1,0:T(8,128)(2,1)S(1)}, bf16[8,512]{1,0:T(8,128)(2,1)S(1)}, u32[]{:S(2)}, u32[]{:S(2)}) collective-permute-start(bf16[8,512]{1,0:T(8,128)(2,1)S(1)} %get-tuple-element.121), channel_id=1, source_target_pairs={{0,12},{4,8},{8,4},{12,0},{1,13},{5,9},{9,5},{13,1},{2,14},{6,10},... | collective-permute-start | bytes 24584 | tf_op jit(solution)/shard_map/ppermute | solution.py:247
  104.4 2.5 %collective-permute-start.16 = (bf16[8,512]{1,0:T(8,128)(2,1)S(1)}, bf16[8,512]{1,0:T(8,128)(2,1)S(1)}, u32[]{:S(2)}, u32[]{:S(2)}) collective-permute-start(bf16[8,512]{1,0:T(8,128)(2,1)S(1)} %get-tuple-element.121), channel_id=1, source_target_pairs={{0,4},{4,0},{8,12},{12,8},{1,5},{5,1},{9,13},{13,9},{2,6},{6,2},{1... | collective-permute-start | bytes 24584 | tf_op jit(solution)/shard_map/ppermute | solution.py:247

commit v6 on v5

--- a/solution.py
+++ b/solution.py
@@ -448,7 +448,7 @@
 
 
 def cg(cz, cx, cy, s, p, q, e, y, first, local):
-    def sweep(next_of, cz, cx, cy):
+    def sweep(next_of, cz, cx, cy, last=False):
         rho = jnp.zeros((8, LANES), F32)
         pe, ee = rho, rho
         below, (now, left) = None, next_of(0)
@@ -466,11 +466,15 @@
                 cx[z],
                 cy[z],
             )
-            e[z] = image
             pe = pe + fold(now * image)
-            ee = ee + fold(image * image)
+            if not last:
+                e[z] = image
+                ee = ee + fold(image * image)
             below, now = now, above
-        rho, pe, ee = total(rho), total(pe), total(ee)
+        rho, pe = total(rho), total(pe)
+        if last:
+            return rho / pe
+        ee = total(ee)
         inverse = 1.0 / pe
         a = rho * inverse
         return a, a * ee * inverse - 1.0
@@ -493,12 +497,13 @@
 
         return next_of
 
-    def later(a, beta):
+    def later(a, beta, last=False):
         def next_of(z):
             old = p[z]
             y[z] = y[z] + a * old
             left = q[z] - a * e[z]
-            q[z] = left
+            if not last:
+                q[z] = left
             new = left + beta * old
             p[z] = new
             return new, left
@@ -508,8 +513,8 @@
     carry = sweep(begin, cz, cx, cy)
     cz, cx, cy = full(cz), full(cx), full(cy)
     carry = sweep(second(*carry), cz, cx, cy)
-    carry = lax.fori_loop(0, INNER - 2, lambda _, c: sweep(later(*c), cz, cx, cy), carry)
-    a = carry[0]
+    carry = lax.fori_loop(0, INNER - 3, lambda _, c: sweep(later(*c), cz, cx, cy), carry)
+    a = sweep(later(*carry, last=True), cz, cx, cy, last=True)
     for z in range(CZ):
         local[z] = s[z] * (y[z] + a * p[z])
 

time: 129 us -> 130 us (level)
  no operation moved by 1% of the time
where the time goes in v6:
time: 130 us; the launch traced here: 129 us
  starting transfers between devices  40 us (31%)
  Pallas kernels  37.8 us (29%)
  blocking collectives  35.3 us (27%)
  waiting for transfers between devices  14.7 us (11%)
    pallas_call x10, Pallas kernels, run(): pl.pallas_call(kernel, out_shape=tuple((pltpu.HBM(a.shape, a.dtype) if m...  37.8 us
    all_to_all x2, blocking collectives, swap(): return lax.all_to_all(x, AX, split_axis=0, concat_axis=0, tiled=True)  35.3 us
    all_to_all x3, starting transfers between devices, swap(): return lax.all_to_all(x, AX, split_axis=0, concat_axis=0, tiled=True)  21.9 us
    ppermute x18, starting transfers between devices, pair(): return [lax.ppermute(first, axis, even), lax.ppermute(second, axis, odd)]  18.1 us
    ppermute x18, waiting for transfers between devices, pair(): return [lax.ppermute(first, axis, even), lax.ppermute(second, axis, odd)]  7.81 us
    all_to_all x3, waiting for transfers between devices, swap(): return lax.all_to_all(x, AX, split_axis=0, concat_axis=0, tiled=True)  6.91 us
  transfers between devices with their start and end apart: 21, of which 10 were waited for; matrix products, arithmetic and copies ran while one was open for 0% of the time, Pallas kernels for 13%

profile of v6, /device:TPU:1, one launch (start us, length us, event | category | flops | bytes accessed | tf_op | source)
XLA Modules:
  0.0 129.0 jit_solution(2039513202617701534)
XLA Ops:
  0.7 0.1 stack.63.refs_0_
  0.8 3.3 %shard_map.86 = (bf16[1280,128]{1,0:T(8,128)(2,1)}, bf16[512,128]{1,0:T(8,128)(2,1)}, bf16[32,512]{1,0:T(8,128)(2,1)}, bf16[512,128]{1,0:T(8,128)(2,1)}, bf16[12...) custom-call(f32[9]{0:T(128)S(1)} %stack.63.refs_0_, ...), custom_call_target="tpu_custom_call" | custom-call | tf_op jit(solution)/shard_map/pallas_call | solution.py:150
  4.1 0.0 copy-start.4
  4.1 0.0 copy-start.1
  4.1 0.0 copy-start
  4.1 0.0 copy-start.3
  4.1 11.5 %all-to-all-start = ((bf16[128,5,2,128]{3,2,1,0:T(2,128)(2,1)}), bf16[128,5,2,128]{3,2,1,0:T(2,128)(2,1)S(1)}, u32[]{:S(2)}, u32[]{:S(2)}) async-start(bf16[128,5,2,128]{3,2,1,0:T(2,128)(2,1)} %bitcast.29), calls=%async_computation | async-start | bytes 655360 | tf_op jit(solution)/shard_map/all_to_all | solution.py:703
  15.6 0.0 copy-start.2
  15.6 0.0 copy-done.4
  15.7 1.1 collective-permute-start.2
  16.8 0.0 copy-done.1
  16.8 0.7 collective-permute-start
  17.5 0.0 copy-done
  17.5 1.8 %collective-permute-start.1 = (bf16[32,256]{1,0:T(8,128)(2,1)S(1)}, bf16[32,256]{1,0:T(8,128)(2,1)S(1)}, u32[]{:S(2)}, u32[]{:S(2)}) collective-permute-start(bf16[32,256]{1,0:T(8,128)(2,1)S(1)} %copy-done), channel_id=1, source_target_pairs={{0,3},{1,2},{2,1},{3,0},{4,7},{5,6},{6,5},{7,4},{8,11},{9,10},{10,... | collective-permute-start | bytes 49160 | tf_op jit(solution)/shard_map/ppermute | solution.py:247
  19.3 0.0 copy-done.3
  19.3 2.0 %collective-permute-start.3 = (bf16[16,256]{1,0:T(8,128)(2,1)S(1)}, bf16[16,256]{1,0:T(8,128)(2,1)S(1)}, u32[]{:S(2)}, u32[]{:S(2)}) collective-permute-start(bf16[16,256]{1,0:T(8,128)(2,1)S(1)} %copy-done.3), channel_id=1, source_target_pairs={{0,112},{16,32},{32,16},{48,64},{64,48},{80,96},{96,80},{112,0},{1... | collective-permute-start | bytes 24584 | tf_op jit(solution)/shard_map/ppermute | solution.py:247
  21.3 2.4 %collective-permute-start.5 = (bf16[8,512]{1,0:T(8,128)(2,1)S(1)}, bf16[8,512]{1,0:T(8,128)(2,1)S(1)}, u32[]{:S(2)}, u32[]{:S(2)}) collective-permute-start(bf16[8,512]{1,0:T(8,128)(2,1)S(1)} %copy-done.2), channel_id=1, source_target_pairs={{0,12},{4,8},{8,4},{12,0},{1,13},{5,9},{9,5},{13,1},{2,14},{6,10},... | collective-permute-start | bytes 24584 | tf_op jit(solution)/shard_map/ppermute | solution.py:247
  23.8 0.0 collective-permute-done.2.refs_3_
  23.8 0.0 collective-permute-start.4
  23.8 0.0 collective-permute-done.3.refs_4_
  23.8 1.6 %collective-permute-done.5.refs_6_ = bf16[8,512]{1,0:T(8,128)(2,1)S(1)} collective-permute-done((bf16[8,512]{1,0:T(8,128)(2,1)S(1)}, bf16[8,512]{1,0:T(8,128)(2,1)S(1)}, u32[]{:S(2)}, u32[]{:S(2)}) %collective-permute-start.5) | collective-permute-done | bytes 8224 | tf_op jit(solution)/shard_map/ppermute | solution.py:247
  25.3 1.2 collective-permute-done.4.refs_5_
  26.6 0.0 collective-permute-done.refs_1_
  26.6 0.0 collective-permute-done.1.refs_2_
  26.6 0.4 all-to-all-done
  27.0 2.1 %shard_map.87 = (bf16[1280,128]{1,0:T(8,128)(2,1)}, bf16[1280,128]{1,0:T(8,128)(2,1)}) custom-call(bf16[1280,128]{1,0:T(8,128)(2,1)S(1)} %bitcast.25, bf16[1,256,256]{2,1,0:T(8,128)(2,1)} %refs_0_.1), custom_call_target="tpu_custom_call" | custom-call | tf_op jit(solution)/shard_map/pallas_call | solution.py:150
  29.1 5.7 %all-to-all-start.1 = ((bf16[128,5,2,128]{3,2,1,0:T(2,128)(2,1)}), bf16[128,5,2,128]{3,2,1,0:T(2,128)(2,1)S(1)}, u32[]{:S(2)}, u32[]{:S(2)}) async-start(bf16[128,5,2,128]{3,2,1,0:T(2,128)(2,1)} %bitcast.30), calls=%async_computation.1 | async-start | bytes 655360 | tf_op jit(solution)/shard_map/all_to_all | solution.py:703
  34.8 8.8 %shard_map.88 = (f32[16,32,256]{2,1,0:T(8,128)}, f32[16,32,256]{2,1,0:T(8,128)}, f32[16,32,256]{2,1,0:T(8,128)}, f32[16,32,256]{2,1,0:T(8,128)}, f32[16,32,256]{...) custom-call(f32[9]{0:T(128)S(1)} %stack.63.refs_0_, ...), custom_call_target="tpu_custom_call" | custom-call | tf_op jit(solution)/shard_map/pallas_call | solution.py:150
  43.7 2.6 %all-to-all-done.1 = bf16[128,5,2,128]{3,2,1,0:T(2,128)(2,1)S(1)} async-done(((bf16[128,5,2,128]{3,2,1,0:T(2,128)(2,1)}), bf16[128,5,2,128]{3,2,1,0:T(2,128)(2,1)S(1)}, u32[]{:S(2)}, u32[]{:S(2)}) %all-to-all-start.1) | async-done | bytes 327712 | tf_op jit(solution)/shard_map/all_to_all | solution.py:703
  46.3 2.8 %shard_map.89 = (f32[16,32,256]{2,1,0:T(8,128)S(1)}, bf16[32,256]{1,0:T(8,128)(2,1)S(1)}, bf16[32,256]{1,0:T(8,128)(2,1)S(1)}, bf16[16,256]{1,0:T(8,128)(2,1)S(1...) custom-call(f32[9]{0:T(128)S(1)} %stack.63.refs_0_, ...), custom_call_target="tpu_custom_call" | custom-call | tf_op jit(solution)/shard_map/pallas_call | solution.py:150
  49.2 1.4 %collective-permute-start.8 = (bf16[16,256]{1,0:T(8,128)(2,1)S(1)}, bf16[16,256]{1,0:T(8,128)(2,1)S(1)}, u32[]{:S(2)}, u32[]{:S(2)}) collective-permute-start(bf16[16,256]{1,0:T(8,128)(2,1)S(1)} %get-tuple-element.98), channel_id=1, source_target_pairs={{0,16},{16,0},{32,48},{48,32},{64,80},{80,64},{96,112},{112,96},{1... | collective-permute-start | bytes 24584 | tf_op jit(solution)/shard_map/ppermute | solution.py:247
  50.5 0.4 collective-permute-start.6
  50.9 0.0 collective-permute-start.7
  50.9 1.4 %collective-permute-start.9 = (bf16[16,256]{1,0:T(8,128)(2,1)S(1)}, bf16[16,256]{1,0:T(8,128)(2,1)S(1)}, u32[]{:S(2)}, u32[]{:S(2)}) collective-permute-start(bf16[16,256]{1,0:T(8,128)(2,1)S(1)} %get-tuple-element.99), channel_id=1, source_target_pairs={{0,112},{16,32},{32,16},{48,64},{64,48},{80,96},{96,80},{112,0},{1... | collective-permute-start | bytes 24584 | tf_op jit(solution)/shard_map/ppermute | solution.py:247
  52.4 2.4 %collective-permute-start.11 = (bf16[8,512]{1,0:T(8,128)(2,1)S(1)}, bf16[8,512]{1,0:T(8,128)(2,1)S(1)}, u32[]{:S(2)}, u32[]{:S(2)}) collective-permute-start(bf16[8,512]{1,0:T(8,128)(2,1)S(1)} %get-tuple-element.100), channel_id=1, source_target_pairs={{0,12},{4,8},{8,4},{12,0},{1,13},{5,9},{9,5},{13,1},{2,14},{6,10},... | collective-permute-start | bytes 24584 | tf_op jit(solution)/shard_map/ppermute | solution.py:247
  54.8 0.0 collective-permute-done.8.refs_11_
  54.8 0.0 collective-permute-start.10
  54.8 0.0 collective-permute-done.9.refs_12_
  54.8 1.3 collective-permute-done.11.refs_14_
  56.1 1.2 collective-permute-done.10.refs_13_
  57.3 0.0 collective-permute-done.6.refs_9_
  57.3 0.0 collective-permute-done.7.refs_10_
  57.3 3.1 %shard_map.90 = (f32[16,32,256]{2,1,0:T(8,128)}, bf16[1280,128]{1,0:T(8,128)(2,1)}, f32[16,32,256]{2,1,0:T(8,128)}) custom-call(f32[9]{0:T(128)S(1)} %stack.63.refs_0_, f32[16,32,256]{2,1,0:T(8,128)S(1)} %get-tuple-element.88.refs_1_, f32[16,32,256]{2,1,0:T(8,128)S(1)} %get-tuple-element.89.refs_2_, f32[16,32,256]{2,1,0:T(8,128)S(1)} %get-tuple-element.90.refs_3_, ...), custom_call_target="tpu_custom_call" | custom-call | tf_op jit(solution)/shard_map/pallas_call | solution.py:150
  60.5 18.3 %all_to_all.31 = bf16[128,5,2,128]{3,2,1,0:T(2,128)(2,1)S(1)} all-to-all(bf16[128,5,2,128]{3,2,1,0:T(2,128)(2,1)} %bitcast.31), channel_id=1, replica_groups=mesh['gx'=8,'gy'=4,'gz'=4] {'gx','gy','gz'}, dimensions={0} | all-to-all | bytes 655360 | tf_op jit(solution)/shard_map/all_to_all | solution.py:703
  78.8 2.2 %shard_map.91 = (bf16[1280,128]{1,0:T(8,128)(2,1)}, f32[8,128]{1,0:T(8,128)}) custom-call(bf16[1,256,256]{2,1,0:T(8,128)(2,1)} %refs_0_.1, bf16[1280,128]{1,0:T(8,128)(2,1)} %get-tuple-element.71.refs_1_, bf16[1280,128]{1,0:T(8,128)(2,1)S(1)} %bitcast.26), custom_call_target="tpu_custom_call" | custom-call | tf_op jit(solution)/shard_map/pallas_call | solution.py:150
  81.0 4.7 %all-to-all-start.3 = ((bf16[128,5,2,128]{3,2,1,0:T(2,128)(2,1)}), bf16[128,5,2,128]{3,2,1,0:T(2,128)(2,1)S(1)}, u32[]{:S(2)}, u32[]{:S(2)}) async-start(bf16[128,5,2,128]{3,2,1,0:T(2,128)(2,1)} %bitcast.32), calls=%async_computation.3 | async-start | bytes 655360 | tf_op jit(solution)/shard_map/all_to_all | solution.py:703
  85.7 7.6 %shard_map.92.refs_5_ = f32[16,32,256]{2,1,0:T(8,128)} custom-call(f32[8,128]{1,0:T(8,128)} %get-tuple-element.104.refs_0_, f32[16,32,256]{2,1,0:T(8,128)} %refs_4_.3, f32[16,32,256]{2,1,0:T(8,128)} %get-tuple-element.106.refs_2_.refs_13_.refs_5_, f32[16,32,256]{2,1,0:T(8,128)} %get-tuple-element.107.refs_3_, ...), custom_call_target="tpu_custom_call" | custom-call | tf_op jit(solution)/shard_map/pallas_call | solution.py:150
  93.4 3.8 %all-to-all-done.3 = bf16[128,5,2,128]{3,2,1,0:T(2,128)(2,1)S(1)} async-done(((bf16[128,5,2,128]{3,2,1,0:T(2,128)(2,1)}), bf16[128,5,2,128]{3,2,1,0:T(2,128)(2,1)S(1)}, u32[]{:S(2)}, u32[]{:S(2)}) %all-to-all-start.3) | async-done | bytes 327712 | tf_op jit(solution)/shard_map/all_to_all | solution.py:703
  97.2 2.9 %shard_map.93 = (f32[16,32,256]{2,1,0:T(8,128)S(1)}, bf16[32,256]{1,0:T(8,128)(2,1)S(1)}, bf16[32,256]{1,0:T(8,128)(2,1)S(1)}, bf16[16,256]{1,0:T(8,128)(2,1)S(1...) custom-call(f32[9]{0:T(128)S(1)} %stack.63.refs_0_, ...), custom_call_target="tpu_custom_call" | custom-call | tf_op jit(solution)/shard_map/pallas_call | solution.py:150
  100.1 1.4 %collective-permute-start.14 = (bf16[16,256]{1,0:T(8,128)(2,1)S(1)}, bf16[16,256]{1,0:T(8,128)(2,1)S(1)}, u32[]{:S(2)}, u32[]{:S(2)}) collective-permute-start(bf16[16,256]{1,0:T(8,128)(2,1)S(1)} %get-tuple-element.119), channel_id=1, source_target_pairs={{0,16},{16,0},{32,48},{48,32},{64,80},{80,64},{96,112},{112,96},{1... | collective-permute-start | bytes 24584 | tf_op jit(solution)/shard_map/ppermute | solution.py:247
  101.5 0.4 collective-permute-start.12
  101.9 0.0 collective-permute-start.13
  101.9 1.2 collective-permute-start.15
  103.1 1.5 %collective-permute-start.17 = (bf16[8,512]{1,0:T(8,128)(2,1)S(1)}, bf16[8,512]{1,0:T(8,128)(2,1)S(1)}, u32[]{:S(2)}, u32[]{:S(2)}) collective-permute-start(bf16[8,512]{1,0:T(8,128)(2,1)S(1)} %get-tuple-element.121), channel_id=1, source_target_pairs={{0,12},{4,8},{8,4},{12,0},{1,13},{5,9},{9,5},{13,1},{2,14},{6,10},... | collective-permute-start | bytes 24584 | tf_op jit(solution)/shard_map/ppermute | solution.py:247
  104.5 0.0 collective-permute-done.14.refs_12_
  104.5 0.0 collective-permute-start.16
  104.5 0.4 collective-permute-done.15.refs_13_
  105.0 1.8 %collective-permute-done.17.refs_15_ = bf16[8,512]{1,0:T(8,128)(2,1)S(1)} collective-permute-done((bf16[8,512]{1,0:T(8,128)(2,1)S(1)}, bf16[8,512]{1,0:T(8,128)(2,1)S(1)}, u32[]{:S(2)}, u32[]{:S(2)}) %collective-permute-start.17) | collective-permute-done | bytes 8224 | tf_op jit(solution)/shard_map/ppermute | solution.py:247
  106.8 0.2 collective-permute-done.16.refs_14_
  107.0 0.0 collective-permute-done.12.refs_10_
  107.0 0.0 collective-permute-done.13.refs_11_
  107.0 2.2 %shard_map.94 = (f32[16,32,256]{2,1,0:T(8,128)}, f32[128,128]{1,0:T(8,128)S(1)}, f32[16,32,256]{2,1,0:T(8,128)}) custom-call(f32[9]{0:T(128)S(1)} %stack.63.refs_0_, f32[16,32,256]{2,1,0:T(8,128)S(1)} %get-tuple-element.108.refs_1_, f32[16,32,256]{2,1,0:T(8,128)S(1)} %get-tuple-element.109.refs_2_, f32[16,32,256]{2,1,0:T(8,128)S(1)} %get-tuple-element.110.refs_3_, ...), custom_call_target="tpu_custom_call" | custom-call | tf_op jit(solution)/shard_map/pallas_call | solution.py:150
  109.2 17.0 %all_to_all.32 = f32[128,1,128]{2,1,0:T(1,128)S(1)} all-to-all(f32[128,1,128]{2,1,0:T(1,128)S(1)} %bitcast.28), channel_id=1, replica_groups=mesh['gx'=8,'gy'=4,'gz'=4] {'gx','gy','gz'}, dimensions={0} | all-to-all | bytes 131072 | tf_op jit(solution)/shard_map/all_to_all | solution.py:703
  126.2 2.6 %shard_map.95 = (f32[16,32,256]{2,1,0:T(8,128)}, f32[16,32,256]{2,1,0:T(8,128)}) custom-call(f32[8,128]{1,0:T(8,128)} %get-tuple-element.104.refs_0_, f32[128,128]{1,0:T(8,128)S(1)} %bitcast.27, f32[16,32,256]{2,1,0:T(8,128)} %get-tuple-element.123.refs_2_, f32[16,32,256]{2,1,0:T(8,128)} %get-tuple-element.124.refs_3_, f32[16,32,256]{2,1,0:T(8,128)} %refs_4_.3, ...), custom_call_target="tpu_custom_call" | custom-call | tf_op jit(solution)/shard_map/pallas_call | solution.py:150
  (1 shorter events, 0.0 us)
Async XLA Ops:
  4.1 11.6 %copy-start.4 = (bf16[16,256]{1,0:T(8,128)(2,1)S(1)}, bf16[16,256]{1,0:T(8,128)(2,1)}, u32[]{:S(2)}) copy-start(bf16[16,256]{1,0:T(8,128)(2,1)} %get-tuple-element.67) | copy-start | bytes 24580
  4.1 12.7 %copy-start.1 = (bf16[32,256]{1,0:T(8,128)(2,1)S(1)}, bf16[32,256]{1,0:T(8,128)(2,1)}, u32[]{:S(2)}) copy-start(bf16[32,256]{1,0:T(8,128)(2,1)} %get-tuple-element.65) | copy-start | bytes 49156
  4.1 13.4 %copy-start = (bf16[32,256]{1,0:T(8,128)(2,1)S(1)}, bf16[32,256]{1,0:T(8,128)(2,1)}, u32[]{:S(2)}) copy-start(bf16[32,256]{1,0:T(8,128)(2,1)} %get-tuple-element.66) | copy-start | bytes 49156
  4.1 15.2 %copy-start.3 = (bf16[16,256]{1,0:T(8,128)(2,1)S(1)}, bf16[16,256]{1,0:T(8,128)(2,1)}, u32[]{:S(2)}) copy-start(bf16[16,256]{1,0:T(8,128)(2,1)} %get-tuple-element.68) | copy-start | bytes 24580
  4.1 22.9 %all-to-all-start = ((bf16[128,5,2,128]{3,2,1,0:T(2,128)(2,1)}), bf16[128,5,2,128]{3,2,1,0:T(2,128)(2,1)S(1)}, u32[]{:S(2)}, u32[]{:S(2)}) async-start(bf16[128,5,2,128]{3,2,1,0:T(2,128)(2,1)} %bitcast.29), calls=%async_computation | async-start | bytes 655360 | tf_op jit(solution)/shard_map/all_to_all | solution.py:703
  15.6 5.7 %copy-start.2 = (bf16[8,512]{1,0:T(8,128)(2,1)S(1)}, bf16[8,512]{1,0:T(8,128)(2,1)}, u32[]{:S(2)}) copy-start(bf16[8,512]{1,0:T(8,128)(2,1)} %get-tuple-element.69) | copy-start | bytes 24580
  15.7 8.1 %collective-permute-start.2 = (bf16[16,256]{1,0:T(8,128)(2,1)S(1)}, bf16[16,256]{1,0:T(8,128)(2,1)S(1)}, u32[]{:S(2)}, u32[]{:S(2)}) collective-permute-start(bf16[16,256]{1,0:T(8,128)(2,1)S(1)} %copy-done.4), channel_id=1, source_target_pairs={{0,16},{16,0},{32,48},{48,32},{64,80},{80,64},{96,112},{112,96},{1... | collective-permute-start | bytes 24584 | tf_op jit(solution)/shard_map/ppermute | solution.py:247
  16.8 9.8 %collective-permute-start = (bf16[32,256]{1,0:T(8,128)(2,1)S(1)}, bf16[32,256]{1,0:T(8,128)(2,1)S(1)}, u32[]{:S(2)}, u32[]{:S(2)}) collective-permute-start(bf16[32,256]{1,0:T(8,128)(2,1)S(1)} %copy-done.1), channel_id=1, source_target_pairs={{0,1},{1,0},{2,3},{3,2},{4,5},{5,4},{6,7},{7,6},{8,9},{9,8},{10,11... | collective-permute-start | bytes 49160 | tf_op jit(solution)/shard_map/ppermute | solution.py:247
  17.5 9.1 %collective-permute-start.1 = (bf16[32,256]{1,0:T(8,128)(2,1)S(1)}, bf16[32,256]{1,0:T(8,128)(2,1)S(1)}, u32[]{:S(2)}, u32[]{:S(2)}) collective-permute-start(bf16[32,256]{1,0:T(8,128)(2,1)S(1)} %copy-done), channel_id=1, source_target_pairs={{0,3},{1,2},{2,1},{3,0},{4,7},{5,6},{6,5},{7,4},{8,11},{9,10},{10,... | collective-permute-start | bytes 49160 | tf_op jit(solution)/shard_map/ppermute | solution.py:247
  19.3 4.5 %collective-permute-start.3 = (bf16[16,256]{1,0:T(8,128)(2,1)S(1)}, bf16[16,256]{1,0:T(8,128)(2,1)S(1)}, u32[]{:S(2)}, u32[]{:S(2)}) collective-permute-start(bf16[16,256]{1,0:T(8,128)(2,1)S(1)} %copy-done.3), channel_id=1, source_target_pairs={{0,112},{16,32},{32,16},{48,64},{64,48},{80,96},{96,80},{112,0},{1... | collective-permute-start | bytes 24584 | tf_op jit(solution)/shard_map/ppermute | solution.py:247
  21.3 4.0 %collective-permute-start.5 = (bf16[8,512]{1,0:T(8,128)(2,1)S(1)}, bf16[8,512]{1,0:T(8,128)(2,1)S(1)}, u32[]{:S(2)}, u32[]{:S(2)}) collective-permute-start(bf16[8,512]{1,0:T(8,128)(2,1)S(1)} %copy-done.2), channel_id=1, source_target_pairs={{0,12},{4,8},{8,4},{12,0},{1,13},{5,9},{9,5},{13,1},{2,14},{6,10},... | collective-permute-start | bytes 24584 | tf_op jit(solution)/shard_map/ppermute | solution.py:247
  23.8 2.8 %collective-permute-start.4 = (bf16[8,512]{1,0:T(8,128)(2,1)S(1)}, bf16[8,512]{1,0:T(8,128)(2,1)S(1)}, u32[]{:S(2)}, u32[]{:S(2)}) collective-permute-start(bf16[8,512]{1,0:T(8,128)(2,1)S(1)} %copy-done.2), channel_id=1, source_target_pairs={{0,4},{4,0},{8,12},{12,8},{1,5},{5,1},{9,13},{13,9},{2,6},{6,2},{1... | collective-permute-start | bytes 24584 | tf_op jit(solution)/shard_map/ppermute | solution.py:247
  29.1 17.2 %all-to-all-start.1 = ((bf16[128,5,2,128]{3,2,1,0:T(2,128)(2,1)}), bf16[128,5,2,128]{3,2,1,0:T(2,128)(2,1)S(1)}, u32[]{:S(2)}, u32[]{:S(2)}) async-start(bf16[128,5,2,128]{3,2,1,0:T(2,128)(2,1)} %bitcast.30), calls=%async_computation.1 | async-start | bytes 655360 | tf_op jit(solution)/shard_map/all_to_all | solution.py:703
  49.2 5.6 %collective-permute-start.8 = (bf16[16,256]{1,0:T(8,128)(2,1)S(1)}, bf16[16,256]{1,0:T(8,128)(2,1)S(1)}, u32[]{:S(2)}, u32[]{:S(2)}) collective-permute-start(bf16[16,256]{1,0:T(8,128)(2,1)S(1)} %get-tuple-element.98), channel_id=1, source_target_pairs={{0,16},{16,0},{32,48},{48,32},{64,80},{80,64},{96,112},{112,96},{1... | collective-permute-start | bytes 24584 | tf_op jit(solution)/shard_map/ppermute | solution.py:247
  50.5 6.8 %collective-permute-start.6 = (bf16[32,256]{1,0:T(8,128)(2,1)S(1)}, bf16[32,256]{1,0:T(8,128)(2,1)S(1)}, u32[]{:S(2)}, u32[]{:S(2)}) collective-permute-start(bf16[32,256]{1,0:T(8,128)(2,1)S(1)} %get-tuple-element.96), channel_id=1, source_target_pairs={{0,1},{1,0},{2,3},{3,2},{4,5},{5,4},{6,7},{7,6},{8,9},{9,8},{10,11... | collective-permute-start | bytes 49160 | tf_op jit(solution)/shard_map/ppermute | solution.py:247
  50.9 6.4 %collective-permute-start.7 = (bf16[32,256]{1,0:T(8,128)(2,1)S(1)}, bf16[32,256]{1,0:T(8,128)(2,1)S(1)}, u32[]{:S(2)}, u32[]{:S(2)}) collective-permute-start(bf16[32,256]{1,0:T(8,128)(2,1)S(1)} %get-tuple-element.97), channel_id=1, source_target_pairs={{0,3},{1,2},{2,1},{3,0},{4,7},{5,6},{6,5},{7,4},{8,11},{9,10},{10,... | collective-permute-start | bytes 49160 | tf_op jit(solution)/shard_map/ppermute | solution.py:247
  50.9 3.9 %collective-permute-start.9 = (bf16[16,256]{1,0:T(8,128)(2,1)S(1)}, bf16[16,256]{1,0:T(8,128)(2,1)S(1)}, u32[]{:S(2)}, u32[]{:S(2)}) collective-permute-start(bf16[16,256]{1,0:T(8,128)(2,1)S(1)} %get-tuple-element.99), channel_id=1, source_target_pairs={{0,112},{16,32},{32,16},{48,64},{64,48},{80,96},{96,80},{112,0},{1... | collective-permute-start | bytes 24584 | tf_op jit(solution)/shard_map/ppermute | solution.py:247
  52.4 3.7 %collective-permute-start.11 = (bf16[8,512]{1,0:T(8,128)(2,1)S(1)}, bf16[8,512]{1,0:T(8,128)(2,1)S(1)}, u32[]{:S(2)}, u32[]{:S(2)}) collective-permute-start(bf16[8,512]{1,0:T(8,128)(2,1)S(1)} %get-tuple-element.100), channel_id=1, source_target_pairs={{0,12},{4,8},{8,4},{12,0},{1,13},{5,9},{9,5},{13,1},{2,14},{6,10},... | collective-permute-start | bytes 24584 | tf_op jit(solution)/shard_map/ppermute | solution.py:247
  54.8 2.5 %collective-permute-start.10 = (bf16[8,512]{1,0:T(8,128)(2,1)S(1)}, bf16[8,512]{1,0:T(8,128)(2,1)S(1)}, u32[]{:S(2)}, u32[]{:S(2)}) collective-permute-start(bf16[8,512]{1,0:T(8,128)(2,1)S(1)} %get-tuple-element.100), channel_id=1, source_target_pairs={{0,4},{4,0},{8,12},{12,8},{1,5},{5,1},{9,13},{13,9},{2,6},{6,2},{1... | collective-permute-start | bytes 24584 | tf_op jit(solution)/shard_map/ppermute | solution.py:247
  81.0 16.2 %all-to-all-start.3 = ((bf16[128,5,2,128]{3,2,1,0:T(2,128)(2,1)}), bf16[128,5,2,128]{3,2,1,0:T(2,128)(2,1)S(1)}, u32[]{:S(2)}, u32[]{:S(2)}) async-start(bf16[128,5,2,128]{3,2,1,0:T(2,128)(2,1)} %bitcast.32), calls=%async_computation.3 | async-start | bytes 655360 | tf_op jit(solution)/shard_map/all_to_all | solution.py:703
  100.1 4.4 %collective-permute-start.14 = (bf16[16,256]{1,0:T(8,128)(2,1)S(1)}, bf16[16,256]{1,0:T(8,128)(2,1)S(1)}, u32[]{:S(2)}, u32[]{:S(2)}) collective-permute-start(bf16[16,256]{1,0:T(8,128)(2,1)S(1)} %get-tuple-element.119), channel_id=1, source_target_pairs={{0,16},{16,0},{32,48},{48,32},{64,80},{80,64},{96,112},{112,96},{1... | collective-permute-start | bytes 24584 | tf_op jit(solution)/shard_map/ppermute | solution.py:247
  101.5 5.6 %collective-permute-start.12 = (bf16[32,256]{1,0:T(8,128)(2,1)S(1)}, bf16[32,256]{1,0:T(8,128)(2,1)S(1)}, u32[]{:S(2)}, u32[]{:S(2)}) collective-permute-start(bf16[32,256]{1,0:T(8,128)(2,1)S(1)} %get-tuple-element.117), channel_id=1, source_target_pairs={{0,1},{1,0},{2,3},{3,2},{4,5},{5,4},{6,7},{7,6},{8,9},{9,8},{10,11... | collective-permute-start | bytes 49160 | tf_op jit(solution)/shard_map/ppermute | solution.py:247
  101.9 5.2 %collective-permute-start.13 = (bf16[32,256]{1,0:T(8,128)(2,1)S(1)}, bf16[32,256]{1,0:T(8,128)(2,1)S(1)}, u32[]{:S(2)}, u32[]{:S(2)}) collective-permute-start(bf16[32,256]{1,0:T(8,128)(2,1)S(1)} %get-tuple-element.118), channel_id=1, source_target_pairs={{0,3},{1,2},{2,1},{3,0},{4,7},{5,6},{6,5},{7,4},{8,11},{9,10},{10,... | collective-permute-start | bytes 49160 | tf_op jit(solution)/shard_map/ppermute | solution.py:247
  101.9 3.1 %collective-permute-start.15 = (bf16[16,256]{1,0:T(8,128)(2,1)S(1)}, bf16[16,256]{1,0:T(8,128)(2,1)S(1)}, u32[]{:S(2)}, u32[]{:S(2)}) collective-permute-start(bf16[16,256]{1,0:T(8,128)(2,1)S(1)} %get-tuple-element.120), channel_id=1, source_target_pairs={{0,112},{16,32},{32,16},{48,64},{64,48},{80,96},{96,80},{112,0},{1... | collective-permute-start | bytes 24584 | tf_op jit(solution)/shard_map/ppermute | solution.py:247
  103.1 3.7 %collective-permute-start.17 = (bf16[8,512]{1,0:T(8,128)(2,1)S(1)}, bf16[8,512]{1,0:T(8,128)(2,1)S(1)}, u32[]{:S(2)}, u32[]{:S(2)}) collective-permute-start(bf16[8,512]{1,0:T(8,128)(2,1)S(1)} %get-tuple-element.121), channel_id=1, source_target_pairs={{0,12},{4,8},{8,4},{12,0},{1,13},{5,9},{9,5},{13,1},{2,14},{6,10},... | collective-permute-start | bytes 24584 | tf_op jit(solution)/shard_map/ppermute | solution.py:247
  104.5 2.5 %collective-permute-start.16 = (bf16[8,512]{1,0:T(8,128)(2,1)S(1)}, bf16[8,512]{1,0:T(8,128)(2,1)S(1)}, u32[]{:S(2)}, u32[]{:S(2)}) collective-permute-start(bf16[8,512]{1,0:T(8,128)(2,1)S(1)} %get-tuple-element.121), channel_id=1, source_target_pairs={{0,4},{4,0},{8,12},{12,8},{1,5},{5,1},{9,13},{13,9},{2,6},{6,2},{1... | collective-permute-start | bytes 24584 | tf_op jit(solution)/shard_map/ppermute | solution.py:247
